TPU v7x, 32 devices: a whole 2x2x4 slice. The times are simulated.
32 devices in a mesh: dp: 16 (over z, y, x), tensor: 2 (over core).
Axes of the slice: x: 2, y: 2, z: 4, core: 2. Of those that a mesh axis runs over, the one named last changes fastest.
Arguments:
- tokens: bfloat16 [16384, 1024], P('dp'), may hold values from -6 to 6
- page_ids: int32 [16384], P('dp'), may hold values from 0 to 31, as said below
- image_of_page: int32 [32], P('dp'), may hold values from 0 to 31, as said below
- memory: bfloat16 [32, 588, 1024], P('dp'), may hold values from -6 to 6
- ln0_gain: float32 [1024], replicated, may hold values from 0.25 to 1.75
- ln0_bias: float32 [1024], replicated, may hold values from -3 to 3
- w_self_query: bfloat16 [1024, 1024], P(None, 'tensor'), may hold values from -0.25 to 0.25
- b_self_query: float32 [1024], P('tensor'), may hold values from -3 to 3
- w_self_key: bfloat16 [1024, 1024], P(None, 'tensor'), may hold values from -0.1875 to 0.1875
- w_self_value: bfloat16 [1024, 1024], P(None, 'tensor'), may hold values from -0.1875 to 0.1875
- b_self_value: float32 [1024], P('tensor'), may hold values from -3 to 3
- w_self_out: bfloat16 [1024, 1024], P('tensor'), may hold values from -0.5 to 0.5
- b_self_out: float32 [1024], replicated, may hold values from -3 to 3
- ln1_gain: float32 [1024], replicated, may hold values from 0.25 to 1.75
- ln1_bias: float32 [1024], replicated, may hold values from -3 to 3
- w_query: bfloat16 [1024, 1024], P(None, 'tensor'), may hold values from -0.25 to 0.25
- b_query: float32 [1024], P('tensor'), may hold values from -3 to 3
- w_key: bfloat16 [1024, 1024], P(None, 'tensor'), may hold values from -0.1875 to 0.1875
- w_value: bfloat16 [1024, 1024], P(None, 'tensor'), may hold values from -0.1875 to 0.1875
- b_value: float32 [1024], P('tensor'), may hold values from -3 to 3
- w_out: bfloat16 [1024, 1024], P('tensor'), may hold values from -0.5 to 0.5
- b_out: float32 [1024], replicated, may hold values from -3 to 3
- ln2_gain: float32 [1024], replicated, may hold values from 0.25 to 1.75
- ln2_bias: float32 [1024], replicated, may hold values from -3 to 3
- w_up: bfloat16 [1024, 4096], P(None, 'tensor'), may hold values from -0.1875 to 0.1875
- b_up: float32 [4096], P('tensor'), may hold values from -3 to 3
- w_down: bfloat16 [4096, 1024], P('tensor'), may hold values from -0.125 to 0.125
- b_down: float32 [1024], replicated, may hold values from -3 to 3
- cotangent: bfloat16 [16384, 1024], P('dp'), may hold values from -6 to 6
Outputs:
- layer_out: bfloat16 [16384, 1024], P('dp')
- d_tokens: bfloat16 [16384, 1024], P('dp')
- d_memory: bfloat16 [32, 588, 1024], P('dp')
- d_ln0_gain: float32 [1024], replicated
- d_ln0_bias: float32 [1024], replicated
- d_w_self_query: float32 [1024, 1024], P('dp', 'tensor')
- d_b_self_query: float32 [1024], P('tensor')
- d_w_self_key: float32 [1024, 1024], P('dp', 'tensor')
- d_w_self_value: float32 [1024, 1024], P('dp', 'tensor')
- d_b_self_value: float32 [1024], P('tensor')
- d_w_self_out: float32 [1024, 1024], P('tensor', 'dp')
- d_b_self_out: float32 [1024], replicated
- d_ln1_gain: float32 [1024], replicated
- d_ln1_bias: float32 [1024], replicated
- d_w_query: float32 [1024, 1024], P('dp', 'tensor')
- d_b_query: float32 [1024], P('tensor')
- d_w_key: float32 [1024, 1024], P('dp', 'tensor')
- d_w_value: float32 [1024, 1024], P('dp', 'tensor')
- d_b_value: float32 [1024], P('tensor')
- d_w_out: float32 [1024, 1024], P('tensor', 'dp')
- d_b_out: float32 [1024], replicated
- d_ln2_gain: float32 [1024], replicated
- d_ln2_bias: float32 [1024], replicated
- d_w_up: float32 [1024, 4096], P('dp', 'tensor')
- d_b_up: float32 [4096], P('tensor')
- d_w_down: float32 [4096, 1024], P('tensor', 'dp')
- d_b_down: float32 [1024], replicated
Inputs may be any that keep to these rules, and one draw needn't show every extreme that they name: `page_ids`: page numbers never fall from row to row. Each block of 1024 rows (rows b * 1024 to b * 1024 + 1023) has exactly 2 rows at which a new page starts, none among its first 256 rows, except that row 0 starts page 0; every other block begins with the last page of the block before. `image_of_page`: the 2 pages that start in block b read the images b * 2 to b * 2 + 1, each once.
All inputs are finite; a program needn't handle non-finite values.
Results may differ from a plain program's by a relative error of at most 0.023.
Values may be sent and summed in bfloat16 or wider, within the bound.
No kernel may reach another device: no remote copies, remote signals or barrier semaphores. Data moves between devices by JAX's collectives and lax.ppermute only.
A program may use at most 320 MiB of HBM per device.

v0:
```python
import math

import jax
import jax.numpy as jnp
from jax import lax
from jax.sharding import PartitionSpec as P

HEAD_WIDTH = 64


EPSILON = 1e-05


def shifted(value, axis, steps):
    count = lax.axis_size(axis)
    initial, last = (max(0, -steps), min(count, count - steps))
    return lax.ppermute(value, axis, [(source, source + steps) for source in range(initial, last)])


def layer_norm(values, gain, bias):
    mean = jnp.mean(values, axis=-1, keepdims=True)
    centered = values - mean
    inverse = lax.rsqrt(jnp.mean(centered * centered, axis=-1, keepdims=True) + EPSILON)
    normed = centered * inverse
    return (normed * gain + bias, normed, inverse)


def norm_back(grad, normed, inverse, gain):
    scaled = grad * gain
    inner = (
        scaled
        - jnp.mean(scaled, axis=-1, keepdims=True)
        - normed * jnp.mean(scaled * normed, axis=-1, keepdims=True)
    )
    return (inner * inverse, jnp.sum(grad * normed, axis=0), jnp.sum(grad, axis=0))


def block_scores(query_block, allowed_block, key_table):
    scores = jnp.einsum("thd,chd->htc", query_block, key_table, preferred_element_type=jnp.float32)
    return jnp.where(allowed_block[None], scores, -1e30)


def attend_forward(query_blocks, allowed, key_table, value_table):
    block_rows = query_blocks.shape[1]
    local_width = query_blocks.shape[2] * query_blocks.shape[3]

    def forward_block(carry, block):
        query_block, allowed_block = block
        scores = block_scores(query_block, allowed_block, key_table)
        highest = jnp.max(scores, axis=-1, keepdims=True)
        raised = jnp.exp(scores - highest)
        total = jnp.sum(raised, axis=-1, keepdims=True)
        weights = (raised / total).astype(jnp.bfloat16)
        mixed = jnp.einsum("htc,chd->thd", weights, value_table, preferred_element_type=jnp.float32)
        return (
            carry,
            (
                mixed.reshape(block_rows, local_width).astype(jnp.bfloat16),
                (highest + jnp.log(total))[..., 0],
            ),
        )

    unused_carry, (attended, log_totals) = lax.scan(
        forward_block, jnp.zeros((), jnp.float32), (query_blocks, allowed)
    )
    return (attended.reshape(-1, local_width), log_totals)


def attend_backward(query_blocks, allowed, log_totals, grad_rows, key_table, value_table):
    block_count, block_rows, local_heads, head_size = query_blocks.shape
    key_count = key_table.shape[0]

    def backward_block(carry, block):
        query_block, allowed_block, log_block, grad_block = block
        scores = block_scores(query_block, allowed_block, key_table)
        probs = jnp.exp(scores - log_block[..., None])
        weights = probs.astype(jnp.bfloat16)
        value_grads = carry[1] + jnp.einsum(
            "htc,thd->chd", weights, grad_block, preferred_element_type=jnp.float32
        )
        grad_probs = jnp.einsum(
            "thd,chd->htc", grad_block, value_table, preferred_element_type=jnp.float32
        )
        grad_scores = (
            probs * (grad_probs - jnp.sum(grad_probs * probs, axis=-1, keepdims=True))
        ).astype(jnp.bfloat16)
        grad_query = jnp.einsum(
            "htc,chd->thd", grad_scores, key_table, preferred_element_type=jnp.float32
        ).astype(jnp.bfloat16)
        key_grads = carry[0] + jnp.einsum(
            "htc,thd->chd", grad_scores, query_block, preferred_element_type=jnp.float32
        )
        return ((key_grads, value_grads), grad_query.reshape(block_rows, local_heads * head_size))

    empty_grads = jnp.zeros((key_count, local_heads, head_size), jnp.float32)
    grad_blocks = grad_rows.reshape(block_count, block_rows, local_heads, head_size)
    (key_grads, value_grads), grad_queries = lax.scan(
        backward_block, (empty_grads, empty_grads), (query_blocks, allowed, log_totals, grad_blocks)
    )
    local_width = local_heads * head_size
    return (
        key_grads.reshape(key_count, local_width),
        value_grads.reshape(key_count, local_width),
        grad_queries.reshape(-1, local_width),
    )


def per_device(
    tokens,
    page_ids,
    image_of_page,
    memory,
    ln0_gain,
    ln0_bias,
    w_self_query,
    b_self_query,
    w_self_key,
    w_self_value,
    b_self_value,
    w_self_out,
    b_self_out,
    ln1_gain,
    ln1_bias,
    w_query,
    b_query,
    w_key,
    w_value,
    b_value,
    w_out,
    b_out,
    ln2_gain,
    ln2_bias,
    w_up,
    b_up,
    w_down,
    b_down,
    cotangent,
):
    row_count, width = tokens.shape
    image_count, memory_rows = (memory.shape[0], memory.shape[1])
    half_width = w_query.shape[1]
    local_heads = half_width // HEAD_WIDTH
    scale = 1.0 / math.sqrt(HEAD_WIDTH)
    block_rows = min(row_count, 512)
    block_count = row_count // block_rows
    own_rows = image_count * memory_rows
    key_count = own_rows + memory_rows
    input_values = tokens.astype(jnp.float32)
    hidden_zero, self_normed_rows, inverse_zero = layer_norm(input_values, ln0_gain, ln0_bias)
    hidden_zero = hidden_zero.astype(jnp.bfloat16)
    self_queries = (
        (jnp.dot(hidden_zero, w_self_query, preferred_element_type=jnp.float32) + b_self_query)
        * scale
    ).astype(jnp.bfloat16)
    self_key_rows = jnp.dot(hidden_zero, w_self_key, preferred_element_type=jnp.float32).astype(
        jnp.bfloat16
    )
    self_values = (
        jnp.dot(hidden_zero, w_self_value, preferred_element_type=jnp.float32) + b_self_value
    ).astype(jnp.bfloat16)
    last_mark = (page_ids == page_ids[row_count - 1]).astype(jnp.bfloat16)
    prior_keys, prior_values, prior_mark = shifted((self_key_rows, self_values, last_mark), "dp", 1)
    self_key_table = jnp.concatenate([prior_keys, self_key_rows], 0).reshape(
        2 * row_count, local_heads, HEAD_WIDTH
    )
    self_value_table = jnp.concatenate([prior_values, self_values], 0).reshape(
        2 * row_count, local_heads, HEAD_WIDTH
    )
    positions = jnp.arange(row_count, dtype=jnp.int32)
    own_ok = (page_ids[:, None] == page_ids[None, :]) & (positions[None, :] <= positions[:, None])
    prior_ok = (prior_mark[None, :] > 0.5) & (page_ids == page_ids[0])[:, None]
    self_allowed = jnp.concatenate([prior_ok, own_ok], 1).reshape(
        block_count, block_rows, 2 * row_count
    )
    self_query_blocks = self_queries.reshape(block_count, block_rows, local_heads, HEAD_WIDTH)
    self_attended, self_logs = attend_forward(
        self_query_blocks, self_allowed, self_key_table, self_value_table
    )
    self_branch = (
        lax.psum(jnp.dot(self_attended, w_self_out, preferred_element_type=jnp.float32), "tensor")
        + b_self_out
    )
    start = input_values + self_branch
    first_page = lax.axis_index("dp") * image_count
    local_page = page_ids - first_page
    picked = local_page[:, None] == jnp.arange(image_count, dtype=jnp.int32)[None, :]
    token_image = jnp.sum(jnp.where(picked, image_of_page[None, :], 0), axis=1)
    token_slot = jnp.where(local_page >= 0, token_image - first_page, image_count)
    key_slot = jnp.repeat(jnp.arange(image_count + 1, dtype=jnp.int32), memory_rows)
    allowed = (token_slot[:, None] == key_slot[None, :]).reshape(block_count, block_rows, key_count)
    last_image = image_of_page[image_count - 1] - first_page
    flat_memory = memory.reshape(own_rows, width)
    keys_here = jnp.dot(flat_memory, w_key, preferred_element_type=jnp.float32).astype(jnp.bfloat16)
    values_here = (
        jnp.dot(flat_memory, w_value, preferred_element_type=jnp.float32) + b_value
    ).astype(jnp.bfloat16)

    def tail_rows(matrix):
        return lax.dynamic_slice_in_dim(matrix, last_image * memory_rows, memory_rows, 0)

    prior_image_keys, prior_image_values = shifted(
        (tail_rows(keys_here), tail_rows(values_here)), "dp", 1
    )
    all_keys = jnp.concatenate([keys_here, prior_image_keys], 0).reshape(
        key_count, local_heads, HEAD_WIDTH
    )
    all_values = jnp.concatenate([values_here, prior_image_values], 0).reshape(
        key_count, local_heads, HEAD_WIDTH
    )
    hidden_one, normed_one, inverse_one = layer_norm(start, ln1_gain, ln1_bias)
    hidden_one = hidden_one.astype(jnp.bfloat16)
    queries = (
        (jnp.dot(hidden_one, w_query, preferred_element_type=jnp.float32) + b_query) * scale
    ).astype(jnp.bfloat16)
    query_blocks = queries.reshape(block_count, block_rows, local_heads, HEAD_WIDTH)
    attended, log_totals = attend_forward(query_blocks, allowed, all_keys, all_values)
    branch = (
        lax.psum(jnp.dot(attended, w_out, preferred_element_type=jnp.float32), "tensor") + b_out
    )
    middle = start + branch
    hidden_two, normed_two, inverse_two = layer_norm(middle, ln2_gain, ln2_bias)
    hidden_two = hidden_two.astype(jnp.bfloat16)
    up_value = jnp.dot(hidden_two, w_up, preferred_element_type=jnp.float32) + b_up
    activated = jax.nn.gelu(up_value, approximate=False).astype(jnp.bfloat16)
    down_sum = lax.psum(
        jnp.dot(activated, w_down, preferred_element_type=jnp.float32).astype(jnp.bfloat16),
        "tensor",
    ).astype(jnp.float32)
    layer_out = (middle + down_sum + b_down).astype(jnp.bfloat16)
    grad_outer = cotangent.astype(jnp.float32)
    grad_down = jnp.einsum("tf,td->fd", activated, cotangent, preferred_element_type=jnp.float32)
    down_bias_grad = jnp.sum(grad_outer, axis=0)
    grad_act = jnp.einsum("td,fd->tf", cotangent, w_down, preferred_element_type=jnp.float32)
    unused_value, gelu_back = jax.vjp(lambda inner: jax.nn.gelu(inner, approximate=False), up_value)
    grad_upvalue = gelu_back(grad_act)[0].astype(jnp.bfloat16)
    grad_up = jnp.einsum("td,tf->df", hidden_two, grad_upvalue, preferred_element_type=jnp.float32)
    up_bias_grad = jnp.sum(grad_upvalue.astype(jnp.float32), axis=0)
    grad_hidden_two = lax.psum(
        jnp.einsum("tf,df->td", grad_upvalue, w_up, preferred_element_type=jnp.float32), "tensor"
    )
    back_two, gain_two_grad, bias_two_grad = norm_back(
        grad_hidden_two, normed_two, inverse_two, ln2_gain
    )
    grad_middle = grad_outer + back_two
    grad_branch = grad_middle.astype(jnp.bfloat16)
    grad_out = jnp.einsum("th,td->hd", attended, grad_branch, preferred_element_type=jnp.float32)
    out_bias_grad = jnp.sum(grad_branch.astype(jnp.float32), axis=0)
    grad_attended = jnp.einsum(
        "td,hd->th", grad_branch, w_out, preferred_element_type=jnp.float32
    ).astype(jnp.bfloat16)
    key_grads, value_grads, grad_queries = attend_backward(
        query_blocks, allowed, log_totals, grad_attended, all_keys, all_values
    )
    returned_keys, returned_values = (
        shifted(key_grads[own_rows:].astype(jnp.bfloat16), "dp", -1).astype(jnp.float32),
        shifted(value_grads[own_rows:].astype(jnp.bfloat16), "dp", -1).astype(jnp.float32),
    )

    def add_back(local_part, returned):
        begin = last_image * memory_rows
        current = lax.dynamic_slice_in_dim(local_part, begin, memory_rows, 0)
        return lax.dynamic_update_slice_in_dim(local_part, current + returned, begin, 0)

    key_total = add_back(key_grads[:own_rows], returned_keys).astype(jnp.bfloat16)
    value_total = add_back(value_grads[:own_rows], returned_values).astype(jnp.bfloat16)
    grad_key = jnp.einsum("md,me->de", flat_memory, key_total, preferred_element_type=jnp.float32)
    grad_value = jnp.einsum(
        "md,me->de", flat_memory, value_total, preferred_element_type=jnp.float32
    )
    value_bias_grad = jnp.sum(value_total.astype(jnp.float32), axis=0)
    memory_part = jnp.einsum(
        "me,de->md", key_total, w_key, preferred_element_type=jnp.float32
    ) + jnp.einsum("me,de->md", value_total, w_value, preferred_element_type=jnp.float32)
    grad_query_w = (
        jnp.einsum("td,th->dh", hidden_one, grad_queries, preferred_element_type=jnp.float32)
        * scale
    )
    query_bias_grad = jnp.sum(grad_queries.astype(jnp.float32), axis=0) * scale
    hidden_part = (
        jnp.einsum("th,dh->td", grad_queries, w_query, preferred_element_type=jnp.float32) * scale
    )
    grad_hidden_one, grad_memory = lax.psum((hidden_part, memory_part), "tensor")
    back_one, gain_one_grad, bias_one_grad = norm_back(
        grad_hidden_one, normed_one, inverse_one, ln1_gain
    )
    grad_start = grad_middle + back_one
    d_memory = grad_memory.reshape(image_count, memory_rows, width).astype(jnp.bfloat16)
    grad_start_low = grad_start.astype(jnp.bfloat16)
    grad_self_out = jnp.einsum(
        "th,td->hd", self_attended, grad_start_low, preferred_element_type=jnp.float32
    )
    self_out_bias_grad = jnp.sum(grad_start_low.astype(jnp.float32), axis=0)
    grad_self_attended = jnp.einsum(
        "td,hd->th", grad_start_low, w_self_out, preferred_element_type=jnp.float32
    ).astype(jnp.bfloat16)
    self_key_grads, self_value_grads, grad_self_queries = attend_backward(
        self_query_blocks,
        self_allowed,
        self_logs,
        grad_self_attended,
        self_key_table,
        self_value_table,
    )
    later_keys, later_values = (
        shifted(self_key_grads[:row_count].astype(jnp.bfloat16), "dp", -1).astype(jnp.float32),
        shifted(self_value_grads[:row_count].astype(jnp.bfloat16), "dp", -1).astype(jnp.float32),
    )
    self_key_total = (self_key_grads[row_count:] + later_keys).astype(jnp.bfloat16)
    self_value_total = (self_value_grads[row_count:] + later_values).astype(jnp.bfloat16)
    grad_self_query_w = (
        jnp.einsum("td,th->dh", hidden_zero, grad_self_queries, preferred_element_type=jnp.float32)
        * scale
    )
    self_query_bias_grad = jnp.sum(grad_self_queries.astype(jnp.float32), axis=0) * scale
    grad_self_key_w = jnp.einsum(
        "td,th->dh", hidden_zero, self_key_total, preferred_element_type=jnp.float32
    )
    grad_self_value_w = jnp.einsum(
        "td,th->dh", hidden_zero, self_value_total, preferred_element_type=jnp.float32
    )
    self_value_bias_grad = jnp.sum(self_value_total.astype(jnp.float32), axis=0)
    zero_part = (
        jnp.einsum("th,dh->td", grad_self_queries, w_self_query, preferred_element_type=jnp.float32)
        * scale
        + jnp.einsum("th,dh->td", self_key_total, w_self_key, preferred_element_type=jnp.float32)
        + jnp.einsum(
            "th,dh->td", self_value_total, w_self_value, preferred_element_type=jnp.float32
        )
    )
    grad_hidden_zero = lax.psum(zero_part.astype(jnp.bfloat16), "tensor").astype(jnp.float32)
    back_zero, gain_zero_grad, bias_zero_grad = norm_back(
        grad_hidden_zero, self_normed_rows, inverse_zero, ln0_gain
    )
    d_tokens = (grad_start + back_zero).astype(jnp.bfloat16)
    (
        s_squery,
        self_key_spec,
        s_svalue,
        s_sout,
        summed_query,
        summed_key,
        summed_value,
        summed_out,
        summed_up,
        summed_down,
    ) = (
        lax.psum_scatter(grad_self_query_w, "dp", scatter_dimension=0, tiled=True),
        lax.psum_scatter(grad_self_key_w, "dp", scatter_dimension=0, tiled=True),
        lax.psum_scatter(grad_self_value_w, "dp", scatter_dimension=0, tiled=True),
        lax.psum_scatter(grad_self_out, "dp", scatter_dimension=1, tiled=True),
        lax.psum_scatter(grad_query_w, "dp", scatter_dimension=0, tiled=True),
        lax.psum_scatter(grad_key, "dp", scatter_dimension=0, tiled=True),
        lax.psum_scatter(grad_value, "dp", scatter_dimension=0, tiled=True),
        lax.psum_scatter(grad_out, "dp", scatter_dimension=1, tiled=True),
        lax.psum_scatter(grad_up, "dp", scatter_dimension=0, tiled=True),
        lax.psum_scatter(grad_down, "dp", scatter_dimension=1, tiled=True),
    )
    small_sums = lax.psum(
        (
            gain_zero_grad,
            bias_zero_grad,
            self_query_bias_grad,
            self_value_bias_grad,
            self_out_bias_grad,
            gain_one_grad,
            bias_one_grad,
            query_bias_grad,
            value_bias_grad,
            out_bias_grad,
            gain_two_grad,
            bias_two_grad,
            up_bias_grad,
            down_bias_grad,
        ),
        "dp",
    )
    return (
        layer_out,
        d_tokens,
        d_memory,
        small_sums[0],
        small_sums[1],
        s_squery,
        small_sums[2],
        self_key_spec,
        s_svalue,
        small_sums[3],
        s_sout,
        small_sums[4],
        small_sums[5],
        small_sums[6],
        summed_query,
        small_sums[7],
        summed_key,
        summed_value,
        small_sums[8],
        summed_out,
        small_sums[9],
        small_sums[10],
        small_sums[11],
        summed_up,
        small_sums[12],
        summed_down,
        small_sums[13],
    )


def solution(mesh):
    in_specs = (
        P("dp", None),
        P("dp"),
        P("dp"),
        P("dp", None, None),
        P(),
        P(),
        P(None, "tensor"),
        P("tensor"),
        P(None, "tensor"),
        P(None, "tensor"),
        P("tensor"),
        P("tensor", None),
        P(),
        P(),
        P(),
        P(None, "tensor"),
        P("tensor"),
        P(None, "tensor"),
        P(None, "tensor"),
        P("tensor"),
        P("tensor", None),
        P(),
        P(),
        P(),
        P(None, "tensor"),
        P("tensor"),
        P("tensor", None),
        P(),
        P("dp", None),
    )
    out_specs = (
        P("dp", None),
        P("dp", None),
        P("dp", None, None),
        P(),
        P(),
        P("dp", "tensor"),
        P("tensor"),
        P("dp", "tensor"),
        P("dp", "tensor"),
        P("tensor"),
        P("tensor", "dp"),
        P(),
        P(),
        P(),
        P("dp", "tensor"),
        P("tensor"),
        P("dp", "tensor"),
        P("dp", "tensor"),
        P("tensor"),
        P("tensor", "dp"),
        P(),
        P(),
        P(),
        P("dp", "tensor"),
        P("tensor"),
        P("tensor", "dp"),
        P(),
    )
    return jax.shard_map(
        per_device, mesh=mesh, in_specs=in_specs, out_specs=out_specs, check_vma=False
    )
```

profile of v0, /device:TPU:0, one launch (start us, length us, event | category | flops | bytes accessed | tf_op | source)
XLA Modules:
  0.0 2042.4 jit_solution(7493587867638328912)
XLA Ops:
  79.6 101.6 %while.54 = (s32[]{:T(128)}, bf16[2,512,512]{2,1,0:T(8,128)(2,1)}, f32[2,8,512]{2,1,0:T(8,128)S(1)}, pred[2,512,2048]{2,1,0:T(8,128)(4,1)}, bf16[2,512,8,64]{1,3...) while((s32[]{:T(128)}, bf16[2,512,512]{2,1,0:T(8,128)(2,1)}, ...), condition=%wide.region_5.6_spmd, body=%wide.region_2.5_spmd.sunk | while | flops 2223239168 | bytes 117571720 | solution.py:63
  249.7 86.3 %while.55 = (s32[]{:T(128)}, bf16[2,512,512]{2,1,0:T(8,128)(2,1)}, f32[2,8,512]{2,1,0:T(8,128)S(1)}, pred[2,512,1764]{1,2,0:T(8,128)(4,1)}, bf16[2,512,8,64]{1,3...) while((s32[]{:T(128)}, bf16[2,512,512]{2,1,0:T(8,128)(2,1)}, ...), condition=%wide.region_13.14_spmd, body=%wide.region_10.13_spmd.sunk | while | flops 1914974208 | bytes 101722248 | solution.py:63
  341.0 32.8 %all-reduce.11.cloned.1.call-done = f32[1024,1024]{1,0:T(8,128)} async-done(((f32[1024,1024]{1,0:T(8,128)}), f32[1024,1024]{1,0:T(8,128)}) %all-reduce.11.cloned.1.call-update) | async-done | bytes 4194320 | tf_op jit(solution)/shard_map/psum | solution.py:218
  386.3 25.4 %convert_reduce_fusion = (f32[2048]{0:T(1024)}, bf16[1024,2048]{1,0:T(8,128)(2,1)S(1)}, f32[1024,2048]{1,0:T(8,128)}) fusion(f32[1024,2048]{1,0:T(8,128)S(1)} %fusion.95, f32[2048]{0:T(1024)S(1)} %copy-done.77, bf16[1024,1024]{1,0:T(8,128)(2,1)S(1)} %copy-done.40, bf16[2048,1024]{1,0:T(8,128)(2,1)S(1)} %copy-done.87), kind=kOutput, calls=%fused_computation.83 | convolution fusion | flops 4452251648 | bytes 27279360 | tf_op jit(solution)/shard_map/td,fd->tf/dot_general | solution.py:233
  420.1 29.7 %all-reduce.13.cloned.1.call-done = f32[1024,1024]{1,0:T(8,128)} async-done(((f32[1024,1024]{1,0:T(8,128)}), f32[1024,1024]{1,0:T(8,128)}) %all-reduce.13.cloned.1.call-update) | async-done | bytes 4194320 | tf_op jit(solution)/shard_map/psum | solution.py:238
  472.3 187.8 %while.56 = (s32[]{:T(128)}, f32[1764,8,64]{0,2,1:T(8,128)}, f32[1764,8,64]{0,2,1:T(8,128)}, bf16[2,512,512]{1,2,0:T(8,128)(2,1)}, bf16[2,512,8,64]{1,3,2,0:T(8,...) while((s32[]{:T(128)}, f32[1764,8,64]{0,2,1:T(8,128)}, ...), condition=%wide.region_23.24_spmd.clone, body=%wide.region_21.23_spmd.clone.sunk | while | flops 4685893632 | bytes 247503024 | solution.py:97
  501.3 20.4 multiply_reduce_fusion.12
  521.7 24.7 %multiply_convert_fusion.7 = bf16[8,512,1764]{1,2,0:T(8,128)(2,1)} fusion(f32[8,512,1764]{1,2,0:T(8,128)} %subtract_exponential_fusion.5, f32[8,512,1764]{1,2,0:T(8,128)} %get-tuple-element.926, f32[8,512]{1,0:T(8,128)S(1)} %get-tuple-element.927), kind=kLoop, calls=%fused_computation.28.clone.1 | loop fusion | flops 21676032 | bytes 72269824 | tf_op jit(solution)/shard_map/while/body/eval_jaxpr/convert_element_type | solution.py:86
  595.1 20.4 multiply_reduce_fusion.12
  615.5 24.7 %multiply_convert_fusion.7 = bf16[8,512,1764]{1,2,0:T(8,128)(2,1)} fusion(f32[8,512,1764]{1,2,0:T(8,128)} %subtract_exponential_fusion.5, f32[8,512,1764]{1,2,0:T(8,128)} %get-tuple-element.926, f32[8,512]{1,0:T(8,128)S(1)} %get-tuple-element.927), kind=kLoop, calls=%fused_computation.28.clone.1 | loop fusion | flops 21676032 | bytes 72269824 | tf_op jit(solution)/shard_map/while/body/eval_jaxpr/convert_element_type | solution.py:86
  716.3 207.7 %while.57 = (s32[]{:T(128)}, f32[2048,8,64]{0,2,1:T(8,128)}, f32[2048,8,64]{0,2,1:T(8,128)}, bf16[2,512,512]{1,2,0:T(8,128)(2,1)}, bf16[2,512,8,64]{1,3,2,0:T(8,...) while((s32[]{:T(128)}, f32[2048,8,64]{0,2,1:T(8,128)}, ...), condition=%wide.region_29.30_spmd.clone, body=%wide.region_27.29_spmd.clone.sunk | while | flops 5473824768 | bytes 369738016 | solution.py:97
  747.5 25.1 %multiply_reduce_fusion.13 = (f32[8,512]{1,0:T(8,128)S(1)}, f32[8,512,2048]{2,1,0:T(8,128)}) fusion(f32[8,512,2048]{2,1,0:T(8,128)} %fusion.226, f32[8,512]{1,0:T(8,128)S(1)} %dynamic-slice_bitcast_fusion.16, pred[512,2048]{1,0:T(8,128)(4,1)S(1)} %dynamic-slice_bitcast_fusion.17, bf16[2048,8,64]{0,2,1:T(8,128)(2,1)} %get-tuple-element.1057, ...), kind=kOutput, calls=%fused_computation.53.clone.1 | convolution fusion | flops 1107292160 | bytes 70811648 | tf_op jit(solution)/shard_map/while/body/eval_jaxpr/thd,chd->htc/dot_general | solution.py:81
  772.6 27.9 %multiply_convert_fusion.8 = bf16[8,512,2048]{2,1,0:T(8,128)(2,1)} fusion(f32[8,512,2048]{2,1,0:T(8,128)} %get-tuple-element.938, f32[8,512,2048]{2,1,0:T(8,128)} %fusion.226, f32[8,512]{1,0:T(8,128)S(1)} %get-tuple-element.939, f32[8,512]{1,0:T(8,128)S(1)} %dynamic-slice_bitcast_fusion.16, pred[512,2048]{1,0:T(8,128)(4,1)S(1)} %dynamic-slice_bitcast_fusion.17), kind=kLoop, calls=%fused_computation.52.clone.1 | loop fusion | flops 41943040 | bytes 84967424 | tf_op jit(solution)/shard_map/while/body/eval_jaxpr/convert_element_type | solution.py:86
  851.0 25.1 %multiply_reduce_fusion.13 = (f32[8,512]{1,0:T(8,128)S(1)}, f32[8,512,2048]{2,1,0:T(8,128)}) fusion(f32[8,512,2048]{2,1,0:T(8,128)} %fusion.226, f32[8,512]{1,0:T(8,128)S(1)} %dynamic-slice_bitcast_fusion.16, pred[512,2048]{1,0:T(8,128)(4,1)S(1)} %dynamic-slice_bitcast_fusion.17, bf16[2048,8,64]{0,2,1:T(8,128)(2,1)} %get-tuple-element.1057, ...), kind=kOutput, calls=%fused_computation.53.clone.1 | convolution fusion | flops 1107292160 | bytes 70811648 | tf_op jit(solution)/shard_map/while/body/eval_jaxpr/thd,chd->htc/dot_general | solution.py:81
  876.1 27.9 %multiply_convert_fusion.8 = bf16[8,512,2048]{2,1,0:T(8,128)(2,1)} fusion(f32[8,512,2048]{2,1,0:T(8,128)} %get-tuple-element.938, f32[8,512,2048]{2,1,0:T(8,128)} %fusion.226, f32[8,512]{1,0:T(8,128)S(1)} %get-tuple-element.939, f32[8,512]{1,0:T(8,128)S(1)} %dynamic-slice_bitcast_fusion.16, pred[512,2048]{1,0:T(8,128)(4,1)S(1)} %dynamic-slice_bitcast_fusion.17), kind=kLoop, calls=%fused_computation.52.clone.1 | loop fusion | flops 41943040 | bytes 84967424 | tf_op jit(solution)/shard_map/while/body/eval_jaxpr/convert_element_type | solution.py:86
  1149.7 80.9 %all-reduce = (f32[1024]{0:T(1024)}, f32[1024]{0:T(1024)}, f32[512]{0:T(512)}, f32[512]{0:T(512)}, f32[1024]{0:T(1024)}, /*index=5*/f32[1024]{0:T(1024)}, f32[10...) all-reduce(f32[1024]{0:T(1024)S(1)} %get-tuple-element.596, ...), channel_id=1, replica_groups=mesh['dp'=16,'tensor'=2] {'dp'}, use_global_device_ids=true, to_apply=%region_35.36 | all-reduce | flops 13312 | bytes 106496 | tf_op jit(solution)/shard_map/psum | solution.py:358
  1238.5 32.3 %reduce-scatter.33.cloned.1.call-done = f32[64,512]{1,0:T(8,128)} async-done(((f32[1024,512]{1,0:T(8,128)}), f32[64,512]{1,0:T(8,128)}) %reduce-scatter.33.cloned.1.call-update) | async-done | bytes 131088
  1270.8 80.6 %reduce-scatter.31.cloned.1.call-done = f32[64,512]{1,0:T(8,128)} async-done(((f32[1024,512]{1,0:T(8,128)}), f32[64,512]{1,0:T(8,128)}) %reduce-scatter.31.cloned.1.call-update) | async-done | bytes 131088
  1351.4 80.8 %reduce-scatter.21.cloned.1.call-done = f32[512,64]{0,1:T(8,128)} async-done(((f32[512,1024]{0,1:T(8,128)}), f32[512,64]{0,1:T(8,128)}) %reduce-scatter.21.cloned.1.call-update) | async-done | bytes 131088 | tf_op jit(solution)/shard_map/reduce_scatter | solution.py:350
  1432.2 80.9 %reduce-scatter.15.cloned.1.call-done = f32[64,512]{1,0:T(8,128)} async-done(((f32[1024,512]{1,0:T(8,128)}), f32[64,512]{1,0:T(8,128)}) %reduce-scatter.15.cloned.1.call-update) | async-done | bytes 131088 | tf_op jit(solution)/shard_map/reduce_scatter | solution.py:347
  1513.0 80.6 %reduce-scatter.17.cloned.1.call-done = f32[64,512]{1,0:T(8,128)} async-done(((f32[1024,512]{1,0:T(8,128)}), f32[64,512]{1,0:T(8,128)}) %reduce-scatter.17.cloned.1.call-update) | async-done | bytes 131088 | tf_op jit(solution)/shard_map/reduce_scatter | solution.py:348
  1593.6 80.9 %reduce-scatter.19.cloned.1.call-done = f32[64,512]{1,0:T(8,128)} async-done(((f32[1024,512]{1,0:T(8,128)}), f32[64,512]{1,0:T(8,128)}) %reduce-scatter.19.cloned.1.call-update) | async-done | bytes 131088 | tf_op jit(solution)/shard_map/reduce_scatter | solution.py:349
  1674.5 178.1 %reduce-scatter.29.cloned.1.call-done = f32[2048,64]{0,1:T(8,128)} async-done(((f32[2048,1024]{0,1:T(8,128)}), f32[2048,64]{0,1:T(8,128)}) %reduce-scatter.29.cloned.1.call-update) | async-done | bytes 524304 | tf_op jit(solution)/shard_map/reduce_scatter | solution.py:356
  1852.5 183.1 %reduce-scatter.27.cloned.1.call-done = f32[64,2048]{1,0:T(8,128)} async-done(((f32[1024,2048]{1,0:T(8,128)}), f32[64,2048]{1,0:T(8,128)}) %reduce-scatter.27.cloned.1.call-update) | async-done | bytes 524304 | tf_op jit(solution)/shard_map/reduce_scatter | solution.py:355
  (460 shorter events, 862.8 us)
Async XLA Ops:
  7.2 225.2 %all-reduce.9.cloned.1.call-start = ((), (), s32[]{:S(2)}) async-start(), calls=%async_computation.10 | async-start | bytes 8388608 | tf_op jit(solution)/shard_map/psum | solution.py:180
  10.7 33.6 %collective-permute-start = (bf16[1024]{0:T(1024)(128)(2,1)S(1)}, bf16[1024]{0:T(1024)(128)(2,1)S(1)}, u32[]{:S(2)}, u32[]{:S(2)}) collective-permute-start(bf16[1024]{0:T(1024)(128)(2,1)S(1)} %get-tuple-element.710), channel_id=1, source_target_pairs={{0,2},{2,4},{4,6},{6,8},{8,10},{10,12},{12,14},{14,16},{16,18},{18... | collective-permute-start | bytes 6152 | tf_op jit(solution)/shard_map/ppermute | solution.py:17
  23.1 27.4 %collective-permute-start.1 = (bf16[1024,512]{1,0:T(8,128)(2,1)}, bf16[1024,512]{1,0:T(8,128)(2,1)}, u32[]{:S(2)}, u32[]{:S(2)}) collective-permute-start(bf16[1024,512]{1,0:T(8,128)(2,1)} %convolution_convert_fusion.6), channel_id=1, source_target_pairs={{0,2},{2,4},{4,6},{6,8},{8,10},{10,12},{12,14},{14,16},{16,18},{18... | collective-permute-start | bytes 3145736 | tf_op jit(solution)/shard_map/ppermute | solution.py:17
  29.9 41.7 %collective-permute-start.2 = (bf16[1024,512]{1,0:T(8,128)(2,1)}, bf16[1024,512]{1,0:T(8,128)(2,1)}, u32[]{:S(2)}, u32[]{:S(2)}) collective-permute-start(bf16[1024,512]{1,0:T(8,128)(2,1)} %add_convert_fusion.5), channel_id=1, source_target_pairs={{0,2},{2,4},{4,6},{6,8},{8,10},{10,12},{12,14},{14,16},{16,18},{18... | collective-permute-start | bytes 3145736 | tf_op jit(solution)/shard_map/ppermute | solution.py:17
  186.9 186.9 %all-reduce.11.cloned.1.call-start = ((), (), s32[]{:S(2)}) async-start(), calls=%async_computation.11 | async-start | bytes 8388608 | tf_op jit(solution)/shard_map/psum | solution.py:218
  197.7 19.2 collective-permute-start.4
  207.0 19.9 collective-permute-start.3
  340.8 109.0 %all-reduce.13.cloned.1.call-start = ((), (), s32[]{:S(2)}) async-start(), calls=%async_computation.12 | async-start | bytes 8388608 | tf_op jit(solution)/shard_map/psum | solution.py:238
  420.0 276.6 %all-reduce.15.cloned.1.call-start = ((), (), s32[]{:S(2)}) async-start(), calls=%async_computation.13 | async-start | bytes 8388608 | tf_op jit(solution)/shard_map/psum | solution.py:282
  666.9 479.1 %all-reduce.17.cloned.1.call-start = ((), (), s32[]{:S(2)}) async-start(), calls=%async_computation.24 | async-start | bytes 8388608 | tf_op jit(solution)/shard_map/psum | solution.py:225
  926.8 28.4 %collective-permute-start.5 = (bf16[1024,512]{0,1:T(8,128)(2,1)}, bf16[1024,512]{0,1:T(8,128)(2,1)}, u32[]{:S(2)}, u32[]{:S(2)}) collective-permute-start(bf16[1024,512]{0,1:T(8,128)(2,1)} %bitcast.22), channel_id=1, source_target_pairs={{2,0},{4,2},{6,4},{8,6},{10,8},{12,10},{14,12},{16,14},{18,16},{20... | collective-permute-start | bytes 3145736 | tf_op jit(solution)/shard_map/ppermute | solution.py:17
  943.7 33.2 %collective-permute-start.6 = (bf16[1024,512]{0,1:T(8,128)(2,1)}, bf16[1024,512]{0,1:T(8,128)(2,1)S(1)}, u32[]{:S(2)}, u32[]{:S(2)}) collective-permute-start(bf16[1024,512]{0,1:T(8,128)(2,1)} %bitcast.272), channel_id=1, source_target_pairs={{2,0},{4,2},{6,4},{8,6},{10,8},{12,10},{14,12},{16,14},{18,16},{20... | collective-permute-start | bytes 3145736 | tf_op jit(solution)/shard_map/ppermute | solution.py:17
  980.0 258.5 %reduce-scatter.25.cloned.1.call-start = ((), (), s32[]{:S(2)}) async-start(), calls=%async_computation.19 | async-start | bytes 2228224 | tf_op jit(solution)/shard_map/reduce_scatter | solution.py:354
  986.0 252.5 %reduce-scatter.23.cloned.1.call-start = ((), (), s32[]{:S(2)}) async-start(), calls=%async_computation.18 | async-start | bytes 2228224 | tf_op jit(solution)/shard_map/reduce_scatter | solution.py:351
  990.5 280.3 %reduce-scatter.33.cloned.1.call-start = ((), (), s32[]{:S(2)}) async-start(), calls=%async_computation.23 | async-start | bytes 2228224
  992.8 17.9 collective-permute-start.8
  1029.0 322.3 %reduce-scatter.31.cloned.1.call-start = ((), (), s32[]{:S(2)}) async-start(), calls=%async_computation.22 | async-start | bytes 2228224
  1030.9 21.6 %collective-permute-start.7 = (bf16[588,512]{1,0:T(8,128)(2,1)S(1)}, bf16[588,512]{1,0:T(8,128)(2,1)S(1)}, u32[]{:S(2)}, u32[]{:S(2)}) collective-permute-start(bf16[588,512]{1,0:T(8,128)(2,1)S(1)} %copy.166), channel_id=1, source_target_pairs={{2,0},{4,2},{6,4},{8,6},{10,8},{12,10},{14,12},{16,14},{18,16},{20... | collective-permute-start | bytes 1806344 | tf_op jit(solution)/shard_map/ppermute | solution.py:17
  1070.9 361.2 %reduce-scatter.21.cloned.1.call-start = ((), (), s32[]{:S(2)}) async-start(), calls=%async_computation.17 | async-start | bytes 2228224 | tf_op jit(solution)/shard_map/reduce_scatter | solution.py:350
  1075.9 437.1 %reduce-scatter.15.cloned.1.call-start = ((), (), s32[]{:S(2)}) async-start(), calls=%async_computation.14 | async-start | bytes 2228224 | tf_op jit(solution)/shard_map/reduce_scatter | solution.py:347
  1080.5 513.1 %reduce-scatter.17.cloned.1.call-start = ((), (), s32[]{:S(2)}) async-start(), calls=%async_computation.15 | async-start | bytes 2228224 | tf_op jit(solution)/shard_map/reduce_scatter | solution.py:348
  1084.8 589.6 %reduce-scatter.19.cloned.1.call-start = ((), (), s32[]{:S(2)}) async-start(), calls=%async_computation.16 | async-start | bytes 2228224 | tf_op jit(solution)/shard_map/reduce_scatter | solution.py:349
  1089.1 763.4 %reduce-scatter.29.cloned.1.call-start = ((), (), s32[]{:S(2)}) async-start(), calls=%async_computation.21 | async-start | bytes 8912896 | tf_op jit(solution)/shard_map/reduce_scatter | solution.py:356
  1100.1 935.5 %reduce-scatter.27.cloned.1.call-start = ((), (), s32[]{:S(2)}) async-start(), calls=%async_computation.20 | async-start | bytes 8912896 | tf_op jit(solution)/shard_map/reduce_scatter | solution.py:355
  (109 other events, 1150.8 us)
Sparse Core Ops, SparseCore 0:
  187.0 30.6 all-reduce.8
  340.9 32.8 all-reduce.10
  420.1 29.6 all-reduce.12
  667.0 29.5 all-reduce.14
  980.1 30.5 all-reduce.16
  1013.5 94.5 reduce-scatter.24
  1111.1 78.6 reduce-scatter.22
  1192.8 77.9 reduce-scatter.32
  1273.8 77.5 reduce-scatter.30
  1354.2 77.9 reduce-scatter.20
  1435.1 77.8 reduce-scatter.14
  1515.8 77.7 reduce-scatter.16
  1596.6 77.8 reduce-scatter.18
  1677.3 175.1 reduce-scatter.28
  1855.4 180.2 reduce-scatter.26
where the time goes:
time: 2050 us; the launch traced here: 2040 us
  waiting for transfers between devices  963 us (47%)
  matrix products  547 us (27%)
  other arithmetic  241 us (12%)
  local copies, waits for them, and re-layouts  149 us (7%)
  blocking collectives  97.5 us (5%)
  starting transfers between devices  28.7 us (1%)
    reduce_scatter x1, waiting for transfers between devices, per_device(): lax.psum_scatter(grad_up, 'dp', scatter_dimension=0, tiled=True)  183 us
    reduce_scatter x1, waiting for transfers between devices, per_device(): lax.psum_scatter(grad_down, 'dp', scatter_dimension=1, tiled=True)  178 us
    unnamed x17, waiting for transfers between devices  113 us
    dot_general x8, matrix products, block_scores(): jnp.einsum('thd,chd->htc', query_block, key_table, preferred_element_type...  109 us
    convert_element_type x4, other arithmetic, backward_block(): grad_scores = (probs * (grad_probs - jnp.sum(grad_probs * probs, axis=-1,...  105 us
    dot_general x4, matrix products, backward_block(): jnp.einsum('thd,chd->htc', grad_block, value_table, preferred_element_typ...  91 us
    ppermute x9, waiting for transfers between devices, shifted(): lax.ppermute(value, axis, [(source, source + steps) for source in range(i...  84.3 us
    reduce_scatter x1, waiting for transfers between devices, per_device(): lax.psum_scatter(grad_self_value_w, 'dp', scatter_dimension=0, tiled=True)  80.9 us
  transfers between devices with their start and end apart: 24, of which 19 were waited for; matrix products, arithmetic and copies ran while one was open for 10% of the time, Pallas kernels for 0%

commit v1 on v0

--- a/solution.py
+++ b/solution.py
@@ -15,6 +15,34 @@
     count = lax.axis_size(axis)
     initial, last = (max(0, -steps), min(count, count - steps))
     return lax.ppermute(value, axis, [(source, source + steps) for source in range(initial, last)])
+
+
+def core_sum(partial):
+    low = partial.astype(jnp.bfloat16)
+    other = lax.ppermute(low, "tensor", [(0, 1), (1, 0)])
+    return low.astype(jnp.float32) + other.astype(jnp.float32)
+
+
+def butterfly_sum(vectors):
+    sizes = [vector.shape[0] for vector in vectors]
+    total = jnp.concatenate(vectors).reshape(-1, 128)
+    count = lax.axis_size("dp")
+    bit = 1
+    while bit < count:
+        total = total + lax.ppermute(total, "dp", [(i, i ^ bit) for i in range(count)])
+        bit *= 2
+    flat = total.reshape(-1)
+    pieces, at = [], 0
+    for size in sizes:
+        pieces.append(flat[at : at + size])
+        at += size
+    return pieces
+
+
+def scattered(gradient, dimension):
+    return lax.psum_scatter(
+        gradient.astype(jnp.bfloat16), "dp", scatter_dimension=dimension, tiled=True
+    ).astype(jnp.float32)
 
 
 def layer_norm(values, gain, bias):
@@ -177,7 +205,7 @@
         self_query_blocks, self_allowed, self_key_table, self_value_table
     )
     self_branch = (
-        lax.psum(jnp.dot(self_attended, w_self_out, preferred_element_type=jnp.float32), "tensor")
+        core_sum(jnp.dot(self_attended, w_self_out, preferred_element_type=jnp.float32))
         + b_self_out
     )
     start = input_values + self_branch
@@ -215,17 +243,14 @@
     query_blocks = queries.reshape(block_count, block_rows, local_heads, HEAD_WIDTH)
     attended, log_totals = attend_forward(query_blocks, allowed, all_keys, all_values)
     branch = (
-        lax.psum(jnp.dot(attended, w_out, preferred_element_type=jnp.float32), "tensor") + b_out
+        core_sum(jnp.dot(attended, w_out, preferred_element_type=jnp.float32)) + b_out
     )
     middle = start + branch
     hidden_two, normed_two, inverse_two = layer_norm(middle, ln2_gain, ln2_bias)
     hidden_two = hidden_two.astype(jnp.bfloat16)
     up_value = jnp.dot(hidden_two, w_up, preferred_element_type=jnp.float32) + b_up
     activated = jax.nn.gelu(up_value, approximate=False).astype(jnp.bfloat16)
-    down_sum = lax.psum(
-        jnp.dot(activated, w_down, preferred_element_type=jnp.float32).astype(jnp.bfloat16),
-        "tensor",
-    ).astype(jnp.float32)
+    down_sum = core_sum(jnp.dot(activated, w_down, preferred_element_type=jnp.float32))
     layer_out = (middle + down_sum + b_down).astype(jnp.bfloat16)
     grad_outer = cotangent.astype(jnp.float32)
     grad_down = jnp.einsum("tf,td->fd", activated, cotangent, preferred_element_type=jnp.float32)
@@ -235,8 +260,8 @@
     grad_upvalue = gelu_back(grad_act)[0].astype(jnp.bfloat16)
     grad_up = jnp.einsum("td,tf->df", hidden_two, grad_upvalue, preferred_element_type=jnp.float32)
     up_bias_grad = jnp.sum(grad_upvalue.astype(jnp.float32), axis=0)
-    grad_hidden_two = lax.psum(
-        jnp.einsum("tf,df->td", grad_upvalue, w_up, preferred_element_type=jnp.float32), "tensor"
+    grad_hidden_two = core_sum(
+        jnp.einsum("tf,df->td", grad_upvalue, w_up, preferred_element_type=jnp.float32)
     )
     back_two, gain_two_grad, bias_two_grad = norm_back(
         grad_hidden_two, normed_two, inverse_two, ln2_gain
@@ -279,7 +304,7 @@
     hidden_part = (
         jnp.einsum("th,dh->td", grad_queries, w_query, preferred_element_type=jnp.float32) * scale
     )
-    grad_hidden_one, grad_memory = lax.psum((hidden_part, memory_part), "tensor")
+    grad_hidden_one, grad_memory = core_sum(hidden_part), core_sum(memory_part)
     back_one, gain_one_grad, bias_one_grad = norm_back(
         grad_hidden_one, normed_one, inverse_one, ln1_gain
     )
@@ -327,7 +352,7 @@
             "th,dh->td", self_value_total, w_self_value, preferred_element_type=jnp.float32
         )
     )
-    grad_hidden_zero = lax.psum(zero_part.astype(jnp.bfloat16), "tensor").astype(jnp.float32)
+    grad_hidden_zero = core_sum(zero_part)
     back_zero, gain_zero_grad, bias_zero_grad = norm_back(
         grad_hidden_zero, self_normed_rows, inverse_zero, ln0_gain
     )
@@ -344,18 +369,18 @@
         summed_up,
         summed_down,
     ) = (
-        lax.psum_scatter(grad_self_query_w, "dp", scatter_dimension=0, tiled=True),
-        lax.psum_scatter(grad_self_key_w, "dp", scatter_dimension=0, tiled=True),
-        lax.psum_scatter(grad_self_value_w, "dp", scatter_dimension=0, tiled=True),
-        lax.psum_scatter(grad_self_out, "dp", scatter_dimension=1, tiled=True),
-        lax.psum_scatter(grad_query_w, "dp", scatter_dimension=0, tiled=True),
-        lax.psum_scatter(grad_key, "dp", scatter_dimension=0, tiled=True),
-        lax.psum_scatter(grad_value, "dp", scatter_dimension=0, tiled=True),
-        lax.psum_scatter(grad_out, "dp", scatter_dimension=1, tiled=True),
-        lax.psum_scatter(grad_up, "dp", scatter_dimension=0, tiled=True),
-        lax.psum_scatter(grad_down, "dp", scatter_dimension=1, tiled=True),
-    )
-    small_sums = lax.psum(
+        scattered(grad_self_query_w, 0),
+        scattered(grad_self_key_w, 0),
+        scattered(grad_self_value_w, 0),
+        scattered(grad_self_out, 1),
+        scattered(grad_query_w, 0),
+        scattered(grad_key, 0),
+        scattered(grad_value, 0),
+        scattered(grad_out, 1),
+        scattered(grad_up, 0),
+        scattered(grad_down, 1),
+    )
+    small_sums = butterfly_sum(
         (
             gain_zero_grad,
             bias_zero_grad,
@@ -371,8 +396,7 @@
             bias_two_grad,
             up_bias_grad,
             down_bias_grad,
-        ),
-        "dp",
+        )
     )
     return (
         layer_out,

time: 2050 us -> 1420 us (0.69)
  waiting for transfers between devices: 963 us -> 400 us
  blocking collectives: 97.5 us -> 0 us
    reduce_scatter x8, waiting for transfers between devices: 684 us -> 301 us  [scattered(): lax.psum_scatter(gradient.astype(jnp.bfloat16), 'dp', scatter_dimension=d...]
    unnamed x17 -> x12, waiting for transfers between devices: 113 us -> 0.17 us
    psum x2 -> x0, blocking collectives: 97.5 us -> none  [the longest x1 80.9 us: per_device(): lax.psum((gain_zero_grad, bias_zero_grad, self_query_bias_grad, self_valu...]
    psum x5 -> x0, waiting for transfers between devices: 81.1 us -> none  [the longest x1 32.8 us: per_device(): lax.psum(jnp.dot(attended, w_out, preferred_element_type=jnp.float32), 't...]
    unnamed x192 -> x203, local copies, waits for them, and re-layouts: 40.5 us -> 49.5 us
  transfers between devices with their start and end apart: 24 -> 30, of which waited for: 19 -> 13; matrix products, arithmetic and copies ran while one was open for 10% -> 54% of each run, Pallas kernels for 0% -> 0%
where the time goes in v1:
time: 1420 us; the launch traced here: 1410 us
  matrix products  533 us (38%)
  waiting for transfers between devices  400 us (28%)
  other arithmetic  253 us (18%)
  local copies, waits for them, and re-layouts  168 us (12%)
  starting transfers between devices  40.6 us (3%)
  between operations  16.4 us (1%)
    reduce_scatter x8, waiting for transfers between devices, scattered(): lax.psum_scatter(gradient.astype(jnp.bfloat16), 'dp', scatter_dimension=d...  301 us
    dot_general x8, matrix products, block_scores(): jnp.einsum('thd,chd->htc', query_block, key_table, preferred_element_type...  109 us
    convert_element_type x4, other arithmetic, backward_block(): grad_scores = (probs * (grad_probs - jnp.sum(grad_probs * probs, axis=-1,...  105 us
    dot_general x4, matrix products, backward_block(): jnp.einsum('thd,chd->htc', grad_block, value_table, preferred_element_typ...  91.3 us
    ppermute x9, waiting for transfers between devices, shifted(): lax.ppermute(value, axis, [(source, source + steps) for source in range(i...  87.8 us
    dot_general x4, matrix products, backward_block(): jnp.einsum('htc,thd->chd', weights, grad_block, preferred_element_type=jn...  62.6 us
    dot_general x4, matrix products, forward_block(): jnp.einsum('htc,chd->thd', weights, value_table, preferred_element_type=j...  60.1 us
    reduce_sum x4, other arithmetic, forward_block(): total = jnp.sum(raised, axis=-1, keepdims=True)  53.7 us
  transfers between devices with their start and end apart: 30, of which 13 were waited for; matrix products, arithmetic and copies ran while one was open for 54% of the time, Pallas kernels for 0%

profile of v1, /device:TPU:0, one launch (start us, length us, event | category | flops | bytes accessed | tf_op | source)
XLA Modules:
  0.0 1412.4 jit_solution(7725661107072997186)
XLA Ops:
  80.7 101.8 %while.54 = (s32[]{:T(128)}, bf16[2,512,512]{2,1,0:T(8,128)(2,1)}, f32[2,8,512]{2,1,0:T(8,128)S(1)}, pred[2,512,2048]{2,1,0:T(8,128)(4,1)}, bf16[2,512,8,64]{1,3...) while((s32[]{:T(128)}, bf16[2,512,512]{2,1,0:T(8,128)(2,1)}, ...), condition=%wide.region_5.6_spmd, body=%wide.region_2.5_spmd.sunk | while | flops 2223239168 | bytes 117571720 | solution.py:91
  111.4 16.1 %fusion.205 = bf16[8,512,64]{1,2,0:T(8,128)(2,1)} fusion(bf16[2048,8,64]{0,2,1:T(8,128)(2,1)} %get-tuple-element.962, f32[8,512,2048]{2,1,0:T(8,128)} %get-tuple-element.905, f32[8,512]{1,0:T(8,128)S(1)} %fusion.204, f32[8,512]{1,0:T(8,128)S(1)} %get-tuple-element.906, pred[512,2048]{1,0:T(8,128)(4,1)} %copy-done.4), kind=kOutput, calls=%fused_computation.6.clone.1 | convolution fusion | flops 1107558400 | bytes 37257216 | tf_op jit(solution)/shard_map/while/body/eval_jaxpr/htc,chd->thd/dot_general | solution.py:82
  162.0 16.1 %fusion.205 = bf16[8,512,64]{1,2,0:T(8,128)(2,1)} fusion(bf16[2048,8,64]{0,2,1:T(8,128)(2,1)} %get-tuple-element.962, f32[8,512,2048]{2,1,0:T(8,128)} %get-tuple-element.905, f32[8,512]{1,0:T(8,128)S(1)} %fusion.204, f32[8,512]{1,0:T(8,128)S(1)} %get-tuple-element.906, pred[512,2048]{1,0:T(8,128)(4,1)} %copy-done.4), kind=kOutput, calls=%fused_computation.6.clone.1 | convolution fusion | flops 1107558400 | bytes 37257216 | tf_op jit(solution)/shard_map/while/body/eval_jaxpr/htc,chd->thd/dot_general | solution.py:82
  232.5 86.2 %while.55 = (s32[]{:T(128)}, bf16[2,512,512]{2,1,0:T(8,128)(2,1)}, f32[2,8,512]{2,1,0:T(8,128)S(1)}, pred[2,512,1764]{1,2,0:T(8,128)(4,1)}, bf16[2,512,8,64]{1,3...) while((s32[]{:T(128)}, bf16[2,512,512]{2,1,0:T(8,128)(2,1)}, ...), condition=%wide.region_12.13_spmd, body=%wide.region_9.12_spmd.sunk | while | flops 1914974208 | bytes 101722248 | solution.py:91
  335.8 26.0 %convert_reduce_fusion = (f32[2048]{0:T(1024)}, bf16[1024,2048]{1,0:T(8,128)(2,1)}, f32[1024,2048]{1,0:T(8,128)}) fusion(f32[1024,2048]{1,0:T(8,128)S(1)} %fusion.102, f32[2048]{0:T(1024)S(1)} %copy-done.74, bf16[1024,1024]{1,0:T(8,128)(2,1)S(1)} %copy-done.32, bf16[2048,1024]{1,0:T(8,128)(2,1)S(1)} %copy-done.84), kind=kOutput, calls=%fused_computation.83 | convolution fusion | flops 4452251648 | bytes 27279360 | tf_op jit(solution)/shard_map/td,fd->tf/dot_general | solution.py:258
  422.6 188.0 %while.56 = (s32[]{:T(128)}, f32[1764,8,64]{0,2,1:T(8,128)}, f32[1764,8,64]{0,2,1:T(8,128)}, bf16[2,512,512]{1,2,0:T(8,128)(2,1)}, bf16[2,512,8,64]{1,3,2,0:T(8,...) while((s32[]{:T(128)}, f32[1764,8,64]{0,2,1:T(8,128)}, ...), condition=%wide.region_19.20_spmd.clone, body=%wide.region_17.19_spmd.clone.sunk | while | flops 4685893632 | bytes 247503024 | solution.py:125
  451.7 20.6 %multiply_reduce_fusion.10 = (f32[8,512]{1,0:T(8,128)S(1)}, f32[8,512,1764]{1,2,0:T(8,128)}) fusion(f32[8,512,1764]{1,2,0:T(8,128)} %subtract_exponential_fusion.5, bf16[1764,8,64]{0,2,1:T(8,128)(2,1)} %get-tuple-element.1021, bf16[2,512,8,64]{1,3,2,0:T(8,128)(2,1)} %get-tuple-element.1020, s32[]{:T(128)S(6)} %copy.283), kind=kOutput, calls=%fused_computation.29.clone.1 | convolution fusion | flops 939290624 | bytes 60243972 | tf_op jit(solution)/shard_map/while/body/eval_jaxpr/thd,chd->htc/dot_general | solution.py:109
  472.2 24.8 %multiply_convert_fusion.10 = bf16[8,512,1764]{1,2,0:T(8,128)(2,1)} fusion(f32[8,512,1764]{1,2,0:T(8,128)} %subtract_exponential_fusion.5, f32[8,512,1764]{1,2,0:T(8,128)} %get-tuple-element.926, f32[8,512]{1,0:T(8,128)S(1)} %get-tuple-element.927), kind=kLoop, calls=%fused_computation.28.clone.1 | loop fusion | flops 21676032 | bytes 72269824 | tf_op jit(solution)/shard_map/while/body/eval_jaxpr/convert_element_type | solution.py:114
  530.8 14.8 %bitcast_add_fusion.12 = f32[1764,8,64]{0,2,1:T(8,128)} fusion(f32[1764,8,64]{0,2,1:T(8,128)} %get-tuple-element.1002, f32[8,512,1764]{1,2,0:T(8,128)} %subtract_exponential_fusion.5, pred[]{:T(512)S(6)} %compare.6, bf16[2,512,8,64]{1,3,2,0:T(8,128)(2,1)} %get-tuple-element.1020, s32[]{:T(128)S(6)} %copy.283), kind=kOutput, calls=%fused_computation.33.clone.1 | convolution fusion | flops 933875712 | bytes 36773892 | tf_op jit(solution)/shard_map/while/body/eval_jaxpr/htc,thd->chd/dot_general | solution.py:106
  545.6 20.4 %multiply_reduce_fusion.10 = (f32[8,512]{1,0:T(8,128)S(1)}, f32[8,512,1764]{1,2,0:T(8,128)}) fusion(f32[8,512,1764]{1,2,0:T(8,128)} %subtract_exponential_fusion.5, bf16[1764,8,64]{0,2,1:T(8,128)(2,1)} %get-tuple-element.1021, bf16[2,512,8,64]{1,3,2,0:T(8,128)(2,1)} %get-tuple-element.1020, s32[]{:T(128)S(6)} %copy.283), kind=kOutput, calls=%fused_computation.29.clone.1 | convolution fusion | flops 939290624 | bytes 60243972 | tf_op jit(solution)/shard_map/while/body/eval_jaxpr/thd,chd->htc/dot_general | solution.py:109
  566.0 24.7 %multiply_convert_fusion.10 = bf16[8,512,1764]{1,2,0:T(8,128)(2,1)} fusion(f32[8,512,1764]{1,2,0:T(8,128)} %subtract_exponential_fusion.5, f32[8,512,1764]{1,2,0:T(8,128)} %get-tuple-element.926, f32[8,512]{1,0:T(8,128)S(1)} %get-tuple-element.927), kind=kLoop, calls=%fused_computation.28.clone.1 | loop fusion | flops 21676032 | bytes 72269824 | tf_op jit(solution)/shard_map/while/body/eval_jaxpr/convert_element_type | solution.py:114
  716.3 208.3 %while.57 = (s32[]{:T(128)}, f32[2048,8,64]{0,2,1:T(8,128)}, f32[2048,8,64]{0,2,1:T(8,128)}, bf16[2,512,512]{1,2,0:T(8,128)(2,1)}, bf16[2,512,8,64]{1,3,2,0:T(8,...) while((s32[]{:T(128)}, f32[2048,8,64]{0,2,1:T(8,128)}, ...), condition=%wide.region_24.25_spmd.clone, body=%wide.region_22.24_spmd.clone.sunk | while | flops 5473824768 | bytes 369738016 | solution.py:125
  731.6 16.0 %bitcast_add_fusion.14 = f32[2048,8,64]{0,2,1:T(8,128)} fusion(f32[2048,8,64]{0,2,1:T(8,128)} %get-tuple-element.1038, f32[8,512,2048]{2,1,0:T(8,128)} %fusion.228, f32[8,512]{1,0:T(8,128)S(1)} %dynamic-slice_bitcast_fusion.16, pred[512,2048]{1,0:T(8,128)(4,1)S(1)} %dynamic-slice_bitcast_fusion.17, pred[]{:T(512)S(6)} %compare.7, ...), kind=kOutput, calls=%fused_computation.60.clone.1 | convolution fusion | flops 1101004800 | bytes 43532292 | tf_op jit(solution)/shard_map/while/body/eval_jaxpr/htc,thd->chd/dot_general | solution.py:106
  747.6 25.1 %multiply_reduce_fusion.11 = (f32[8,512]{1,0:T(8,128)S(1)}, f32[8,512,2048]{2,1,0:T(8,128)}) fusion(f32[8,512,2048]{2,1,0:T(8,128)} %fusion.228, f32[8,512]{1,0:T(8,128)S(1)} %dynamic-slice_bitcast_fusion.16, pred[512,2048]{1,0:T(8,128)(4,1)S(1)} %dynamic-slice_bitcast_fusion.17, bf16[2048,8,64]{0,2,1:T(8,128)(2,1)} %get-tuple-element.1057, ...), kind=kOutput, calls=%fused_computation.53.clone.1 | convolution fusion | flops 1107292160 | bytes 70811648 | tf_op jit(solution)/shard_map/while/body/eval_jaxpr/thd,chd->htc/dot_general | solution.py:109
  772.7 28.0 %multiply_convert_fusion.11 = bf16[8,512,2048]{2,1,0:T(8,128)(2,1)} fusion(f32[8,512,2048]{2,1,0:T(8,128)} %get-tuple-element.938, f32[8,512,2048]{2,1,0:T(8,128)} %fusion.228, f32[8,512]{1,0:T(8,128)S(1)} %get-tuple-element.939, f32[8,512]{1,0:T(8,128)S(1)} %dynamic-slice_bitcast_fusion.16, pred[512,2048]{1,0:T(8,128)(4,1)S(1)} %dynamic-slice_bitcast_fusion.17), kind=kLoop, calls=%fused_computation.52.clone.1 | loop fusion | flops 41943040 | bytes 84967424 | tf_op jit(solution)/shard_map/while/body/eval_jaxpr/convert_element_type | solution.py:114
  833.4 18.0 %bitcast_add_fusion.14 = f32[2048,8,64]{0,2,1:T(8,128)} fusion(f32[2048,8,64]{0,2,1:T(8,128)} %get-tuple-element.1038, f32[8,512,2048]{2,1,0:T(8,128)} %fusion.228, f32[8,512]{1,0:T(8,128)S(1)} %dynamic-slice_bitcast_fusion.16, pred[512,2048]{1,0:T(8,128)(4,1)S(1)} %dynamic-slice_bitcast_fusion.17, pred[]{:T(512)S(6)} %compare.7, ...), kind=kOutput, calls=%fused_computation.60.clone.1 | convolution fusion | flops 1101004800 | bytes 43532292 | tf_op jit(solution)/shard_map/while/body/eval_jaxpr/htc,thd->chd/dot_general | solution.py:106
  851.4 25.2 %multiply_reduce_fusion.11 = (f32[8,512]{1,0:T(8,128)S(1)}, f32[8,512,2048]{2,1,0:T(8,128)}) fusion(f32[8,512,2048]{2,1,0:T(8,128)} %fusion.228, f32[8,512]{1,0:T(8,128)S(1)} %dynamic-slice_bitcast_fusion.16, pred[512,2048]{1,0:T(8,128)(4,1)S(1)} %dynamic-slice_bitcast_fusion.17, bf16[2048,8,64]{0,2,1:T(8,128)(2,1)} %get-tuple-element.1057, ...), kind=kOutput, calls=%fused_computation.53.clone.1 | convolution fusion | flops 1107292160 | bytes 70811648 | tf_op jit(solution)/shard_map/while/body/eval_jaxpr/thd,chd->htc/dot_general | solution.py:109
  876.5 27.9 %multiply_convert_fusion.11 = bf16[8,512,2048]{2,1,0:T(8,128)(2,1)} fusion(f32[8,512,2048]{2,1,0:T(8,128)} %get-tuple-element.938, f32[8,512,2048]{2,1,0:T(8,128)} %fusion.228, f32[8,512]{1,0:T(8,128)S(1)} %get-tuple-element.939, f32[8,512]{1,0:T(8,128)S(1)} %dynamic-slice_bitcast_fusion.16, pred[512,2048]{1,0:T(8,128)(4,1)S(1)} %dynamic-slice_bitcast_fusion.17), kind=kLoop, calls=%fused_computation.52.clone.1 | loop fusion | flops 41943040 | bytes 84967424 | tf_op jit(solution)/shard_map/while/body/eval_jaxpr/convert_element_type | solution.py:114
  935.0 27.2 %collective-permute-done.11 = bf16[1024,512]{0,1:T(8,128)(2,1)S(1)} collective-permute-done((bf16[1024,512]{0,1:T(8,128)(2,1)S(1)}, bf16[1024,512]{0,1:T(8,128)(2,1)S(1)}, u32[]{:S(2)}, u32[]{:S(2)}) %collective-permute-start.11) | collective-permute-done | bytes 1048608 | tf_op jit(solution)/shard_map/ppermute | solution.py:17
  969.8 27.3 %collective-permute-done.10 = bf16[1024,512]{0,1:T(8,128)(2,1)S(1)} collective-permute-done((bf16[1024,512]{0,1:T(8,128)(2,1)S(1)}, bf16[1024,512]{0,1:T(8,128)(2,1)S(1)}, u32[]{:S(2)}, u32[]{:S(2)}) %collective-permute-start.10) | collective-permute-done | bytes 1048608 | tf_op jit(solution)/shard_map/ppermute | solution.py:17
  1096.3 39.9 %reduce-scatter.19.cloned.1.call-done = bf16[64,512]{1,0:T(8,128)(2,1)} async-done(((bf16[1024,512]{1,0:T(8,128)(2,1)}), bf16[64,512]{1,0:T(8,128)(2,1)}) %reduce-scatter.19.cloned.1.call-update) | async-done | bytes 65552 | tf_op jit(solution)/shard_map/reduce_scatter | solution.py:43
  1137.7 75.3 %reduce-scatter.17.cloned.1.call-done = bf16[64,512]{1,0:T(8,128)(2,1)} async-done(((bf16[1024,512]{1,0:T(8,128)(2,1)}), bf16[64,512]{1,0:T(8,128)(2,1)}) %reduce-scatter.17.cloned.1.call-update) | async-done | bytes 65552 | tf_op jit(solution)/shard_map/reduce_scatter | solution.py:43
  1216.3 90.5 %reduce-scatter.27.cloned.1.call-done = bf16[64,2048]{1,0:T(8,128)(2,1)} async-done(((bf16[1024,2048]{1,0:T(8,128)(2,1)}), bf16[64,2048]{1,0:T(8,128)(2,1)}) %reduce-scatter.27.cloned.1.call-update) | async-done | bytes 262160 | tf_op jit(solution)/shard_map/reduce_scatter | solution.py:43
  1308.5 95.1 %reduce-scatter.29.cloned.1.call-done = bf16[2048,64]{0,1:T(8,128)(2,1)} async-done(((bf16[2048,1024]{0,1:T(8,128)(2,1)}), bf16[2048,64]{0,1:T(8,128)(2,1)}) %reduce-scatter.29.cloned.1.call-update) | async-done | bytes 262160 | tf_op jit(solution)/shard_map/reduce_scatter | solution.py:43
  (491 shorter events, 735.5 us)
Async XLA Ops:
  7.2 1032.0 %reduce-scatter.25.cloned.1.call-start = ((), (), s32[]{:S(2)}) async-start(), calls=%async_computation.15 | async-start | bytes 1114112 | tf_op jit(solution)/shard_map/reduce_scatter | solution.py:43
  10.6 47.4 %collective-permute-start = (bf16[1024]{0:T(1024)(128)(2,1)S(1)}, bf16[1024]{0:T(1024)(128)(2,1)S(1)}, u32[]{:S(2)}, u32[]{:S(2)}) collective-permute-start(bf16[1024]{0:T(1024)(128)(2,1)S(1)} %get-tuple-element.708), channel_id=1, source_target_pairs={{0,2},{2,4},{4,6},{6,8},{8,10},{10,12},{12,14},{14,16},{16,18},{18... | collective-permute-start | bytes 6152 | tf_op jit(solution)/shard_map/ppermute | solution.py:17
  22.7 38.3 %collective-permute-start.1 = (bf16[1024,512]{1,0:T(8,128)(2,1)}, bf16[1024,512]{1,0:T(8,128)(2,1)}, u32[]{:S(2)}, u32[]{:S(2)}) collective-permute-start(bf16[1024,512]{1,0:T(8,128)(2,1)} %convolution_convert_fusion.17), channel_id=1, source_target_pairs={{0,2},{2,4},{4,6},{6,8},{8,10},{10,12},{12,14},{14,16},{16,18},{18... | collective-permute-start | bytes 3145736 | tf_op jit(solution)/shard_map/ppermute | solution.py:17
  29.5 43.1 %collective-permute-start.2 = (bf16[1024,512]{1,0:T(8,128)(2,1)}, bf16[1024,512]{1,0:T(8,128)(2,1)}, u32[]{:S(2)}, u32[]{:S(2)}) collective-permute-start(bf16[1024,512]{1,0:T(8,128)(2,1)} %add_convert_fusion.7), channel_id=1, source_target_pairs={{0,2},{2,4},{4,6},{6,8},{8,10},{10,12},{12,14},{14,16},{16,18},{18... | collective-permute-start | bytes 3145736 | tf_op jit(solution)/shard_map/ppermute | solution.py:17
  44.1 153.9 %collective-permute-start.5 = (bf16[588,512]{1,0:T(8,128)(2,1)}, bf16[588,512]{1,0:T(8,128)(2,1)}, u32[]{:S(2)}, u32[]{:S(2)}) collective-permute-start(bf16[588,512]{1,0:T(8,128)(2,1)} %constant_dynamic-slice_fusion), channel_id=1, source_target_pairs={{0,2},{2,4},{4,6},{6,8},{8,10},{10,12},{12,14},{14,16},{16,18},{18... | collective-permute-start | bytes 1806344 | tf_op jit(solution)/shard_map/ppermute | solution.py:17
  187.5 27.3 %collective-permute-start.3 = (bf16[1024,1024]{0,1:T(8,128)(2,1)}, bf16[1024,1024]{0,1:T(8,128)(2,1)}, u32[]{:S(2)}, u32[]{:S(2)}) collective-permute-start(bf16[1024,1024]{0,1:T(8,128)(2,1)} %convolution_convert_fusion.8), channel_id=1, source_target_pairs={{0,1},{1,0},{2,3},{3,2},{4,5},{5,4},{6,7},{7,6},{8,9},{9,8},{10,11... | collective-permute-start | bytes 6291464 | tf_op jit(solution)/shard_map/ppermute | solution.py:22
  191.1 18.3 %collective-permute-start.4 = (bf16[588,512]{1,0:T(8,128)(2,1)}, bf16[588,512]{1,0:T(8,128)(2,1)S(1)}, u32[]{:S(2)}, u32[]{:S(2)}) collective-permute-start(bf16[588,512]{1,0:T(8,128)(2,1)} %constant_dynamic-slice_fusion.1), channel_id=1, source_target_pairs={{0,2},{2,4},{4,6},{6,8},{8,10},{10,12},{12,14},{14,16},{16,18},{18... | collective-permute-start | bytes 1806344 | tf_op jit(solution)/shard_map/ppermute | solution.py:17
  414.3 626.5 %reduce-scatter.23.cloned.1.call-start = ((), (), s32[]{:S(2)}) async-start(), calls=%async_computation.14 | async-start | bytes 1114112 | tf_op jit(solution)/shard_map/reduce_scatter | solution.py:43
  616.8 425.5 %reduce-scatter.33.cloned.1.call-start = ((), (), s32[]{:S(2)}) async-start(), calls=%async_computation.19 | async-start | bytes 1114112
  619.5 22.1 %collective-permute-start.13 = (bf16[588,512]{1,0:T(8,128)(2,1)}, bf16[588,512]{1,0:T(8,128)(2,1)}, u32[]{:S(2)}, u32[]{:S(2)}) collective-permute-start(bf16[588,512]{1,0:T(8,128)(2,1)} %copy.219), channel_id=1, source_target_pairs={{2,0},{4,2},{6,4},{8,6},{10,8},{12,10},{14,12},{16,14},{18,16},{20... | collective-permute-start | bytes 1806344 | tf_op jit(solution)/shard_map/ppermute | solution.py:17
  623.5 30.6 %collective-permute-start.14 = (bf16[588,512]{1,0:T(8,128)(2,1)}, bf16[588,512]{1,0:T(8,128)(2,1)}, u32[]{:S(2)}, u32[]{:S(2)}) collective-permute-start(bf16[588,512]{1,0:T(8,128)(2,1)} %copy.221), channel_id=1, source_target_pairs={{2,0},{4,2},{6,4},{8,6},{10,8},{12,10},{14,12},{16,14},{18,16},{20... | collective-permute-start | bytes 1806344 | tf_op jit(solution)/shard_map/ppermute | solution.py:17
  676.0 368.0 %reduce-scatter.31.cloned.1.call-start = ((), (), s32[]{:S(2)}) async-start(), calls=%async_computation.18 | async-start | bytes 1114112
  676.0 15.3 %collective-permute-start.9 = (bf16[1024,1024]{0,1:T(8,128)(2,1)S(1)}, bf16[1024,1024]{0,1:T(8,128)(2,1)}, u32[]{:S(2)}, u32[]{:S(2)}) collective-permute-start(bf16[1024,1024]{0,1:T(8,128)(2,1)S(1)} %multiply_convert_fusion.3), channel_id=1, source_target_pairs={{0,1},{1,0},{2,3},{3,2},{4,5},{5,4},{6,7},{7,6},{8,9},{9,8},{10,11... | collective-permute-start | bytes 6291464 | tf_op jit(solution)/shard_map/ppermute | solution.py:22
  691.2 376.0 %reduce-scatter.21.cloned.1.call-start = ((), (), s32[]{:S(2)}) async-start(), calls=%async_computation.13 | async-start | bytes 1114112 | tf_op jit(solution)/shard_map/reduce_scatter | solution.py:43
  715.2 353.5 %reduce-scatter.15.cloned.1.call-start = ((), (), s32[]{:S(2)}) async-start(), calls=%async_computation.10 | async-start | bytes 1114112 | tf_op jit(solution)/shard_map/reduce_scatter | solution.py:43
  930.0 206.2 %reduce-scatter.19.cloned.1.call-start = ((), (), s32[]{:S(2)}) async-start(), calls=%async_computation.12 | async-start | bytes 1114112 | tf_op jit(solution)/shard_map/reduce_scatter | solution.py:43
  931.8 30.4 %collective-permute-start.11 = (bf16[1024,512]{0,1:T(8,128)(2,1)S(1)}, bf16[1024,512]{0,1:T(8,128)(2,1)S(1)}, u32[]{:S(2)}, u32[]{:S(2)}) collective-permute-start(bf16[1024,512]{0,1:T(8,128)(2,1)S(1)} %bitcast.304), channel_id=1, source_target_pairs={{2,0},{4,2},{6,4},{8,6},{10,8},{12,10},{14,12},{16,14},{18,16},{20... | collective-permute-start | bytes 3145736 | tf_op jit(solution)/shard_map/ppermute | solution.py:17
  964.8 248.1 %reduce-scatter.17.cloned.1.call-start = ((), (), s32[]{:S(2)}) async-start(), calls=%async_computation.11 | async-start | bytes 1114112 | tf_op jit(solution)/shard_map/reduce_scatter | solution.py:43
  966.6 30.5 %collective-permute-start.10 = (bf16[1024,512]{0,1:T(8,128)(2,1)S(1)}, bf16[1024,512]{0,1:T(8,128)(2,1)S(1)}, u32[]{:S(2)}, u32[]{:S(2)}) collective-permute-start(bf16[1024,512]{0,1:T(8,128)(2,1)S(1)} %bitcast.305), channel_id=1, source_target_pairs={{2,0},{4,2},{6,4},{8,6},{10,8},{12,10},{14,12},{16,14},{18,16},{20... | collective-permute-start | bytes 3145736 | tf_op jit(solution)/shard_map/ppermute | solution.py:17
  1000.8 306.0 %reduce-scatter.27.cloned.1.call-start = ((), (), s32[]{:S(2)}) async-start(), calls=%async_computation.16 | async-start | bytes 4456448 | tf_op jit(solution)/shard_map/reduce_scatter | solution.py:43
  1011.0 392.6 %reduce-scatter.29.cloned.1.call-start = ((), (), s32[]{:S(2)}) async-start(), calls=%async_computation.17 | async-start | bytes 4456448 | tf_op jit(solution)/shard_map/reduce_scatter | solution.py:43
  1027.1 18.6 %collective-permute-start.12 = (bf16[1024,1024]{0,1:T(8,128)(2,1)}, bf16[1024,1024]{0,1:T(8,128)(2,1)}, u32[]{:S(2)}, u32[]{:S(2)}) collective-permute-start(bf16[1024,1024]{0,1:T(8,128)(2,1)} %add_convert_fusion.3), channel_id=1, source_target_pairs={{0,1},{1,0},{2,3},{3,2},{4,5},{5,4},{6,7},{7,6},{8,9},{9,8},{10,11... | collective-permute-start | bytes 6291464 | tf_op jit(solution)/shard_map/ppermute | solution.py:22
  1049.9 20.3 %collective-permute-start.16 = (f32[104,128]{1,0:T(8,128)S(1)}, f32[104,128]{1,0:T(8,128)S(1)}, u32[]{:S(2)}, u32[]{:S(2)}) collective-permute-start(f32[104,128]{1,0:T(8,128)S(1)} %bitcast.306), channel_id=1, source_target_pairs={{0,2},{2,0},{4,6},{6,4},{8,10},{10,8},{12,14},{14,12},{16,18},{18,... | collective-permute-start | bytes 159752 | tf_op jit(solution)/shard_map/ppermute | solution.py:32
  1079.3 135.2 %collective-permute-start.19 = (f32[104,128]{1,0:T(8,128)S(1)}, f32[104,128]{1,0:T(8,128)S(1)}, u32[]{:S(2)}, u32[]{:S(2)}) collective-permute-start(f32[104,128]{1,0:T(8,128)S(1)} %add.318), channel_id=1, source_target_pairs={{0,16},{2,18},{4,20},{6,22},{8,24},{10,26},{12,28},{14,30},{16,0},... | collective-permute-start | bytes 159752 | tf_op jit(solution)/shard_map/ppermute | solution.py:32
  (111 other events, 1050.4 us)
Sparse Core Ops, SparseCore 0:
  414.4 81.5 reduce-scatter.24
  616.9 99.4 reduce-scatter.22
  718.7 76.6 reduce-scatter.32
  797.6 74.2 reduce-scatter.30
  874.0 89.1 reduce-scatter.20
  965.3 91.7 reduce-scatter.14
  1059.4 76.6 reduce-scatter.18
  1138.5 74.3 reduce-scatter.16
  1215.2 91.4 reduce-scatter.26
  1308.9 94.6 reduce-scatter.28

commit v2 on v1

--- a/solution.py
+++ b/solution.py
@@ -1,8 +1,11 @@
+import functools
 import math
 
 import jax
 import jax.numpy as jnp
 from jax import lax
+from jax.experimental import pallas as pl
+from jax.experimental.pallas import tpu as pltpu
 from jax.sharding import PartitionSpec as P
 
 HEAD_WIDTH = 64
@@ -63,74 +66,471 @@
     return (inner * inverse, jnp.sum(grad * normed, axis=0), jnp.sum(grad, axis=0))
 
 
-def block_scores(query_block, allowed_block, key_table):
-    scores = jnp.einsum("thd,chd->htc", query_block, key_table, preferred_element_type=jnp.float32)
-    return jnp.where(allowed_block[None], scores, -1e30)
-
-
-def attend_forward(query_blocks, allowed, key_table, value_table):
-    block_rows = query_blocks.shape[1]
-    local_width = query_blocks.shape[2] * query_blocks.shape[3]
-
-    def forward_block(carry, block):
-        query_block, allowed_block = block
-        scores = block_scores(query_block, allowed_block, key_table)
-        highest = jnp.max(scores, axis=-1, keepdims=True)
-        raised = jnp.exp(scores - highest)
-        total = jnp.sum(raised, axis=-1, keepdims=True)
-        weights = (raised / total).astype(jnp.bfloat16)
-        mixed = jnp.einsum("htc,chd->thd", weights, value_table, preferred_element_type=jnp.float32)
-        return (
-            carry,
-            (
-                mixed.reshape(block_rows, local_width).astype(jnp.bfloat16),
-                (highest + jnp.log(total))[..., 0],
-            ),
-        )
-
-    unused_carry, (attended, log_totals) = lax.scan(
-        forward_block, jnp.zeros((), jnp.float32), (query_blocks, allowed)
-    )
-    return (attended.reshape(-1, local_width), log_totals)
-
-
-def attend_backward(query_blocks, allowed, log_totals, grad_rows, key_table, value_table):
-    block_count, block_rows, local_heads, head_size = query_blocks.shape
-    key_count = key_table.shape[0]
-
-    def backward_block(carry, block):
-        query_block, allowed_block, log_block, grad_block = block
-        scores = block_scores(query_block, allowed_block, key_table)
-        probs = jnp.exp(scores - log_block[..., None])
-        weights = probs.astype(jnp.bfloat16)
-        value_grads = carry[1] + jnp.einsum(
-            "htc,thd->chd", weights, grad_block, preferred_element_type=jnp.float32
-        )
-        grad_probs = jnp.einsum(
-            "thd,chd->htc", grad_block, value_table, preferred_element_type=jnp.float32
-        )
-        grad_scores = (
-            probs * (grad_probs - jnp.sum(grad_probs * probs, axis=-1, keepdims=True))
-        ).astype(jnp.bfloat16)
-        grad_query = jnp.einsum(
-            "htc,chd->thd", grad_scores, key_table, preferred_element_type=jnp.float32
-        ).astype(jnp.bfloat16)
-        key_grads = carry[0] + jnp.einsum(
-            "htc,thd->chd", grad_scores, query_block, preferred_element_type=jnp.float32
-        )
-        return ((key_grads, value_grads), grad_query.reshape(block_rows, local_heads * head_size))
-
-    empty_grads = jnp.zeros((key_count, local_heads, head_size), jnp.float32)
-    grad_blocks = grad_rows.reshape(block_count, block_rows, local_heads, head_size)
-    (key_grads, value_grads), grad_queries = lax.scan(
-        backward_block, (empty_grads, empty_grads), (query_blocks, allowed, log_totals, grad_blocks)
-    )
-    local_width = local_heads * head_size
-    return (
-        key_grads.reshape(key_count, local_width),
-        value_grads.reshape(key_count, local_width),
-        grad_queries.reshape(-1, local_width),
-    )
+BF = jnp.bfloat16
+F32 = jnp.float32
+NEG = -1e30
+TILE = 256
+PAIR = 2 * HEAD_WIDTH
+VMEM_LIMIT = 60 * 1024 * 1024
+
+
+def nt(left, right):
+    return lax.dot_general(left, right, (((1,), (1,)), ((), ())), preferred_element_type=F32)
+
+
+def nn(left, right):
+    return lax.dot_general(left, right, (((1,), (0,)), ((), ())), preferred_element_type=F32)
+
+
+def head_half(pair, half):
+    lane = lax.broadcasted_iota(jnp.int32, pair.shape, 1)
+    keep = lane < HEAD_WIDTH if half == 0 else lane >= HEAD_WIDTH
+    return jnp.where(keep, pair, jnp.zeros_like(pair))
+
+
+def span(index, size=TILE):
+    return pl.ds(pl.multiple_of(index * size, size), size)
+
+
+HEAD_ROWS = 80
+
+
+def column_max(values):
+    rows = values.shape[0]
+    groups = max(1, rows // 64)
+    step = -(-(rows // groups) // 8) * 8
+    parts = []
+    at = 0
+    while at < rows:
+        end = min(rows, at + step)
+        parts.append(jnp.max(values[at:end], axis=0, keepdims=True))
+        at = end
+    while len(parts) > 1:
+        parts = [jnp.maximum(*parts[i : i + 2]) if i + 1 < len(parts) else parts[i] for i in range(0, len(parts), 2)]
+    return parts[0]
+
+
+def extended(values, target, columns):
+    turned = values.T
+    extra = jnp.where(lax.broadcasted_iota(jnp.int32, (HEAD_ROWS - HEAD_WIDTH, turned.shape[1]), 0) == 0, 1.0, 0.0).astype(BF)
+    for h in range(turned.shape[0] // HEAD_WIDTH):
+        base = h * HEAD_ROWS
+        target[base : base + HEAD_WIDTH, columns] = turned[h * HEAD_WIDTH : (h + 1) * HEAD_WIDTH, :]
+        target[base + HEAD_WIDTH : base + HEAD_ROWS, columns] = extra
+
+
+def lane_rows(i):
+    return i * TILE + lax.broadcasted_iota(jnp.int32, (1, TILE), 1)
+
+
+def self_forward_body(meta, q_ref, kp_ref, k_ref, vp_ref, v_ref, o_ref, log_ref,
+                      vpt, vt, qm, bias, m_s, acc, done, scores):
+    rows = q_ref.shape[0]
+    pairs = q_ref.shape[1] // PAIR
+    b1, b2, p0 = meta[0], meta[1], meta[2]
+    tiles = rows // TILE
+    first_prior = p0 // TILE
+    prior_rows = (b1 + TILE - 1) // TILE
+
+    def turn_own(j, c):
+        extended(v_ref[span(j), :], vt, span(j))
+        return c
+
+    lax.fori_loop(0, tiles, turn_own, 0)
+
+    def turn_prior(j, c):
+        extended(vp_ref[span(j), :], vpt, span(j))
+        return c
+
+    lax.fori_loop(jnp.where(b1 > 0, first_prior, tiles), tiles, turn_prior, 0)
+
+    def key_step(keys, values_t, j):
+        for pair in range(pairs):
+            key_pair = keys[span(j), pair * PAIR : pair * PAIR + PAIR]
+            for half in range(2):
+                scores[2 * pair + half] = nt(key_pair, qm[2 * pair + half])
+        for pair in range(pairs):
+            for half in range(2):
+                h = 2 * pair + half
+                heads = slice(h * HEAD_ROWS, (h + 1) * HEAD_ROWS)
+                s = scores[h] + bias[...]
+                m_old = m_s[h : h + 1, :]
+                m_new = jnp.maximum(m_old, column_max(s))
+                alpha = jnp.exp(m_old - m_new)
+                e = jnp.exp(s - m_new)
+                m_s[h : h + 1, :] = m_new
+                acc[heads, :] = acc[heads, :] * alpha + nn(values_t[heads, span(j)], e.astype(BF))
+
+    def row_tile(i, c):
+        t = lane_rows(i)
+        start = jnp.where(t < b1, 0, jnp.where(t < b2, b1, b2))
+        for pair in range(pairs):
+            q_pair = q_ref[span(i), pair * PAIR : pair * PAIR + PAIR]
+            for half in range(2):
+                qm[2 * pair + half] = head_half(q_pair, half)
+        m_s[...] = jnp.full_like(m_s, NEG)
+        acc[...] = jnp.zeros_like(acc)
+
+        def prior(j, c2):
+            r = j * TILE + lax.broadcasted_iota(jnp.int32, (TILE, TILE), 0)
+            bias[...] = jnp.where((r >= p0) & (t < b1), 0.0, NEG)
+            key_step(kp_ref, vpt, j)
+            return c2
+
+        lax.fori_loop(jnp.where(i < prior_rows, first_prior, tiles), tiles, prior, 0)
+        t_first = i * TILE
+        lowest = jnp.where(t_first < b1, 0, jnp.where(t_first < b2, b1, b2))
+
+        def own(j, c2):
+            r = j * TILE + lax.broadcasted_iota(jnp.int32, (TILE, TILE), 0)
+            bias[...] = jnp.where((r <= t) & (r >= start), 0.0, NEG)
+            key_step(k_ref, vt, j)
+            return c2
+
+        lax.fori_loop(lowest // TILE, i + 1, own, 0)
+        for h in range(2 * pairs):
+            base = h * HEAD_ROWS
+            total = acc[base + HEAD_WIDTH : base + HEAD_WIDTH + 1, :]
+            log_ref[h : h + 1, span(i)] = m_s[h : h + 1, :] + jnp.log(total)
+            done[h * HEAD_WIDTH : (h + 1) * HEAD_WIDTH, :] = acc[base : base + HEAD_WIDTH, :] * (1.0 / total)
+        o_ref[span(i), :] = done[...].T.astype(BF)
+        return c
+
+    lax.fori_loop(0, tiles, row_tile, 0)
+
+
+SMEM_SPEC = pl.BlockSpec(memory_space=pltpu.SMEM)
+VMEM_SPEC = pl.BlockSpec(memory_space=pltpu.VMEM)
+
+
+def self_forward(meta, q, k_prior, k, v_prior, v):
+    rows, width = q.shape
+    heads = width // HEAD_WIDTH
+    return pl.pallas_call(
+        self_forward_body,
+        out_shape=(jax.ShapeDtypeStruct((rows, width), BF), jax.ShapeDtypeStruct((heads, rows), F32)),
+        in_specs=[SMEM_SPEC] + [VMEM_SPEC] * 5,
+        out_specs=(VMEM_SPEC, VMEM_SPEC),
+        scratch_shapes=[
+            pltpu.VMEM((heads * HEAD_ROWS, rows), BF),
+            pltpu.VMEM((heads * HEAD_ROWS, rows), BF),
+            pltpu.VMEM((heads, TILE, PAIR), BF),
+            pltpu.VMEM((TILE, TILE), F32),
+            pltpu.VMEM((heads, TILE), F32),
+            pltpu.VMEM((heads * HEAD_ROWS, TILE), F32),
+            pltpu.VMEM((width, TILE), F32),
+            pltpu.VMEM((heads, TILE, TILE), F32),
+        ],
+        compiler_params=pltpu.CompilerParams(vmem_limit_bytes=VMEM_LIMIT),
+        cost_estimate=pl.CostEstimate(flops=2 * 2 * rows * rows * width, bytes_accessed=8 * rows * width * 2, transcendentals=rows * rows * heads),
+        name="self_forward",
+    )(meta, q, k_prior, k, v_prior, v)
+
+
+def grad_rows(do_ref, o_ref, i, width):
+    heads = width // HEAD_WIDTH
+    product = do_ref[span(i), :].astype(F32) * o_ref[span(i), :].astype(F32)
+    high = product.astype(BF)
+    low = (product - high.astype(F32)).astype(BF)
+    head = lax.broadcasted_iota(jnp.int32, (heads, width), 0)
+    column = lax.broadcasted_iota(jnp.int32, (heads, width), 1) // HEAD_WIDTH
+    pick = jnp.where(head == column, 1.0, 0.0).astype(BF)
+    return nt(pick, high) + nt(pick, low)
+
+
+def halves(source, i, target, pairs):
+    for pair in range(pairs):
+        value = source[span(i), pair * PAIR : pair * PAIR + PAIR]
+        for half in range(2):
+            target[2 * pair + half] = head_half(value, half)
+
+
+def grad_step(pairs, keys, values, keys_t, key_slice, key_lanes, qm, dom, shift, delta, bias, dk, dv, dqt, scores, grads):
+    for pair in range(pairs):
+        cols = slice(pair * PAIR, pair * PAIR + PAIR)
+        key_pair = keys[key_slice, cols]
+        value_pair = values[key_slice, cols]
+        for half in range(2):
+            h = 2 * pair + half
+            scores[h] = nt(key_pair, qm[h])
+            grads[h] = nt(value_pair, dom[h])
+    for pair in range(pairs):
+        cols = slice(pair * PAIR, pair * PAIR + PAIR)
+        dv_pair = dv[key_slice, cols]
+        dk_pair = dk[key_slice, cols]
+        for half in range(2):
+            h = 2 * pair + half
+            heads = slice(h * HEAD_WIDTH, (h + 1) * HEAD_WIDTH)
+            s = scores[h]
+            if bias is not None:
+                s = s + bias[...]
+            p = jnp.exp(s - shift[h : h + 1, :])
+            dp = grads[h]
+            ds = (p * (dp - delta[h : h + 1, :])).astype(BF)
+            dv_pair = dv_pair + nn(p.astype(BF), dom[h])
+            dk_pair = dk_pair + nn(ds, qm[h])
+            dqt[heads, :] = dqt[heads, :] + nn(keys_t[heads, key_lanes], ds)
+        dv[key_slice, cols] = dv_pair
+        dk[key_slice, cols] = dk_pair
+
+
+def self_prior_back_body(meta, q_ref, do_ref, o_ref, log_ref, k_ref, v_ref, dk_ref, dv_ref, dq_ref,
+                         kt, qm, dom, bias, delta, shift, dqt, dk, dv, scores, grads):
+    rows, width = q_ref.shape
+    pairs = width // PAIR
+    b1, p0 = meta[0], meta[2]
+    tiles = rows // TILE
+    first_prior = p0 // TILE
+    prior_rows = (b1 + TILE - 1) // TILE
+    dk[...] = jnp.zeros_like(dk)
+    dv[...] = jnp.zeros_like(dv)
+
+    def turn(j, c):
+        kt[:, span(j)] = k_ref[span(j), :].T
+        return c
+
+    lax.fori_loop(jnp.where(b1 > 0, first_prior, tiles), tiles, turn, 0)
+
+    def row_tile(i, c):
+        dqt[...] = jnp.zeros_like(dqt)
+        t = lane_rows(i)
+
+        @pl.when(i < prior_rows)
+        def _():
+            halves(q_ref, i, qm, pairs)
+            halves(do_ref, i, dom, pairs)
+            delta[...] = grad_rows(do_ref, o_ref, i, width)
+            shift[...] = log_ref[:, span(i)]
+
+        def prior(j, c2):
+            r = j * TILE + lax.broadcasted_iota(jnp.int32, (TILE, TILE), 0)
+            bias[...] = jnp.where((r >= p0) & (t < b1), 0.0, NEG)
+            grad_step(pairs, k_ref, v_ref, kt, span(j), span(j), qm, dom, shift, delta, bias, dk, dv, dqt, scores, grads)
+            return c2
+
+        lax.fori_loop(jnp.where(i < prior_rows, first_prior, tiles), tiles, prior, 0)
+        dq_ref[span(i), :] = dqt[...].T
+        return c
+
+    lax.fori_loop(0, tiles, row_tile, 0)
+    dk_ref[...] = dk[...].astype(BF)
+    dv_ref[...] = dv[...].astype(BF)
+
+
+def self_own_back_body(meta, q_ref, do_ref, o_ref, log_ref, k_ref, v_ref, dqp_ref, dk_ref, dv_ref, dq_ref,
+                       kt, qm, dom, bias, delta, shift, dqt, dk, dv, scores, grads):
+    rows, width = q_ref.shape
+    pairs = width // PAIR
+    b1, b2 = meta[0], meta[1]
+    tiles = rows // TILE
+    dk[...] = jnp.zeros_like(dk)
+    dv[...] = jnp.zeros_like(dv)
+
+    def turn(j, c):
+        kt[:, span(j)] = k_ref[span(j), :].T
+        return c
+
+    lax.fori_loop(0, tiles, turn, 0)
+
+    def row_tile(i, c):
+        dqt[...] = jnp.zeros_like(dqt)
+        t = lane_rows(i)
+        start = jnp.where(t < b1, 0, jnp.where(t < b2, b1, b2))
+        halves(q_ref, i, qm, pairs)
+        halves(do_ref, i, dom, pairs)
+        delta[...] = grad_rows(do_ref, o_ref, i, width)
+        shift[...] = log_ref[:, span(i)]
+        t_first = i * TILE
+        lowest = jnp.where(t_first < b1, 0, jnp.where(t_first < b2, b1, b2))
+
+        def own(j, c2):
+            r = j * TILE + lax.broadcasted_iota(jnp.int32, (TILE, TILE), 0)
+            bias[...] = jnp.where((r <= t) & (r >= start), 0.0, NEG)
+            grad_step(pairs, k_ref, v_ref, kt, span(j), span(j), qm, dom, shift, delta, bias, dk, dv, dqt, scores, grads)
+            return c2
+
+        lax.fori_loop(lowest // TILE, i + 1, own, 0)
+        dq_ref[span(i), :] = (dqp_ref[span(i), :] + dqt[...].T).astype(BF)
+        return c
+
+    lax.fori_loop(0, tiles, row_tile, 0)
+    dk_ref[...] = dk[...]
+    dv_ref[...] = dv[...]
+
+
+def self_back_scratch(rows, width):
+    heads = width // HEAD_WIDTH
+    return [
+        pltpu.VMEM((width, rows), BF),
+        pltpu.VMEM((heads, TILE, PAIR), BF),
+        pltpu.VMEM((heads, TILE, PAIR), BF),
+        pltpu.VMEM((TILE, TILE), F32),
+        pltpu.VMEM((heads, TILE), F32),
+        pltpu.VMEM((heads, TILE), F32),
+        pltpu.VMEM((width, TILE), F32),
+        pltpu.VMEM((rows, width), F32),
+        pltpu.VMEM((rows, width), F32),
+        pltpu.VMEM((heads, TILE, TILE), F32),
+        pltpu.VMEM((heads, TILE, TILE), F32),
+    ]
+
+
+def self_prior_back(meta, q, do, o, logs, k_prior, v_prior):
+    rows, width = q.shape
+    return pl.pallas_call(
+        self_prior_back_body,
+        out_shape=(jax.ShapeDtypeStruct((rows, width), BF), jax.ShapeDtypeStruct((rows, width), BF),
+                   jax.ShapeDtypeStruct((rows, width), F32)),
+        in_specs=[SMEM_SPEC] + [VMEM_SPEC] * 6,
+        out_specs=(VMEM_SPEC,) * 3,
+        scratch_shapes=self_back_scratch(rows, width),
+        compiler_params=pltpu.CompilerParams(vmem_limit_bytes=VMEM_LIMIT),
+        cost_estimate=pl.CostEstimate(flops=3 * rows * rows * width, bytes_accessed=8 * rows * width * 2, transcendentals=rows * rows * 4),
+        name="self_prior_back",
+    )(meta, q, do, o, logs, k_prior, v_prior)
+
+
+def self_own_back(meta, q, do, o, logs, k, v, dq_prior):
+    rows, width = q.shape
+    return pl.pallas_call(
+        self_own_back_body,
+        out_shape=(jax.ShapeDtypeStruct((rows, width), F32), jax.ShapeDtypeStruct((rows, width), F32),
+                   jax.ShapeDtypeStruct((rows, width), BF)),
+        in_specs=[SMEM_SPEC] + [VMEM_SPEC] * 7,
+        out_specs=(VMEM_SPEC,) * 3,
+        scratch_shapes=self_back_scratch(rows, width),
+        compiler_params=pltpu.CompilerParams(vmem_limit_bytes=VMEM_LIMIT),
+        cost_estimate=pl.CostEstimate(flops=5 * rows * rows * width, bytes_accessed=8 * rows * width * 2, transcendentals=rows * rows * 4),
+        name="self_own_back",
+    )(meta, q, do, o, logs, k, v, dq_prior)
+
+
+def segments(meta, rows):
+    return ((0, meta[0], meta[3]), (meta[0], meta[1], meta[4]), (meta[1], rows, meta[5]))
+
+
+def cross_forward_body(used, meta, q_ref, k_ref, v_ref, o_ref, log_ref, vt, qm, acc, scores):
+    rows, width = q_ref.shape
+    pairs = width // PAIR
+    padded = k_ref.shape[0] // 3
+    for slot in range(3):
+        extended(v_ref[slot * padded : (slot + 1) * padded, :], vt.at[slot], slice(None))
+    for first, last, slot in segments(meta, rows):
+        keys = pl.ds(pl.multiple_of(slot * padded, 16), padded)
+
+        def tile(i, c):
+            halves(q_ref, i, qm, pairs)
+            t = lane_rows(i)
+            inside = (t >= first) & (t < last)
+            for pair in range(pairs):
+                key_pair = k_ref[keys, pair * PAIR : pair * PAIR + PAIR]
+                for half in range(2):
+                    scores[2 * pair + half] = nt(key_pair, qm[2 * pair + half])
+            for pair in range(pairs):
+                for half in range(2):
+                    h = 2 * pair + half
+                    heads = slice(h * HEAD_WIDTH, (h + 1) * HEAD_WIDTH)
+                    s = scores[h]
+                    if used < padded:
+                        row = lax.broadcasted_iota(jnp.int32, s.shape, 0)
+                        s = jnp.where(row < used, s, NEG)
+                    m = column_max(s)
+                    e = jnp.exp(s - m)
+                    mixed = nn(vt[slot, h * HEAD_ROWS : (h + 1) * HEAD_ROWS, :], e.astype(BF))
+                    total = mixed[HEAD_WIDTH : HEAD_WIDTH + 1, :]
+                    acc[heads, :] = mixed[:HEAD_WIDTH, :] * (1.0 / total)
+                    log_ref[h : h + 1, span(i)] = jnp.where(
+                        inside, m + jnp.log(total), log_ref[h : h + 1, span(i)]
+                    )
+            column = i * TILE + lax.broadcasted_iota(jnp.int32, (TILE, width), 0)
+            keep = (column >= first) & (column < last)
+            o_ref[span(i), :] = jnp.where(keep, acc[...].T, o_ref[span(i), :].astype(F32)).astype(BF)
+            return c
+
+        lax.fori_loop(first // TILE, jnp.where(last > first, (last + TILE - 1) // TILE, 0), tile, 0)
+
+
+def cross_forward(used, meta, q, k, v):
+    rows, width = q.shape
+    heads = width // HEAD_WIDTH
+    padded = k.shape[0] // 3
+    return pl.pallas_call(
+        functools.partial(cross_forward_body, used),
+        out_shape=(jax.ShapeDtypeStruct((rows, width), BF), jax.ShapeDtypeStruct((heads, rows), F32)),
+        in_specs=[SMEM_SPEC] + [VMEM_SPEC] * 3,
+        out_specs=(VMEM_SPEC, VMEM_SPEC),
+        scratch_shapes=[
+            pltpu.VMEM((3, heads * HEAD_ROWS, padded), BF),
+            pltpu.VMEM((heads, TILE, PAIR), BF),
+            pltpu.VMEM((width, TILE), F32),
+            pltpu.VMEM((heads, padded, TILE), F32),
+        ],
+        compiler_params=pltpu.CompilerParams(vmem_limit_bytes=VMEM_LIMIT),
+        cost_estimate=pl.CostEstimate(flops=4 * rows * padded * width, bytes_accessed=8 * rows * width * 2, transcendentals=rows * padded * heads),
+        name="cross_forward",
+    )(meta, q, k, v)
+
+
+def cross_back_body(used, meta, q_ref, do_ref, o_ref, log_ref, k_ref, v_ref, dk_ref, dv_ref, dq_ref,
+                    kt, qm, dom, delta, shift, dqt, dk, dv, scores, grads):
+    rows, width = q_ref.shape
+    pairs = width // PAIR
+    padded = k_ref.shape[0] // 3
+    dk[...] = jnp.zeros_like(dk)
+    dv[...] = jnp.zeros_like(dv)
+    for slot in range(3):
+        kt[slot] = k_ref[slot * padded : (slot + 1) * padded, :].T
+    for first, last, slot in segments(meta, rows):
+        keys = pl.ds(pl.multiple_of(slot * padded, 16), padded)
+
+        def tile(i, c):
+            halves(q_ref, i, qm, pairs)
+            halves(do_ref, i, dom, pairs)
+            t = lane_rows(i)
+            inside = (t >= first) & (t < last)
+            delta[...] = grad_rows(do_ref, o_ref, i, width)
+            shift[...] = jnp.where(inside, log_ref[:, span(i)], -NEG)
+            dqt[...] = jnp.zeros_like(dqt)
+            grad_step(pairs, k_ref, v_ref, kt.at[slot], keys, slice(None), qm, dom, shift, delta, None, dk, dv, dqt, scores, grads)
+            column = i * TILE + lax.broadcasted_iota(jnp.int32, (TILE, width), 0)
+            keep = (column >= first) & (column < last)
+            dq_ref[span(i), :] = jnp.where(keep, dqt[...].T, dq_ref[span(i), :].astype(F32)).astype(BF)
+            return c
+
+        lax.fori_loop(first // TILE, jnp.where(last > first, (last + TILE - 1) // TILE, 0), tile, 0)
+    inner = lax.broadcasted_iota(jnp.int32, (padded, width), 0) < used
+    for slot in range(3):
+        part = slice(slot * padded, (slot + 1) * padded)
+        dk_ref[part, :] = jnp.where(inner, dk[part, :], 0.0).astype(BF)
+        dv_ref[part, :] = jnp.where(inner, dv[part, :], 0.0).astype(BF)
+
+
+def cross_back(used, meta, q, do, o, logs, k, v):
+    rows, width = q.shape
+    heads = width // HEAD_WIDTH
+    padded = k.shape[0] // 3
+    return pl.pallas_call(
+        functools.partial(cross_back_body, used),
+        out_shape=(jax.ShapeDtypeStruct(k.shape, BF), jax.ShapeDtypeStruct(k.shape, BF),
+                   jax.ShapeDtypeStruct((rows, width), BF)),
+        in_specs=[SMEM_SPEC] + [VMEM_SPEC] * 6,
+        out_specs=(VMEM_SPEC,) * 3,
+        scratch_shapes=[
+            pltpu.VMEM((3, width, padded), BF),
+            pltpu.VMEM((heads, TILE, PAIR), BF),
+            pltpu.VMEM((heads, TILE, PAIR), BF),
+            pltpu.VMEM((heads, TILE), F32),
+            pltpu.VMEM((heads, TILE), F32),
+            pltpu.VMEM((width, TILE), F32),
+            pltpu.VMEM(k.shape, F32),
+            pltpu.VMEM(k.shape, F32),
+            pltpu.VMEM((heads, padded, TILE), F32),
+            pltpu.VMEM((heads, padded, TILE), F32),
+        ],
+        compiler_params=pltpu.CompilerParams(vmem_limit_bytes=VMEM_LIMIT),
+        cost_estimate=pl.CostEstimate(flops=10 * rows * padded * width, bytes_accessed=12 * rows * width * 2, transcendentals=rows * padded * heads),
+        name="cross_back",
+    )(meta, q, do, o, logs, k, v)
 
 
 def per_device(
@@ -167,12 +567,15 @@
     row_count, width = tokens.shape
     image_count, memory_rows = (memory.shape[0], memory.shape[1])
     half_width = w_query.shape[1]
-    local_heads = half_width // HEAD_WIDTH
     scale = 1.0 / math.sqrt(HEAD_WIDTH)
-    block_rows = min(row_count, 512)
-    block_count = row_count // block_rows
-    own_rows = image_count * memory_rows
-    key_count = own_rows + memory_rows
+    padded_rows = -(-memory_rows // 16) * 16
+    own_rows = image_count * padded_rows
+    first_page = lax.axis_index("dp") * image_count
+    local_page = page_ids - first_page
+    begins = [jnp.sum((local_page < page).astype(jnp.int32)) for page in range(image_count)]
+    prior_begin = shifted(jnp.full((128,), begins[1], jnp.int32), "dp", 1)[0]
+    slots = [jnp.int32(image_count)] + [image_of_page[page] - first_page for page in range(image_count)]
+    meta = jnp.stack(begins + [prior_begin] + slots).astype(jnp.int32)
     input_values = tokens.astype(jnp.float32)
     hidden_zero, self_normed_rows, inverse_zero = layer_norm(input_values, ln0_gain, ln0_bias)
     hidden_zero = hidden_zero.astype(jnp.bfloat16)
@@ -186,62 +589,36 @@
     self_values = (
         jnp.dot(hidden_zero, w_self_value, preferred_element_type=jnp.float32) + b_self_value
     ).astype(jnp.bfloat16)
-    last_mark = (page_ids == page_ids[row_count - 1]).astype(jnp.bfloat16)
-    prior_keys, prior_values, prior_mark = shifted((self_key_rows, self_values, last_mark), "dp", 1)
-    self_key_table = jnp.concatenate([prior_keys, self_key_rows], 0).reshape(
-        2 * row_count, local_heads, HEAD_WIDTH
-    )
-    self_value_table = jnp.concatenate([prior_values, self_values], 0).reshape(
-        2 * row_count, local_heads, HEAD_WIDTH
-    )
-    positions = jnp.arange(row_count, dtype=jnp.int32)
-    own_ok = (page_ids[:, None] == page_ids[None, :]) & (positions[None, :] <= positions[:, None])
-    prior_ok = (prior_mark[None, :] > 0.5) & (page_ids == page_ids[0])[:, None]
-    self_allowed = jnp.concatenate([prior_ok, own_ok], 1).reshape(
-        block_count, block_rows, 2 * row_count
-    )
-    self_query_blocks = self_queries.reshape(block_count, block_rows, local_heads, HEAD_WIDTH)
-    self_attended, self_logs = attend_forward(
-        self_query_blocks, self_allowed, self_key_table, self_value_table
+    prior_keys, prior_values = shifted((self_key_rows, self_values), "dp", 1)
+    self_attended, self_logs = self_forward(
+        meta, self_queries, prior_keys, self_key_rows, prior_values, self_values
     )
     self_branch = (
         core_sum(jnp.dot(self_attended, w_self_out, preferred_element_type=jnp.float32))
         + b_self_out
     )
     start = input_values + self_branch
-    first_page = lax.axis_index("dp") * image_count
-    local_page = page_ids - first_page
-    picked = local_page[:, None] == jnp.arange(image_count, dtype=jnp.int32)[None, :]
-    token_image = jnp.sum(jnp.where(picked, image_of_page[None, :], 0), axis=1)
-    token_slot = jnp.where(local_page >= 0, token_image - first_page, image_count)
-    key_slot = jnp.repeat(jnp.arange(image_count + 1, dtype=jnp.int32), memory_rows)
-    allowed = (token_slot[:, None] == key_slot[None, :]).reshape(block_count, block_rows, key_count)
     last_image = image_of_page[image_count - 1] - first_page
-    flat_memory = memory.reshape(own_rows, width)
+    flat_memory = jnp.pad(memory, ((0, 0), (0, padded_rows - memory_rows), (0, 0))).reshape(own_rows, width)
     keys_here = jnp.dot(flat_memory, w_key, preferred_element_type=jnp.float32).astype(jnp.bfloat16)
     values_here = (
         jnp.dot(flat_memory, w_value, preferred_element_type=jnp.float32) + b_value
     ).astype(jnp.bfloat16)
 
     def tail_rows(matrix):
-        return lax.dynamic_slice_in_dim(matrix, last_image * memory_rows, memory_rows, 0)
+        return lax.dynamic_slice_in_dim(matrix, last_image * padded_rows, padded_rows, 0)
 
     prior_image_keys, prior_image_values = shifted(
         (tail_rows(keys_here), tail_rows(values_here)), "dp", 1
     )
-    all_keys = jnp.concatenate([keys_here, prior_image_keys], 0).reshape(
-        key_count, local_heads, HEAD_WIDTH
-    )
-    all_values = jnp.concatenate([values_here, prior_image_values], 0).reshape(
-        key_count, local_heads, HEAD_WIDTH
-    )
+    all_keys = jnp.concatenate([keys_here, prior_image_keys], 0)
+    all_values = jnp.concatenate([values_here, prior_image_values], 0)
     hidden_one, normed_one, inverse_one = layer_norm(start, ln1_gain, ln1_bias)
     hidden_one = hidden_one.astype(jnp.bfloat16)
     queries = (
         (jnp.dot(hidden_one, w_query, preferred_element_type=jnp.float32) + b_query) * scale
     ).astype(jnp.bfloat16)
-    query_blocks = queries.reshape(block_count, block_rows, local_heads, HEAD_WIDTH)
-    attended, log_totals = attend_forward(query_blocks, allowed, all_keys, all_values)
+    attended, log_totals = cross_forward(memory_rows, meta, queries, all_keys, all_values)
     branch = (
         core_sum(jnp.dot(attended, w_out, preferred_element_type=jnp.float32)) + b_out
     )
@@ -273,8 +650,8 @@
     grad_attended = jnp.einsum(
         "td,hd->th", grad_branch, w_out, preferred_element_type=jnp.float32
     ).astype(jnp.bfloat16)
-    key_grads, value_grads, grad_queries = attend_backward(
-        query_blocks, allowed, log_totals, grad_attended, all_keys, all_values
+    key_grads, value_grads, grad_queries = cross_back(
+        memory_rows, meta, queries, grad_attended, attended, log_totals, all_keys, all_values
     )
     returned_keys, returned_values = (
         shifted(key_grads[own_rows:].astype(jnp.bfloat16), "dp", -1).astype(jnp.float32),
@@ -282,12 +659,12 @@
     )
 
     def add_back(local_part, returned):
-        begin = last_image * memory_rows
-        current = lax.dynamic_slice_in_dim(local_part, begin, memory_rows, 0)
+        begin = last_image * padded_rows
+        current = lax.dynamic_slice_in_dim(local_part, begin, padded_rows, 0)
         return lax.dynamic_update_slice_in_dim(local_part, current + returned, begin, 0)
 
-    key_total = add_back(key_grads[:own_rows], returned_keys).astype(jnp.bfloat16)
-    value_total = add_back(value_grads[:own_rows], returned_values).astype(jnp.bfloat16)
+    key_total = add_back(key_grads[:own_rows].astype(jnp.float32), returned_keys).astype(jnp.bfloat16)
+    value_total = add_back(value_grads[:own_rows].astype(jnp.float32), returned_values).astype(jnp.bfloat16)
     grad_key = jnp.einsum("md,me->de", flat_memory, key_total, preferred_element_type=jnp.float32)
     grad_value = jnp.einsum(
         "md,me->de", flat_memory, value_total, preferred_element_type=jnp.float32
@@ -309,7 +686,7 @@
         grad_hidden_one, normed_one, inverse_one, ln1_gain
     )
     grad_start = grad_middle + back_one
-    d_memory = grad_memory.reshape(image_count, memory_rows, width).astype(jnp.bfloat16)
+    d_memory = grad_memory.reshape(image_count, padded_rows, width)[:, :memory_rows].astype(jnp.bfloat16)
     grad_start_low = grad_start.astype(jnp.bfloat16)
     grad_self_out = jnp.einsum(
         "th,td->hd", self_attended, grad_start_low, preferred_element_type=jnp.float32
@@ -318,20 +695,22 @@
     grad_self_attended = jnp.einsum(
         "td,hd->th", grad_start_low, w_self_out, preferred_element_type=jnp.float32
     ).astype(jnp.bfloat16)
-    self_key_grads, self_value_grads, grad_self_queries = attend_backward(
-        self_query_blocks,
-        self_allowed,
+    prior_key_grads, prior_value_grads, prior_query_grads = self_prior_back(
+        meta, self_queries, grad_self_attended, self_attended, self_logs, prior_keys, prior_values
+    )
+    later_keys, later_values = shifted((prior_key_grads, prior_value_grads), "dp", -1)
+    self_key_grads, self_value_grads, grad_self_queries = self_own_back(
+        meta,
+        self_queries,
+        grad_self_attended,
+        self_attended,
         self_logs,
-        grad_self_attended,
-        self_key_table,
-        self_value_table,
-    )
-    later_keys, later_values = (
-        shifted(self_key_grads[:row_count].astype(jnp.bfloat16), "dp", -1).astype(jnp.float32),
-        shifted(self_value_grads[:row_count].astype(jnp.bfloat16), "dp", -1).astype(jnp.float32),
-    )
-    self_key_total = (self_key_grads[row_count:] + later_keys).astype(jnp.bfloat16)
-    self_value_total = (self_value_grads[row_count:] + later_values).astype(jnp.bfloat16)
+        self_key_rows,
+        self_values,
+        prior_query_grads,
+    )
+    self_key_total = (self_key_grads + later_keys.astype(jnp.float32)).astype(jnp.bfloat16)
+    self_value_total = (self_value_grads + later_values.astype(jnp.float32)).astype(jnp.bfloat16)
     grad_self_query_w = (
         jnp.einsum("td,th->dh", hidden_zero, grad_self_queries, preferred_element_type=jnp.float32)
         * scale

time: 1420 us -> 1120 us (0.79)
  matrix products: 533 us -> 133 us
  waiting for transfers between devices: 400 us -> 734 us
  other arithmetic: 253 us -> 77.2 us
  local copies, waits for them, and re-layouts: 168 us -> 44.6 us
  Pallas kernels: 0 us -> 76.1 us
    dot_general x28 -> x0, matrix products: 393 us -> none  [the longest x8 109 us: block_scores(): jnp.einsum('thd,chd->htc', query_block, key_table, preferred_element_type...]
    reduce_scatter x8 -> x10, waiting for transfers between devices: 301 us -> 569 us  [scattered(): lax.psum_scatter(gradient.astype(jnp.bfloat16), 'dp', scatter_dimension=d...]
    convert_element_type x7 -> x2, other arithmetic: 113 us -> 1.94 us  [the longest x1 1.62 us: per_device(): value_grads[:own_rows].astype(jnp.float32)]
    pallas_call x0 -> x5, Pallas kernels: none -> 76.1 us  [the longest x1 25.4 us: cross_back(): pl.pallas_call(functools.partial(cross_back_body, used), out_shape=(jax.S...]
    ppermute x9, waiting for transfers between devices: 87.8 us -> 152 us  [shifted(): lax.ppermute(value, axis, [(source, source + steps) for source in range(i...]
    reduce_sum x5 -> x1, other arithmetic: 53.8 us -> 0.64 us  [per_device(): jnp.sum((local_page < page).astype(jnp.int32))]
    dynamic_update_slice x14 -> x0, local copies, waits for them, and re-layouts: 29.3 us -> none  [the longest x2 15.5 us: add_back(): lax.dynamic_update_slice_in_dim(local_part, current + returned, begin, 0)]
    reshape x5 -> x0, local copies, waits for them, and re-layouts: 15.3 us -> none  [the longest x2 6.7 us: attend_backward(): grad_rows.reshape(block_count, block_rows, local_heads, head_size)]
  transfers between devices with their start and end apart: 30 -> 30, of which waited for: 13 -> 18; matrix products, arithmetic and copies ran while one was open for 54% -> 15% of each run, Pallas kernels for 0% -> 5%
where the time goes in v2:
time: 1120 us; the launch traced here: 1110 us
  waiting for transfers between devices  734 us (66%)
  matrix products  133 us (12%)
  other arithmetic  77.2 us (7%)
  Pallas kernels  76.1 us (7%)
  local copies, waits for them, and re-layouts  44.6 us (4%)
  starting transfers between devices  30.4 us (3%)
  between operations  17 us (2%)
    reduce_scatter x10, waiting for transfers between devices, scattered(): lax.psum_scatter(gradient.astype(jnp.bfloat16), 'dp', scatter_dimension=d...  569 us
    ppermute x9, waiting for transfers between devices, shifted(): lax.ppermute(value, axis, [(source, source + steps) for source in range(i...  152 us
    unnamed x155, local copies, waits for them, and re-layouts  35 us
    ppermute x9, starting transfers between devices, shifted(): lax.ppermute(value, axis, [(source, source + steps) for source in range(i...  28.2 us
    pallas_call x1, Pallas kernels, cross_back(): pl.pallas_call(functools.partial(cross_back_body, used), out_shape=(jax.S...  25.4 us
    dot_general x1, matrix products, per_device(): jnp.einsum('td,fd->tf', cotangent, w_down, preferred_element_type=jnp.flo...  25.2 us
  transfers between devices with their start and end apart: 30, of which 18 were waited for; matrix products, arithmetic and copies ran while one was open for 15% of the time, Pallas kernels for 5%

profile of v2, /device:TPU:0, one launch (start us, length us, event | category | flops | bytes accessed | tf_op | source)
XLA Modules:
  0.0 1112.6 jit_solution(9098237582901722416)
XLA Ops:
  36.0 28.7 %collective-permute-done = s32[128]{0:T(128)S(1)} collective-permute-done((s32[128]{0:T(128)S(1)}, s32[128]{0:T(128)S(1)}, u32[]{:S(2)}, u32[]{:S(2)}) %collective-permute-start) | collective-permute-done | bytes 544 | tf_op jit(solution)/shard_map/ppermute | solution.py:20
  66.6 12.3 %self_forward.1 = (bf16[1024,512]{1,0:T(8,128)(2,1)}, f32[8,1024]{1,0:T(8,128)}) custom-call(s32[6]{0:T(128)} %stack.19.meta, bf16[1024,512]{1,0:T(8,128)(2,1)} %multiply_convert_fusion.5.q_ref, bf16[1024,512]{1,0:T(8,128)(2,1)} %collective-permute-done.1.kp_ref.k_ref, bf16[1024,512]{1,0:T(8,128)(2,1)} %convolution_convert_fusion.15.k_ref, ...), custom_call_target="tpu_custom_call" | custom-call | flops 2147483648 | bytes 8388608 | tf_op jit(solution)/shard_map/self_forward/pallas_call | solution.py:209
  90.5 8.5 collective-permute-start.4
  103.0 9.8 collective-permute-done.4
  114.2 11.2 %collective-permute-done.5 = bf16[592,512]{1,0:T(8,128)(2,1)S(1)} collective-permute-done((bf16[592,512]{1,0:T(8,128)(2,1)S(1)}, bf16[592,512]{1,0:T(8,128)(2,1)S(1)}, u32[]{:S(2)}, u32[]{:S(2)}) %collective-permute-start.5) | collective-permute-done | bytes 606240 | tf_op jit(solution)/shard_map/ppermute | solution.py:20
  135.6 12.7 %cross_forward.1 = (bf16[1024,512]{1,0:T(8,128)(2,1)}, f32[8,1024]{1,0:T(8,128)}) custom-call(s32[6]{0:T(128)} %stack.19.meta, bf16[1024,512]{1,0:T(8,128)(2,1)} %multiply_convert_fusion.4.q_ref, bf16[1776,512]{1,0:T(8,128)(2,1)} %pad_maximum_fusion.k_ref, bf16[1776,512]{1,0:T(8,128)(2,1)} %pad_maximum_fusion.1.v_ref), custom_call_target="tpu_custom_call" | custom-call | flops 1241513984 | bytes 8388608 | tf_op jit(solution)/shard_map/cross_forward/pallas_call | solution.py:457
  165.0 25.2 %convert_reduce_fusion = (f32[2048]{0:T(1024)S(1)}, bf16[1024,2048]{1,0:T(8,128)(2,1)}, f32[1024,2048]{1,0:T(8,128)}) fusion(f32[1024,2048]{1,0:T(8,128)S(1)} %fusion.41, f32[2048]{0:T(1024)S(1)} %copy-done.47, bf16[1024,1024]{1,0:T(8,128)(2,1)S(1)} %copy-done.29, bf16[2048,1024]{1,0:T(8,128)(2,1)S(1)} %copy-done.56), kind=kOutput, calls=%fused_computation.2 | convolution fusion | flops 4452251648 | bytes 27279360 | tf_op jit(solution)/shard_map/td,fd->tf/dot_general | solution.py:635
  190.2 10.0 multiply_convert_fusion
  239.4 25.4 %cross_back.1 = (bf16[1776,512]{1,0:T(8,128)(2,1)}, bf16[1776,512]{1,0:T(8,128)(2,1)}, bf16[1024,512]{1,0:T(8,128)(2,1)}) custom-call(s32[6]{0:T(128)} %stack.19.meta, bf16[1024,512]{1,0:T(8,128)(2,1)} %multiply_convert_fusion.4.q_ref, bf16[1024,512]{1,0:T(8,128)(2,1)} %convolution_convert_fusion.14.do_ref, bf16[1024,512]{1,0:T(8,128)(2,1)} %get-tuple-element.41.o_ref, ...), custom_call_target="tpu_custom_call" | custom-call | flops 3103784960 | bytes 12582912 | tf_op jit(solution)/shard_map/cross_back/pallas_call | solution.py:512
  275.4 20.7 %collective-permute-done.13 = bf16[592,512]{1,0:T(8,128)(2,1)S(1)} collective-permute-done((bf16[592,512]{1,0:T(8,128)(2,1)S(1)}, bf16[592,512]{1,0:T(8,128)(2,1)S(1)}, u32[]{:S(2)}, u32[]{:S(2)}) %collective-permute-start.13) | collective-permute-done | bytes 606240 | tf_op jit(solution)/shard_map/ppermute | solution.py:20
  304.7 18.4 %collective-permute-done.14 = bf16[592,512]{1,0:T(8,128)(2,1)S(1)} collective-permute-done((bf16[592,512]{1,0:T(8,128)(2,1)S(1)}, bf16[592,512]{1,0:T(8,128)(2,1)S(1)}, u32[]{:S(2)}, u32[]{:S(2)}) %collective-permute-start.14) | collective-permute-done | bytes 606240 | tf_op jit(solution)/shard_map/ppermute | solution.py:20
  344.4 19.7 %self_own_back.1 = (f32[1024,512]{1,0:T(8,128)}, f32[1024,512]{1,0:T(8,128)}, bf16[1024,512]{1,0:T(8,128)(2,1)}) custom-call(s32[6]{0:T(128)} %stack.19.meta, bf16[1024,512]{1,0:T(8,128)(2,1)} %multiply_convert_fusion.5.q_ref, bf16[1024,512]{1,0:T(8,128)(2,1)} %convolution_convert_fusion.13.do_ref, bf16[1024,512]{1,0:T(8,128)(2,1)} %get-tuple-element.40.o_ref, ...), custom_call_target="tpu_custom_call" | custom-call | flops 2684354560 | bytes 8388608 | tf_op jit(solution)/shard_map/self_own_back/pallas_call | solution.py:395
  374.4 35.7 %collective-permute-done.10 = bf16[1024,512]{1,0:T(8,128)(2,1)S(1)} collective-permute-done((bf16[1024,512]{1,0:T(8,128)(2,1)}, bf16[1024,512]{1,0:T(8,128)(2,1)S(1)}, u32[]{:S(2)}, u32[]{:S(2)}) %collective-permute-start.10) | collective-permute-done | bytes 1048608 | tf_op jit(solution)/shard_map/ppermute | solution.py:20
  417.3 27.8 %collective-permute-done.11 = bf16[1024,512]{1,0:T(8,128)(2,1)S(1)} collective-permute-done((bf16[1024,512]{1,0:T(8,128)(2,1)}, bf16[1024,512]{1,0:T(8,128)(2,1)S(1)}, u32[]{:S(2)}, u32[]{:S(2)}) %collective-permute-start.11) | collective-permute-done | bytes 1048608 | tf_op jit(solution)/shard_map/ppermute | solution.py:20
  450.4 10.1 convolution_convert_fusion.1
  460.6 9.4 convolution_convert_fusion
  491.7 38.4 %reduce-scatter.21.cloned.1.call-done = bf16[64,512]{1,0:T(8,128)(2,1)} async-done(((bf16[1024,512]{1,0:T(8,128)(2,1)}), bf16[64,512]{1,0:T(8,128)(2,1)}) %reduce-scatter.21.cloned.1.call-update) | async-done | bytes 65552 | tf_op jit(solution)/shard_map/reduce_scatter | solution.py:46
  531.6 74.9 %reduce-scatter.23.cloned.1.call-done = bf16[64,512]{1,0:T(8,128)(2,1)} async-done(((bf16[1024,512]{1,0:T(8,128)(2,1)}), bf16[64,512]{1,0:T(8,128)(2,1)}) %reduce-scatter.23.cloned.1.call-update) | async-done | bytes 65552 | tf_op jit(solution)/shard_map/reduce_scatter | solution.py:46
  619.7 63.1 %reduce-scatter.11.cloned.1.call-done = bf16[64,512]{1,0:T(8,128)(2,1)} async-done(((bf16[1024,512]{1,0:T(8,128)(2,1)}), bf16[64,512]{1,0:T(8,128)(2,1)}) %reduce-scatter.11.cloned.1.call-update) | async-done | bytes 65552 | tf_op jit(solution)/shard_map/reduce_scatter | solution.py:46
  684.4 75.1 %reduce-scatter.17.cloned.1.call-done = bf16[512,64]{0,1:T(8,128)(2,1)} async-done(((bf16[512,1024]{0,1:T(8,128)(2,1)}), bf16[512,64]{0,1:T(8,128)(2,1)}) %reduce-scatter.17.cloned.1.call-update) | async-done | bytes 65552 | tf_op jit(solution)/shard_map/reduce_scatter | solution.py:46
  779.1 56.7 %reduce-scatter.13.cloned.1.call-done = bf16[64,512]{1,0:T(8,128)(2,1)} async-done(((bf16[1024,512]{1,0:T(8,128)(2,1)}), bf16[64,512]{1,0:T(8,128)(2,1)}) %reduce-scatter.13.cloned.1.call-update) | async-done | bytes 65552 | tf_op jit(solution)/shard_map/reduce_scatter | solution.py:46
  837.4 75.4 %reduce-scatter.15.cloned.1.call-done = bf16[64,512]{1,0:T(8,128)(2,1)} async-done(((bf16[1024,512]{1,0:T(8,128)(2,1)}), bf16[64,512]{1,0:T(8,128)(2,1)}) %reduce-scatter.15.cloned.1.call-update) | async-done | bytes 65552 | tf_op jit(solution)/shard_map/reduce_scatter | solution.py:46
  916.1 90.6 %reduce-scatter.27.cloned.1.call-done = bf16[64,2048]{1,0:T(8,128)(2,1)} async-done(((bf16[1024,2048]{1,0:T(8,128)(2,1)}), bf16[64,2048]{1,0:T(8,128)(2,1)}) %reduce-scatter.27.cloned.1.call-update) | async-done | bytes 262160 | tf_op jit(solution)/shard_map/reduce_scatter | solution.py:46
  1008.5 95.1 %reduce-scatter.29.cloned.1.call-done = bf16[2048,64]{0,1:T(8,128)(2,1)} async-done(((bf16[2048,1024]{0,1:T(8,128)(2,1)}), bf16[2048,64]{0,1:T(8,128)(2,1)}) %reduce-scatter.29.cloned.1.call-update) | async-done | bytes 262160 | tf_op jit(solution)/shard_map/reduce_scatter | solution.py:46
  (302 shorter events, 240.5 us)
Async XLA Ops:
  7.2 481.4 %reduce-scatter.25.cloned.1.call-start = ((), (), s32[]{:S(2)}) async-start(), calls=%async_computation.17 | async-start | bytes 1114112 | tf_op jit(solution)/shard_map/reduce_scatter | solution.py:46
  14.5 52.1 %collective-permute-start.1 = (bf16[1024,512]{1,0:T(8,128)(2,1)}, bf16[1024,512]{1,0:T(8,128)(2,1)}, u32[]{:S(2)}, u32[]{:S(2)}) collective-permute-start(bf16[1024,512]{1,0:T(8,128)(2,1)} %convolution_convert_fusion.15.k_ref), channel_id=1, source_target_pairs={{0,2},{2,4},{4,6},{6,8},{8,10},{10,12},{12,14},{14,16},{16,18},{18... | collective-permute-start | bytes 3145736 | tf_op jit(solution)/shard_map/ppermute | solution.py:20
  22.8 43.8 %collective-permute-start.2 = (bf16[1024,512]{1,0:T(8,128)(2,1)}, bf16[1024,512]{1,0:T(8,128)(2,1)}, u32[]{:S(2)}, u32[]{:S(2)}) collective-permute-start(bf16[1024,512]{1,0:T(8,128)(2,1)} %add_convert_fusion.9.v_ref), channel_id=1, source_target_pairs={{0,2},{2,4},{4,6},{6,8},{8,10},{10,12},{12,14},{14,16},{16,18},{18... | collective-permute-start | bytes 3145736 | tf_op jit(solution)/shard_map/ppermute | solution.py:20
  27.5 37.2 %collective-permute-start = (s32[128]{0:T(128)S(1)}, s32[128]{0:T(128)S(1)}, u32[]{:S(2)}, u32[]{:S(2)}) collective-permute-start(s32[128]{0:T(128)S(1)} %broadcast_in_dim.2), channel_id=1, source_target_pairs={{0,2},{2,4},{4,6},{6,8},{8,10},{10,12},{12,14},{14,16},{16,18},{18... | collective-permute-start | bytes 1544 | tf_op jit(solution)/shard_map/ppermute | solution.py:20
  83.1 43.7 %collective-permute-start.3 = (bf16[1024,1024]{0,1:T(8,128)(2,1)}, bf16[1024,1024]{0,1:T(8,128)(2,1)}, u32[]{:S(2)}, u32[]{:S(2)}) collective-permute-start(bf16[1024,1024]{0,1:T(8,128)(2,1)} %convolution_convert_fusion.6), channel_id=1, source_target_pairs={{0,1},{1,0},{2,3},{3,2},{4,5},{5,4},{6,7},{7,6},{8,9},{9,8},{10,11... | collective-permute-start | bytes 6291464 | tf_op jit(solution)/shard_map/ppermute | solution.py:25
  90.5 22.3 %collective-permute-start.4 = (bf16[592,512]{1,0:T(8,128)(2,1)S(1)}, bf16[592,512]{1,0:T(8,128)(2,1)S(1)}, u32[]{:S(2)}, u32[]{:S(2)}) collective-permute-start(bf16[592,512]{1,0:T(8,128)(2,1)S(1)} %constant_dynamic-slice_fusion.1), channel_id=1, source_target_pairs={{0,2},{2,4},{4,6},{6,8},{8,10},{10,12},{12,14},{14,16},{16,18},{18... | collective-permute-start | bytes 1818632 | tf_op jit(solution)/shard_map/ppermute | solution.py:20
  100.6 24.8 %collective-permute-start.5 = (bf16[592,512]{1,0:T(8,128)(2,1)S(1)}, bf16[592,512]{1,0:T(8,128)(2,1)S(1)}, u32[]{:S(2)}, u32[]{:S(2)}) collective-permute-start(bf16[592,512]{1,0:T(8,128)(2,1)S(1)} %constant_dynamic-slice_fusion), channel_id=1, source_target_pairs={{0,2},{2,4},{4,6},{6,8},{8,10},{10,12},{12,14},{14,16},{16,18},{18... | collective-permute-start | bytes 1818632 | tf_op jit(solution)/shard_map/ppermute | solution.py:20
  234.9 255.3 %reduce-scatter.19.cloned.1.call-start = ((), (), s32[]{:S(2)}) async-start(), calls=%async_computation.14 | async-start | bytes 1114112 | tf_op jit(solution)/shard_map/reduce_scatter | solution.py:46
  268.3 261.8 %reduce-scatter.21.cloned.1.call-start = ((), (), s32[]{:S(2)}) async-start(), calls=%async_computation.15 | async-start | bytes 1114112 | tf_op jit(solution)/shard_map/reduce_scatter | solution.py:46
  269.6 26.5 %collective-permute-start.13 = (bf16[592,512]{1,0:T(8,128)(2,1)S(1)}, bf16[592,512]{1,0:T(8,128)(2,1)S(1)}, u32[]{:S(2)}, u32[]{:S(2)}) collective-permute-start(bf16[592,512]{1,0:T(8,128)(2,1)S(1)} %slice.114), channel_id=1, source_target_pairs={{2,0},{4,2},{6,4},{8,6},{10,8},{12,10},{14,12},{16,14},{18,16},{20... | collective-permute-start | bytes 1818632 | tf_op jit(solution)/shard_map/ppermute | solution.py:20
  300.4 306.1 %reduce-scatter.23.cloned.1.call-start = ((), (), s32[]{:S(2)}) async-start(), calls=%async_computation.16 | async-start | bytes 1114112 | tf_op jit(solution)/shard_map/reduce_scatter | solution.py:46
  300.5 25.8 %collective-permute-start.9 = (bf16[1024,1024]{0,1:T(8,128)(2,1)}, bf16[1024,1024]{0,1:T(8,128)(2,1)}, u32[]{:S(2)}, u32[]{:S(2)}) collective-permute-start(bf16[1024,1024]{0,1:T(8,128)(2,1)} %multiply_convert_fusion.1), channel_id=1, source_target_pairs={{0,1},{1,0},{2,3},{3,2},{4,5},{5,4},{6,7},{7,6},{8,9},{9,8},{10,11... | collective-permute-start | bytes 6291464 | tf_op jit(solution)/shard_map/ppermute | solution.py:25
  326.1 356.8 %reduce-scatter.11.cloned.1.call-start = ((), (), s32[]{:S(2)}) async-start(), calls=%async_computation.10 | async-start | bytes 1114112 | tf_op jit(solution)/shard_map/reduce_scatter | solution.py:46
  368.3 391.2 %reduce-scatter.17.cloned.1.call-start = ((), (), s32[]{:S(2)}) async-start(), calls=%async_computation.13 | async-start | bytes 1114112 | tf_op jit(solution)/shard_map/reduce_scatter | solution.py:46
  373.1 462.8 %reduce-scatter.13.cloned.1.call-start = ((), (), s32[]{:S(2)}) async-start(), calls=%async_computation.11 | async-start | bytes 1114112 | tf_op jit(solution)/shard_map/reduce_scatter | solution.py:46
  373.1 37.0 %collective-permute-start.10 = (bf16[1024,512]{1,0:T(8,128)(2,1)}, bf16[1024,512]{1,0:T(8,128)(2,1)S(1)}, u32[]{:S(2)}, u32[]{:S(2)}) collective-permute-start(bf16[1024,512]{1,0:T(8,128)(2,1)} %get-tuple-element.48), channel_id=1, source_target_pairs={{2,0},{4,2},{6,4},{8,6},{10,8},{12,10},{14,12},{16,14},{18,16},{20... | collective-permute-start | bytes 3145736 | tf_op jit(solution)/shard_map/ppermute | solution.py:20
  415.6 497.1 %reduce-scatter.15.cloned.1.call-start = ((), (), s32[]{:S(2)}) async-start(), calls=%async_computation.12 | async-start | bytes 1114112 | tf_op jit(solution)/shard_map/reduce_scatter | solution.py:46
  415.7 29.4 %collective-permute-start.11 = (bf16[1024,512]{1,0:T(8,128)(2,1)}, bf16[1024,512]{1,0:T(8,128)(2,1)S(1)}, u32[]{:S(2)}, u32[]{:S(2)}) collective-permute-start(bf16[1024,512]{1,0:T(8,128)(2,1)} %get-tuple-element.50), channel_id=1, source_target_pairs={{2,0},{4,2},{6,4},{8,6},{10,8},{12,10},{14,12},{16,14},{18,16},{20... | collective-permute-start | bytes 3145736 | tf_op jit(solution)/shard_map/ppermute | solution.py:20
  450.3 556.3 %reduce-scatter.27.cloned.1.call-start = ((), (), s32[]{:S(2)}) async-start(), calls=%async_computation.18 | async-start | bytes 4456448 | tf_op jit(solution)/shard_map/reduce_scatter | solution.py:46
  460.5 643.0 %reduce-scatter.29.cloned.1.call-start = ((), (), s32[]{:S(2)}) async-start(), calls=%async_computation.19 | async-start | bytes 4456448 | tf_op jit(solution)/shard_map/reduce_scatter | solution.py:46
  477.2 130.8 %collective-permute-start.12 = (bf16[1024,1024]{0,1:T(8,128)(2,1)}, bf16[1024,1024]{0,1:T(8,128)(2,1)}, u32[]{:S(2)}, u32[]{:S(2)}) collective-permute-start(bf16[1024,1024]{0,1:T(8,128)(2,1)} %add_convert_fusion.3), channel_id=1, source_target_pairs={{0,1},{1,0},{2,3},{3,2},{4,5},{5,4},{6,7},{7,6},{8,9},{9,8},{10,11... | collective-permute-start | bytes 6291464 | tf_op jit(solution)/shard_map/ppermute | solution.py:25
  487.7 124.6 %collective-permute-start.15 = (bf16[1184,1024]{1,0:T(8,128)(2,1)}, bf16[1184,1024]{1,0:T(8,128)(2,1)}, u32[]{:S(2)}, u32[]{:S(2)}) collective-permute-start(bf16[1184,1024]{1,0:T(8,128)(2,1)} %add_convert_fusion.2), channel_id=1, source_target_pairs={{0,1},{1,0},{2,3},{3,2},{4,5},{5,4},{6,7},{7,6},{8,9},{9,8},{10,11... | collective-permute-start | bytes 7274504 | tf_op jit(solution)/shard_map/ppermute | solution.py:25
  612.2 148.8 %collective-permute-start.16 = (f32[104,128]{1,0:T(8,128)S(1)}, f32[104,128]{1,0:T(8,128)S(1)}, u32[]{:S(2)}, u32[]{:S(2)}) collective-permute-start(f32[104,128]{1,0:T(8,128)S(1)} %bitcast.95), channel_id=1, source_target_pairs={{0,2},{2,0},{4,6},{6,4},{8,10},{10,8},{12,14},{14,12},{16,18},{18,... | collective-permute-start | bytes 159752 | tf_op jit(solution)/shard_map/ppermute | solution.py:35
  769.5 144.7 %collective-permute-start.19 = (f32[104,128]{1,0:T(8,128)S(1)}, f32[104,128]{1,0:T(8,128)S(1)}, u32[]{:S(2)}, u32[]{:S(2)}) collective-permute-start(f32[104,128]{1,0:T(8,128)S(1)} %add.262), channel_id=1, source_target_pairs={{0,16},{2,18},{4,20},{6,22},{8,24},{10,26},{12,28},{14,30},{16,0},... | collective-permute-start | bytes 159752 | tf_op jit(solution)/shard_map/ppermute | solution.py:35
  (75 other events, 1323.4 us)
Sparse Core Ops, SparseCore 0:
  235.0 104.8 reduce-scatter.24
  342.3 109.2 reduce-scatter.18
  453.8 76.2 reduce-scatter.20
  532.3 74.1 reduce-scatter.22
  608.6 74.2 reduce-scatter.10
  685.1 74.3 reduce-scatter.16
  761.8 74.0 reduce-scatter.12
  838.2 74.4 reduce-scatter.14
  915.1 91.5 reduce-scatter.26
  1008.8 94.6 reduce-scatter.28

commit v3 on v2

v3 whole, which is shorter than its diff:
```python
import functools
import math

import jax
import jax.numpy as jnp
from jax import lax
from jax.experimental import pallas as pl
from jax.experimental.pallas import tpu as pltpu
from jax.sharding import PartitionSpec as P

HEAD_WIDTH = 64


EPSILON = 1e-05


def shifted(value, axis, steps):
    count = lax.axis_size(axis)
    initial, last = (max(0, -steps), min(count, count - steps))
    return lax.ppermute(value, axis, [(source, source + steps) for source in range(initial, last)])


def butterfly_sum(vectors):
    sizes = [vector.shape[0] for vector in vectors]
    total = jnp.concatenate(vectors).reshape(-1, 128)
    count = lax.axis_size("dp")
    bit = 1
    while bit < count:
        total = total + lax.ppermute(total, "dp", [(i, i ^ bit) for i in range(count)])
        bit *= 2
    flat = total.reshape(-1)
    pieces, at = [], 0
    for size in sizes:
        pieces.append(flat[at : at + size])
        at += size
    return pieces


def layer_norm(values, gain, bias):
    mean = jnp.mean(values, axis=-1, keepdims=True)
    centered = values - mean
    inverse = lax.rsqrt(jnp.mean(centered * centered, axis=-1, keepdims=True) + EPSILON)
    normed = centered * inverse
    return (normed * gain + bias, normed, inverse)


def norm_back(grad, normed, inverse, gain):
    scaled = grad * gain
    inner = (
        scaled
        - jnp.mean(scaled, axis=-1, keepdims=True)
        - normed * jnp.mean(scaled * normed, axis=-1, keepdims=True)
    )
    return (inner * inverse, jnp.sum(grad * normed, axis=0), jnp.sum(grad, axis=0))


BF = jnp.bfloat16
F32 = jnp.float32
NEG = -1e30
TILE = 256
HEAD_WIDTH = 64
PAIR = 2 * HEAD_WIDTH
VMEM_LIMIT = 60 * 1024 * 1024


def nt(left, right):
    return lax.dot_general(left, right, (((1,), (1,)), ((), ())), preferred_element_type=F32)


def nn(left, right):
    return lax.dot_general(left, right, (((1,), (0,)), ((), ())), preferred_element_type=F32)


def head_half(pair, half):
    lane = lax.broadcasted_iota(jnp.int32, pair.shape, 1)
    keep = lane < HEAD_WIDTH if half == 0 else lane >= HEAD_WIDTH
    return jnp.where(keep, pair, jnp.zeros_like(pair))


def span(index, size=TILE):
    return pl.ds(pl.multiple_of(index * size, size), size)


HEAD_ROWS = 80


def column_max(values):
    rows = values.shape[0]
    groups = max(1, rows // 64)
    step = -(-(rows // groups) // 8) * 8
    parts = []
    at = 0
    while at < rows:
        end = min(rows, at + step)
        parts.append(jnp.max(values[at:end], axis=0, keepdims=True))
        at = end
    while len(parts) > 1:
        parts = [jnp.maximum(*parts[i : i + 2]) if i + 1 < len(parts) else parts[i] for i in range(0, len(parts), 2)]
    return parts[0]


def extended(values, target, columns):
    turned = values.T
    extra = jnp.where(lax.broadcasted_iota(jnp.int32, (HEAD_ROWS - HEAD_WIDTH, turned.shape[1]), 0) == 0, 1.0, 0.0).astype(BF)
    for h in range(turned.shape[0] // HEAD_WIDTH):
        base = h * HEAD_ROWS
        target[base : base + HEAD_WIDTH, columns] = turned[h * HEAD_WIDTH : (h + 1) * HEAD_WIDTH, :]
        target[base + HEAD_WIDTH : base + HEAD_ROWS, columns] = extra


def lane_rows(i):
    return i * TILE + lax.broadcasted_iota(jnp.int32, (1, TILE), 1)


def self_forward_body(meta, q_ref, kp_ref, k_ref, vp_ref, v_ref, o_ref, log_ref,
                      vpt, vt, qm, bias, m_s, acc, done, scores):
    rows = q_ref.shape[0]
    pairs = q_ref.shape[1] // PAIR
    b1, b2, p0 = meta[0], meta[1], meta[2]
    tiles = rows // TILE
    offset = rows - kp_ref.shape[0]
    prior_tiles = kp_ref.shape[0] // TILE
    first_prior = (p0 - offset) // TILE
    prior_rows = (b1 + TILE - 1) // TILE

    def turn_own(j, c):
        extended(v_ref[span(j), :], vt, span(j))
        return c

    lax.fori_loop(0, tiles, turn_own, 0)

    def turn_prior(j, c):
        extended(vp_ref[span(j), :], vpt, span(j))
        return c

    lax.fori_loop(jnp.where(b1 > 0, first_prior, prior_tiles), prior_tiles, turn_prior, 0)

    def key_step(keys, values_t, j):
        for pair in range(pairs):
            key_pair = keys[span(j), pair * PAIR : pair * PAIR + PAIR]
            for half in range(2):
                scores[2 * pair + half] = nt(key_pair, qm[2 * pair + half])
        for pair in range(pairs):
            for half in range(2):
                h = 2 * pair + half
                heads = slice(h * HEAD_ROWS, (h + 1) * HEAD_ROWS)
                s = scores[h] + bias[...]
                m_old = m_s[h : h + 1, :]
                m_new = jnp.maximum(m_old, column_max(s))
                alpha = jnp.exp(m_old - m_new)
                e = jnp.exp(s - m_new)
                m_s[h : h + 1, :] = m_new
                acc[heads, :] = acc[heads, :] * alpha + nn(values_t[heads, span(j)], e.astype(BF))

    def row_tile(i, c):
        t = lane_rows(i)
        start = jnp.where(t < b1, 0, jnp.where(t < b2, b1, b2))
        for pair in range(pairs):
            q_pair = q_ref[span(i), pair * PAIR : pair * PAIR + PAIR]
            for half in range(2):
                qm[2 * pair + half] = head_half(q_pair, half)
        m_s[...] = jnp.full_like(m_s, NEG)
        acc[...] = jnp.zeros_like(acc)

        def prior(j, c2):
            r = offset + j * TILE + lax.broadcasted_iota(jnp.int32, (TILE, TILE), 0)
            bias[...] = jnp.where((r >= p0) & (t < b1), 0.0, NEG)
            key_step(kp_ref, vpt, j)
            return c2

        lax.fori_loop(jnp.where(i < prior_rows, first_prior, prior_tiles), prior_tiles, prior, 0)
        t_first = i * TILE
        lowest = jnp.where(t_first < b1, 0, jnp.where(t_first < b2, b1, b2))

        def own(j, c2):
            r = j * TILE + lax.broadcasted_iota(jnp.int32, (TILE, TILE), 0)
            bias[...] = jnp.where((r <= t) & (r >= start), 0.0, NEG)
            key_step(k_ref, vt, j)
            return c2

        lax.fori_loop(lowest // TILE, i + 1, own, 0)
        for h in range(2 * pairs):
            base = h * HEAD_ROWS
            total = acc[base + HEAD_WIDTH : base + HEAD_WIDTH + 1, :]
            log_ref[h : h + 1, span(i)] = m_s[h : h + 1, :] + jnp.log(total)
            done[h * HEAD_WIDTH : (h + 1) * HEAD_WIDTH, :] = acc[base : base + HEAD_WIDTH, :] * (1.0 / total)
        o_ref[span(i), :] = done[...].T.astype(BF)
        return c

    lax.fori_loop(0, tiles, row_tile, 0)


SMEM_SPEC = pl.BlockSpec(memory_space=pltpu.SMEM)
VMEM_SPEC = pl.BlockSpec(memory_space=pltpu.VMEM)


def self_forward(meta, q, k_prior, k, v_prior, v):
    rows, width = q.shape
    heads = width // HEAD_WIDTH
    return pl.pallas_call(
        self_forward_body,
        out_shape=(jax.ShapeDtypeStruct((rows, width), BF), jax.ShapeDtypeStruct((heads, rows), F32)),
        in_specs=[SMEM_SPEC] + [VMEM_SPEC] * 5,
        out_specs=(VMEM_SPEC, VMEM_SPEC),
        scratch_shapes=[
            pltpu.VMEM((heads * HEAD_ROWS, k_prior.shape[0]), BF),
            pltpu.VMEM((heads * HEAD_ROWS, rows), BF),
            pltpu.VMEM((heads, TILE, PAIR), BF),
            pltpu.VMEM((TILE, TILE), F32),
            pltpu.VMEM((heads, TILE), F32),
            pltpu.VMEM((heads * HEAD_ROWS, TILE), F32),
            pltpu.VMEM((width, TILE), F32),
            pltpu.VMEM((heads, TILE, TILE), F32),
        ],
        compiler_params=pltpu.CompilerParams(vmem_limit_bytes=VMEM_LIMIT),
        cost_estimate=pl.CostEstimate(flops=2 * 2 * rows * rows * width, bytes_accessed=8 * rows * width * 2, transcendentals=rows * rows * heads),
        name="self_forward",
    )(meta, q, k_prior, k, v_prior, v)


def grad_rows(do_ref, o_ref, i, width):
    heads = width // HEAD_WIDTH
    product = do_ref[span(i), :].astype(F32) * o_ref[span(i), :].astype(F32)
    high = product.astype(BF)
    low = (product - high.astype(F32)).astype(BF)
    head = lax.broadcasted_iota(jnp.int32, (heads, width), 0)
    column = lax.broadcasted_iota(jnp.int32, (heads, width), 1) // HEAD_WIDTH
    pick = jnp.where(head == column, 1.0, 0.0).astype(BF)
    return nt(pick, high) + nt(pick, low)


def halves(source, i, target, pairs):
    for pair in range(pairs):
        value = source[span(i), pair * PAIR : pair * PAIR + PAIR]
        for half in range(2):
            target[2 * pair + half] = head_half(value, half)


def grad_step(pairs, keys, values, keys_t, key_slice, key_lanes, qm, dom, shift, delta, bias, dk, dv, dqt, scores, grads):
    for pair in range(pairs):
        cols = slice(pair * PAIR, pair * PAIR + PAIR)
        key_pair = keys[key_slice, cols]
        value_pair = values[key_slice, cols]
        for half in range(2):
            h = 2 * pair + half
            scores[h] = nt(key_pair, qm[h])
            grads[h] = nt(value_pair, dom[h])
    for pair in range(pairs):
        cols = slice(pair * PAIR, pair * PAIR + PAIR)
        dv_pair = dv[key_slice, cols]
        dk_pair = dk[key_slice, cols]
        for half in range(2):
            h = 2 * pair + half
            heads = slice(h * HEAD_WIDTH, (h + 1) * HEAD_WIDTH)
            s = scores[h]
            if bias is not None:
                s = s + bias[...]
            p = jnp.exp(s - shift[h : h + 1, :])
            dp = grads[h]
            ds = (p * (dp - delta[h : h + 1, :])).astype(BF)
            dv_pair = dv_pair + nn(p.astype(BF), dom[h])
            dk_pair = dk_pair + nn(ds, qm[h])
            dqt[heads, :] = dqt[heads, :] + nn(keys_t[heads, key_lanes], ds)
        dv[key_slice, cols] = dv_pair
        dk[key_slice, cols] = dk_pair


def self_prior_back_body(meta, q_ref, do_ref, o_ref, log_ref, k_ref, v_ref, dk_ref, dv_ref, dq_ref,
                         kt, qm, dom, bias, delta, shift, dqt, dk, dv, scores, grads):
    rows, width = q_ref.shape
    pairs = width // PAIR
    b1, p0 = meta[0], meta[2]
    tiles = rows // TILE
    offset = rows - k_ref.shape[0]
    prior_tiles = k_ref.shape[0] // TILE
    first_prior = (p0 - offset) // TILE
    prior_rows = (b1 + TILE - 1) // TILE
    dk[...] = jnp.zeros_like(dk)
    dv[...] = jnp.zeros_like(dv)

    def turn(j, c):
        kt[:, span(j)] = k_ref[span(j), :].T
        return c

    lax.fori_loop(jnp.where(b1 > 0, first_prior, prior_tiles), prior_tiles, turn, 0)

    def row_tile(i, c):
        dqt[...] = jnp.zeros_like(dqt)
        t = lane_rows(i)

        @pl.when(i < prior_rows)
        def _():
            halves(q_ref, i, qm, pairs)
            halves(do_ref, i, dom, pairs)
            delta[...] = grad_rows(do_ref, o_ref, i, width)
            shift[...] = log_ref[:, span(i)]

        def prior(j, c2):
            r = offset + j * TILE + lax.broadcasted_iota(jnp.int32, (TILE, TILE), 0)
            bias[...] = jnp.where((r >= p0) & (t < b1), 0.0, NEG)
            grad_step(pairs, k_ref, v_ref, kt, span(j), span(j), qm, dom, shift, delta, bias, dk, dv, dqt, scores, grads)
            return c2

        lax.fori_loop(jnp.where(i < prior_rows, first_prior, prior_tiles), prior_tiles, prior, 0)
        dq_ref[span(i), :] = dqt[...].T
        return c

    lax.fori_loop(0, tiles, row_tile, 0)
    dk_ref[...] = dk[...].astype(BF)
    dv_ref[...] = dv[...].astype(BF)


def self_own_back_body(meta, q_ref, do_ref, o_ref, log_ref, k_ref, v_ref, dqp_ref, dk_ref, dv_ref, dq_ref,
                       kt, qm, dom, bias, delta, shift, dqt, dk, dv, scores, grads):
    rows, width = q_ref.shape
    pairs = width // PAIR
    b1, b2 = meta[0], meta[1]
    tiles = rows // TILE
    dk[...] = jnp.zeros_like(dk)
    dv[...] = jnp.zeros_like(dv)

    def turn(j, c):
        kt[:, span(j)] = k_ref[span(j), :].T
        return c

    lax.fori_loop(0, tiles, turn, 0)

    def row_tile(i, c):
        dqt[...] = jnp.zeros_like(dqt)
        t = lane_rows(i)
        start = jnp.where(t < b1, 0, jnp.where(t < b2, b1, b2))
        halves(q_ref, i, qm, pairs)
        halves(do_ref, i, dom, pairs)
        delta[...] = grad_rows(do_ref, o_ref, i, width)
        shift[...] = log_ref[:, span(i)]
        t_first = i * TILE
        lowest = jnp.where(t_first < b1, 0, jnp.where(t_first < b2, b1, b2))

        def own(j, c2):
            r = j * TILE + lax.broadcasted_iota(jnp.int32, (TILE, TILE), 0)
            bias[...] = jnp.where((r <= t) & (r >= start), 0.0, NEG)
            grad_step(pairs, k_ref, v_ref, kt, span(j), span(j), qm, dom, shift, delta, bias, dk, dv, dqt, scores, grads)
            return c2

        lax.fori_loop(lowest // TILE, i + 1, own, 0)
        dq_ref[span(i), :] = (dqp_ref[span(i), :] + dqt[...].T).astype(BF)
        return c

    lax.fori_loop(0, tiles, row_tile, 0)
    dk_ref[...] = dk[...].astype(BF)
    dv_ref[...] = dv[...].astype(BF)


def self_back_scratch(keys, width):
    heads = width // HEAD_WIDTH
    return [
        pltpu.VMEM((width, keys), BF),
        pltpu.VMEM((heads, TILE, PAIR), BF),
        pltpu.VMEM((heads, TILE, PAIR), BF),
        pltpu.VMEM((TILE, TILE), F32),
        pltpu.VMEM((heads, TILE), F32),
        pltpu.VMEM((heads, TILE), F32),
        pltpu.VMEM((width, TILE), F32),
        pltpu.VMEM((keys, width), F32),
        pltpu.VMEM((keys, width), F32),
        pltpu.VMEM((heads, TILE, TILE), F32),
        pltpu.VMEM((heads, TILE, TILE), F32),
    ]


def self_prior_back(meta, q, do, o, logs, k_prior, v_prior):
    rows, width = q.shape
    return pl.pallas_call(
        self_prior_back_body,
        out_shape=(jax.ShapeDtypeStruct(k_prior.shape, BF), jax.ShapeDtypeStruct(k_prior.shape, BF),
                   jax.ShapeDtypeStruct((rows, width), F32)),
        in_specs=[SMEM_SPEC] + [VMEM_SPEC] * 6,
        out_specs=(VMEM_SPEC,) * 3,
        scratch_shapes=self_back_scratch(k_prior.shape[0], width),
        compiler_params=pltpu.CompilerParams(vmem_limit_bytes=VMEM_LIMIT),
        cost_estimate=pl.CostEstimate(flops=3 * rows * rows * width, bytes_accessed=8 * rows * width * 2, transcendentals=rows * rows * 4),
        name="self_prior_back",
    )(meta, q, do, o, logs, k_prior, v_prior)


def self_own_back(meta, q, do, o, logs, k, v, dq_prior):
    rows, width = q.shape
    return pl.pallas_call(
        self_own_back_body,
        out_shape=(jax.ShapeDtypeStruct((rows, width), BF),) * 3,
        in_specs=[SMEM_SPEC] + [VMEM_SPEC] * 7,
        out_specs=(VMEM_SPEC,) * 3,
        scratch_shapes=self_back_scratch(rows, width),
        compiler_params=pltpu.CompilerParams(vmem_limit_bytes=VMEM_LIMIT),
        cost_estimate=pl.CostEstimate(flops=5 * rows * rows * width, bytes_accessed=8 * rows * width * 2, transcendentals=rows * rows * 4),
        name="self_own_back",
    )(meta, q, do, o, logs, k, v, dq_prior)


def segments(meta, rows):
    return ((0, meta[0], None), (meta[0], meta[1], meta[4]), (meta[1], rows, meta[5]))


def cross_forward_body(used, meta, q_ref, kp_ref, k_ref, vp_ref, v_ref, o_ref, log_ref, vpt, vt, qm, acc, scores):
    rows, width = q_ref.shape
    pairs = width // PAIR
    padded = kp_ref.shape[0]
    images = k_ref.shape[0] // padded
    for slot in range(images):
        extended(v_ref[slot * padded : (slot + 1) * padded, :], vt.at[slot], slice(None))
    extended(vp_ref[...], vpt, slice(None))
    for first, last, slot in segments(meta, rows):
        own = slot is not None
        keys = pl.ds(pl.multiple_of(slot * padded, 16), padded) if own else slice(None)
        key_table = k_ref if own else kp_ref
        value_table = vt.at[slot] if own else vpt

        def tile(i, c):
            halves(q_ref, i, qm, pairs)
            t = lane_rows(i)
            inside = (t >= first) & (t < last)
            for pair in range(pairs):
                key_pair = key_table[keys, pair * PAIR : pair * PAIR + PAIR]
                for half in range(2):
                    scores[2 * pair + half] = nt(key_pair, qm[2 * pair + half])
            for h in range(2 * pairs):
                heads = slice(h * HEAD_WIDTH, (h + 1) * HEAD_WIDTH)
                s = scores[h]
                if used < padded:
                    row = lax.broadcasted_iota(jnp.int32, s.shape, 0)
                    s = jnp.where(row < used, s, NEG)
                m = column_max(s)
                e = jnp.exp(s - m)
                mixed = nn(value_table[h * HEAD_ROWS : (h + 1) * HEAD_ROWS, :], e.astype(BF))
                total = mixed[HEAD_WIDTH : HEAD_WIDTH + 1, :]
                acc[heads, :] = mixed[:HEAD_WIDTH, :] * (1.0 / total)
                log_ref[h : h + 1, span(i)] = jnp.where(
                    inside, m + jnp.log(total), log_ref[h : h + 1, span(i)]
                )
            column = i * TILE + lax.broadcasted_iota(jnp.int32, (TILE, width), 0)
            keep = (column >= first) & (column < last)
            o_ref[span(i), :] = jnp.where(keep, acc[...].T, o_ref[span(i), :].astype(F32)).astype(BF)
            return c

        lax.fori_loop(first // TILE, jnp.where(last > first, (last + TILE - 1) // TILE, 0), tile, 0)


def cross_forward(used, meta, q, k_prior, k, v_prior, v):
    rows, width = q.shape
    heads = width // HEAD_WIDTH
    padded = k_prior.shape[0]
    return pl.pallas_call(
        functools.partial(cross_forward_body, used),
        out_shape=(jax.ShapeDtypeStruct((rows, width), BF), jax.ShapeDtypeStruct((heads, rows), F32)),
        in_specs=[SMEM_SPEC] + [VMEM_SPEC] * 5,
        out_specs=(VMEM_SPEC, VMEM_SPEC),
        scratch_shapes=[
            pltpu.VMEM((heads * HEAD_ROWS, padded), BF),
            pltpu.VMEM((k.shape[0] // padded, heads * HEAD_ROWS, padded), BF),
            pltpu.VMEM((heads, TILE, PAIR), BF),
            pltpu.VMEM((width, TILE), F32),
            pltpu.VMEM((heads, padded, TILE), F32),
        ],
        compiler_params=pltpu.CompilerParams(vmem_limit_bytes=VMEM_LIMIT),
        cost_estimate=pl.CostEstimate(flops=16 * rows * padded * width, bytes_accessed=8 * rows * width * 2, transcendentals=rows * padded * heads),
        name="cross_forward",
    )(meta, q, k_prior, k, v_prior, v)


def cross_back_body(used, meta, q_ref, do_ref, o_ref, log_ref, kp_ref, k_ref, vp_ref, v_ref, dkp_ref, dk_ref, dvp_ref, dv_ref,
                    dq_ref, kpt, kt, qm, dom, delta, shift, dqt, dkp, dk, dvp, dv, scores, grads):
    rows, width = q_ref.shape
    pairs = width // PAIR
    padded = kp_ref.shape[0]
    images = k_ref.shape[0] // padded
    for item in (dkp, dk, dvp, dv):
        item[...] = jnp.zeros_like(item)
    for slot in range(images):
        kt[slot] = k_ref[slot * padded : (slot + 1) * padded, :].T
    kpt[...] = kp_ref[...].T
    for first, last, slot in segments(meta, rows):
        own = slot is not None
        keys = pl.ds(pl.multiple_of(slot * padded, 16), padded) if own else slice(None)
        tables = (k_ref, v_ref, kt.at[slot]) if own else (kp_ref, vp_ref, kpt)
        sums = (dk, dv) if own else (dkp, dvp)

        def tile(i, c):
            halves(q_ref, i, qm, pairs)
            halves(do_ref, i, dom, pairs)
            t = lane_rows(i)
            inside = (t >= first) & (t < last)
            delta[...] = grad_rows(do_ref, o_ref, i, width)
            shift[...] = jnp.where(inside, log_ref[:, span(i)], -NEG)
            dqt[...] = jnp.zeros_like(dqt)
            grad_step(pairs, *tables, keys, slice(None), qm, dom, shift, delta, None, *sums, dqt, scores, grads)
            column = i * TILE + lax.broadcasted_iota(jnp.int32, (TILE, width), 0)
            keep = (column >= first) & (column < last)
            dq_ref[span(i), :] = jnp.where(keep, dqt[...].T, dq_ref[span(i), :].astype(F32)).astype(BF)
            return c

        lax.fori_loop(first // TILE, jnp.where(last > first, (last + TILE - 1) // TILE, 0), tile, 0)
    inner = lax.broadcasted_iota(jnp.int32, (padded, width), 0) < used
    for source, target in ((dkp, dkp_ref), (dk, dk_ref), (dvp, dvp_ref), (dv, dv_ref)):
        for slot in range(source.shape[0] // padded):
            part = slice(slot * padded, (slot + 1) * padded)
            target[part, :] = jnp.where(inner, source[part, :], 0.0).astype(BF)


def cross_back(used, meta, q, do, o, logs, k_prior, k, v_prior, v):
    rows, width = q.shape
    heads = width // HEAD_WIDTH
    padded = k_prior.shape[0]
    tables = (k_prior, k, v_prior, v)
    return pl.pallas_call(
        functools.partial(cross_back_body, used),
        out_shape=tuple(jax.ShapeDtypeStruct(table.shape, BF) for table in tables) + (jax.ShapeDtypeStruct((rows, width), BF),),
        in_specs=[SMEM_SPEC] + [VMEM_SPEC] * 8,
        out_specs=(VMEM_SPEC,) * 5,
        scratch_shapes=[
            pltpu.VMEM((width, padded), BF),
            pltpu.VMEM((k.shape[0] // padded, width, padded), BF),
            pltpu.VMEM((heads, TILE, PAIR), BF),
            pltpu.VMEM((heads, TILE, PAIR), BF),
            pltpu.VMEM((heads, TILE), F32),
            pltpu.VMEM((heads, TILE), F32),
            pltpu.VMEM((width, TILE), F32),
        ]
        + [pltpu.VMEM(table.shape, F32) for table in tables]
        + [pltpu.VMEM((heads, padded, TILE), F32)] * 2,
        compiler_params=pltpu.CompilerParams(vmem_limit_bytes=VMEM_LIMIT),
        cost_estimate=pl.CostEstimate(flops=40 * rows * padded * width, bytes_accessed=12 * rows * width * 2, transcendentals=rows * padded * heads),
        name="cross_back",
    )(meta, q, do, o, logs, *tables)


SQRT_HALF = 0.7071067811865476
GAUSS = 0.3989422804014327
ROW_CHUNK = 256


def error_function(x):
    x = jnp.clip(x, -4.0, 4.0)
    z = x * x
    top = -2.72614225801306e-10
    for term in (2.77068142495902e-08, -2.10102402082508e-06, -5.69250639462346e-05,
                 -7.34990630326855e-04, -2.95459980854025e-03, -1.60960333262415e-02):
        top = top * z + term
    low = -1.45660718464996e-05
    for term in (-2.13374055278905e-04, -1.68282697438203e-03, -7.37332916720468e-03, -1.42647390514189e-02):
        low = low * z + term
    return x * top / low


def row_norm(values):
    mean = jnp.mean(values, axis=-1, keepdims=True)
    centered = values - mean
    inverse = lax.rsqrt(jnp.mean(centered * centered, axis=-1, keepdims=True) + EPSILON)
    return centered * inverse, inverse


def chunk_place(index, inner, outer):
    return (index % inner) * outer + index // inner


def feed_forward_body(inner, outer, start_ref, own_ref, other_ref, b_out, gain, shift_in, dy_ref, w_up, b_up, w_down,
                      y1_ref, down_ref, dh_ref, grads_ref, db_ref,
                      h2, h2t, dyt, acc_down, acc_dh, u_s, da_s, g_s, du_s):
    step = pl.program_id(0)
    rows, width = dy_ref.shape
    tile = w_up.shape[1]
    chunks = rows // ROW_CHUNK

    @pl.when(step == 0)
    def _():
        for r in range(chunks):
            part = slice(r * ROW_CHUNK, (r + 1) * ROW_CHUNK)
            y1 = start_ref[part, :] + (own_ref[part, :].astype(F32) + other_ref[part, :].astype(F32)) + b_out[...]
            y1_ref[part, :] = y1
            normed, _ = row_norm(y1)
            low = (normed * gain[...] + shift_in[...]).astype(BF)
            h2[part, :] = low
            h2t[:, part] = low.T
            dyt[:, part] = dy_ref[part, :].T
        acc_down[...] = jnp.zeros_like(acc_down)
        acc_dh[...] = jnp.zeros_like(acc_dh)

    for r in range(chunks):
        part = slice(r * ROW_CHUNK, (r + 1) * ROW_CHUNK)
        u_s[part, :] = nn(h2[part, :], w_up[...]) + b_up[...]
        da_s[part, :] = nt(dy_ref[part, :], w_down[...])
    total = jnp.zeros((1, tile), F32)
    for r in range(chunks):
        part = slice(r * ROW_CHUNK, (r + 1) * ROW_CHUNK)
        u = u_s[part, :]
        half = 0.5 + 0.5 * error_function(u * SQRT_HALF)
        g = (u * half).astype(BF)
        slope = half + u * (GAUSS * jnp.exp(-0.5 * u * u))
        du = (da_s[part, :] * slope).astype(BF)
        g_s[part, :] = g
        du_s[part, :] = du
        total = total + jnp.sum(du.astype(F32), axis=0, keepdims=True)
        down = nn(g, w_down[...])
        dh = nt(du, w_up[...])
        acc_down[part, :] += down
        acc_dh[part, :] += dh

    db_ref[...] = total
    piece = width // (inner * outer)
    for source, turned, at in ((du_s, h2t, 0), (g_s, dyt, tile)):
        for r in range(width // ROW_CHUNK):
            part = slice(r * ROW_CHUNK, (r + 1) * ROW_CHUNK)
            product = nn(turned[part, :], source[...]).astype(BF)
            for c in range(ROW_CHUNK // piece):
                place = chunk_place(r * (ROW_CHUNK // piece) + c, inner, outer) * piece
                grads_ref[place : place + piece, at : at + tile] = product[c * piece : (c + 1) * piece, :]

    @pl.when(step == pl.num_programs(0) - 1)
    def _():
        down_ref[...] = acc_down[...].astype(BF)
        dh_ref[...] = acc_dh[...].astype(BF)


def feed_forward(inner, outer, tile, start, own, other, b_out, gain, shift_in, dy, w_up, b_up, w_down):
    rows, width = dy.shape
    hidden = w_up.shape[1]
    whole = lambda shape: pl.BlockSpec(shape, lambda k: (0, 0), pipeline_mode=pl.Buffered(1))
    row = whole((1, width))
    full = whole((rows, width))
    return pl.pallas_call(
        functools.partial(feed_forward_body, inner, outer),
        grid=(hidden // tile,),
        out_shape=(
            jax.ShapeDtypeStruct((rows, width), F32),
            jax.ShapeDtypeStruct((rows, width), BF),
            jax.ShapeDtypeStruct((rows, width), BF),
            jax.ShapeDtypeStruct((width, 2 * hidden), BF),
            jax.ShapeDtypeStruct((1, hidden), F32),
        ),
        in_specs=[full, full, full, row, row, row, full,
                  pl.BlockSpec((width, tile), lambda k: (0, k)),
                  pl.BlockSpec((1, tile), lambda k: (0, k)),
                  pl.BlockSpec((tile, width), lambda k: (k, 0))],
        out_specs=(full, full, full, pl.BlockSpec((width, 2 * tile), lambda k: (0, k)), pl.BlockSpec((1, tile), lambda k: (0, k))),
        scratch_shapes=[
            pltpu.VMEM((rows, width), BF),
            pltpu.VMEM((width, rows), BF),
            pltpu.VMEM((width, rows), BF),
            pltpu.VMEM((rows, width), F32),
            pltpu.VMEM((rows, width), F32),
            pltpu.VMEM((rows, tile), F32),
            pltpu.VMEM((rows, tile), F32),
            pltpu.VMEM((rows, tile), BF),
            pltpu.VMEM((rows, tile), BF),
        ],
        compiler_params=pltpu.CompilerParams(vmem_limit_bytes=VMEM_LIMIT),
        cost_estimate=pl.CostEstimate(flops=12 * rows * width * hidden, bytes_accessed=30 * rows * width, transcendentals=rows * hidden * 2),
        name="feed_forward",
    )(start, own, other, b_out.reshape(1, -1), gain.reshape(1, -1), shift_in.reshape(1, -1), dy, w_up, b_up.reshape(1, -1), w_down)


def bit_orders(count):
    bits = list(range(count.bit_length() - 1))
    return bits, [bits[1], bits[0]] + bits[2:]


def place_code(position, order):
    code = 0
    for rank, bit in enumerate(order):
        if position >> (len(order) - 1 - rank) & 1:
            code |= 1 << bit
    return code


def weight_grads_body(count, products, left_count, right_count, me, *refs):
    lefts, rights = refs[:left_count], refs[left_count : left_count + right_count]
    outs = refs[left_count + right_count : left_count + right_count + 4]
    turned = refs[left_count + right_count + 4 : -1]
    natural = refs[-1]
    width = lefts[0].shape[1]
    columns = rights[0].shape[1]
    piece = width // count
    orders = bit_orders(count)
    for left, target in zip(lefts, turned):
        for r in range(width // ROW_CHUNK):
            part = slice(r * ROW_CHUNK, (r + 1) * ROW_CHUNK)
            target[part, :] = left[:, part].T
    for number, (terms, factor) in enumerate(products):
        store = natural.at[number % 2]
        for r in range(width // ROW_CHUNK):
            part = slice(r * ROW_CHUNK, (r + 1) * ROW_CHUNK)
            total = None
            for left, right in terms:
                product = nn(turned[left][part, :], rights[right][...])
                total = product if total is None else total + product
            store[part, :] = (total * factor if factor != 1.0 else total).astype(BF)
        side = number // (len(products) // 2)
        at = number % (len(products) // 2) * columns
        keep, send = outs[2 * side], outs[2 * side + 1]
        for position in range(count):
            source = pl.multiple_of((me[0] ^ place_code(position, orders[side])) * piece, piece)
            target = keep if position < count // 2 else send
            row = position % (count // 2) * piece
            target[row : row + piece, at : at + columns] = store[pl.ds(source, piece), :]


def weight_grads(count, me, lefts, rights, products):
    width = lefts[0].shape[1]
    columns = rights[0].shape[1]
    half = jax.ShapeDtypeStruct((width // 2, columns * len(products) // 2), BF)
    flops = sum(2 * width * columns * lefts[left].shape[0] for terms, _ in products for left, _ in terms)
    return pl.pallas_call(
        functools.partial(weight_grads_body, count, products, len(lefts), len(rights)),
        out_shape=(half,) * 4,
        in_specs=[SMEM_SPEC] + [VMEM_SPEC] * (len(lefts) + len(rights)),
        out_specs=(VMEM_SPEC,) * 4,
        scratch_shapes=[pltpu.VMEM((width, left.shape[0]), BF) for left in lefts] + [pltpu.VMEM((2, width, columns), BF)],
        compiler_params=pltpu.CompilerParams(vmem_limit_bytes=VMEM_LIMIT),
        cost_estimate=pl.CostEstimate(flops=2 * flops, bytes_accessed=16 * width * width, transcendentals=0),
        name="weight_grads",
    )(me, *lefts, *rights)


def fold_body(joined, sides, *refs):
    ins, outs = refs[: 2 * sides], refs[2 * sides :]
    for side in range(sides):
        keep, got = ins[2 * side], ins[2 * side + 1]
        rows, columns = keep.shape
        total = keep[...].astype(F32) + got[...].astype(F32)
        if len(outs) == 1:
            outs[0][...] = total
            continue
        out_keep, out_send = (outs[0], outs[1]) if joined else (outs[2 * side], outs[2 * side + 1])
        at = side * columns if joined else 0
        out_keep[:, at : at + columns] = total[: rows // 2].astype(BF)
        out_send[:, at : at + columns] = total[rows // 2 :].astype(BF)


def fold(parts, joined, last):
    sides = len(parts) // 2
    rows, columns = parts[0].shape
    if last:
        shapes = (jax.ShapeDtypeStruct((rows, columns), F32),)
    elif joined:
        shapes = (jax.ShapeDtypeStruct((rows // 2, columns * sides), BF),) * 2
    else:
        shapes = (jax.ShapeDtypeStruct((rows // 2, columns), BF),) * (2 * sides)
    return pl.pallas_call(
        functools.partial(fold_body, joined, sides),
        out_shape=shapes,
        in_specs=[VMEM_SPEC] * len(parts),
        out_specs=(VMEM_SPEC,) * len(shapes),
        cost_estimate=pl.CostEstimate(flops=rows * columns * sides, bytes_accessed=6 * rows * columns * sides, transcendentals=0),
        compiler_params=pltpu.CompilerParams(vmem_limit_bytes=32 * 1024 * 1024),
        name="fold",
    )(*parts)


def exchanged(value, bit, count):
    return lax.ppermute(value, "dp", [(i, i ^ (1 << bit)) for i in range(count)])


def cube_sum(halves_in, count):
    keep_a, send_a, keep_b, send_b = halves_in
    first, second = bit_orders(count)
    levels = len(first)
    parts = (keep_a, exchanged(send_a, first[0], count), keep_b, exchanged(send_b, second[0], count))
    keep_a, send_a, keep_b, send_b = fold(parts, False, False)
    parts = (keep_a, exchanged(send_a, first[1], count), keep_b, exchanged(send_b, second[1], count))
    keep, send = fold(parts, True, False)
    for level in range(2, levels):
        result = fold((keep, exchanged(send, first[level], count)), False, level == levels - 1)
        if level < levels - 1:
            keep, send = result
    return result[0]


def padded_memory_body(source, target):
    rows = source.shape[1]
    target[...] = jnp.zeros_like(target)
    target[:rows, :] = source[0]


def padded_memory(memory, padded):
    images, rows, width = memory.shape
    return pl.pallas_call(
        padded_memory_body,
        grid=(images,),
        out_shape=jax.ShapeDtypeStruct((images * padded, width), memory.dtype),
        in_specs=[pl.BlockSpec((1, rows, width), lambda i: (i, 0, 0))],
        out_specs=pl.BlockSpec((padded, width), lambda i: (i, 0)),
        cost_estimate=pl.CostEstimate(flops=0, bytes_accessed=4 * images * padded * width, transcendentals=0),
        name="padded_memory",
    )(memory)


def memory_total_body(where, own, other, mine, theirs, target):
    image = pl.program_id(0)
    rows = target.shape[1]
    half = mine.shape[1]
    last = jnp.where(image == where[0], 1.0, 0.0)
    first_core = where[1] == 0
    target_rows = slice(0, rows)
    for side in range(2):
        columns = slice(side * half, (side + 1) * half)
        extra = jnp.where(first_core if side == 0 else jnp.logical_not(first_core), mine[...].astype(F32), theirs[...].astype(F32))
        total = own[:, columns].astype(F32) + other[:, columns].astype(F32) + last * extra
        target[0, target_rows, columns] = total[:rows].astype(BF)


def memory_total(rows, where, own, other, mine, theirs):
    padded = mine.shape[0]
    images, width = own.shape[0] // padded, own.shape[1]
    block = pl.BlockSpec((padded, width), lambda i: (i, 0))
    half = pl.BlockSpec(mine.shape, lambda i: (0, 0))
    return pl.pallas_call(
        memory_total_body,
        grid=(images,),
        out_shape=jax.ShapeDtypeStruct((images, rows, width), BF),
        in_specs=[SMEM_SPEC, block, block, half, half],
        out_specs=pl.BlockSpec((1, rows, width), lambda i: (i, 0, 0)),
        compiler_params=pltpu.CompilerParams(vmem_limit_bytes=32 * 1024 * 1024),
        cost_estimate=pl.CostEstimate(flops=0, bytes_accessed=8 * images * padded * width, transcendentals=0),
        name="memory_total",
    )(where, own, other, mine, theirs)


def core_swap(value):
    return lax.ppermute(value, "tensor", [(0, 1), (1, 0)])


def core_half(value, core):
    half = value.shape[1] // 2
    return jnp.where(core == 0, value[:, :half], value[:, half:])


def other_half(value, core):
    half = value.shape[1] // 2
    return jnp.where(core == 0, value[:, half:], value[:, :half])


def rejoined(mine, theirs, core):
    return jnp.concatenate([jnp.where(core == 0, mine, theirs), jnp.where(core == 0, theirs, mine)], 1)


def fetched(value, core):
    mine = shifted(core_half(value, core), "dp", 1)
    return rejoined(mine, core_swap(mine), core)


def given_back(partial, core):
    low = partial.astype(BF)
    total = core_half(low, core).astype(F32) + core_swap(other_half(low, core)).astype(F32)
    mine = shifted(total.astype(BF), "dp", -1)
    return mine, core_swap(mine)


def two_level_scatter(stacked, count):
    inner = min(4, count)
    outer = count // inner
    near = [[o * inner + i for i in range(inner)] for o in range(outer)]
    far = [[o * inner + i for o in range(outer)] for i in range(inner)]
    first = lax.psum_scatter(stacked, "dp", scatter_dimension=0, axis_index_groups=near, tiled=True)
    return lax.psum_scatter(first, "dp", scatter_dimension=0, axis_index_groups=far, tiled=True)


def per_device(
    tokens,
    page_ids,
    image_of_page,
    memory,
    ln0_gain,
    ln0_bias,
    w_self_query,
    b_self_query,
    w_self_key,
    w_self_value,
    b_self_value,
    w_self_out,
    b_self_out,
    ln1_gain,
    ln1_bias,
    w_query,
    b_query,
    w_key,
    w_value,
    b_value,
    w_out,
    b_out,
    ln2_gain,
    ln2_bias,
    w_up,
    b_up,
    w_down,
    b_down,
    cotangent,
):
    count = lax.axis_size("dp")
    me = lax.axis_index("dp")
    core = lax.axis_index("tensor")
    row_count, width = tokens.shape
    image_count, memory_rows = (memory.shape[0], memory.shape[1])
    scale = 1.0 / math.sqrt(HEAD_WIDTH)
    padded_rows = -(-memory_rows // 16) * 16
    first_page = me * image_count
    local_page = page_ids - first_page
    begins = [jnp.sum((local_page < page).astype(jnp.int32)) for page in range(image_count)]
    prior_begin = shifted(jnp.full((128,), begins[1], jnp.int32), "dp", 1)[0]
    slots = [jnp.int32(image_count)] + [image_of_page[page] - first_page for page in range(image_count)]
    meta = jnp.stack(begins + [prior_begin] + slots).astype(jnp.int32)
    last_image = image_of_page[image_count - 1] - first_page
    skipped = row_count // 4
    prior_tokens = fetched(tokens[skipped:], core)
    flat_memory = padded_memory(memory, padded_rows)
    prior_memory = fetched(
        lax.dynamic_slice_in_dim(flat_memory, last_image * padded_rows, padded_rows, 0), core
    )

    def project(rows, weight, bias=None):
        product = jnp.dot(rows, weight, preferred_element_type=F32)
        return (product if bias is None else product + bias).astype(BF)

    def back(grads, weight):
        return jnp.einsum("th,dh->td", grads, weight, preferred_element_type=F32)

    input_values = tokens.astype(F32)
    hidden_zero, self_normed_rows, inverse_zero = layer_norm(input_values, ln0_gain, ln0_bias)
    hidden_zero = hidden_zero.astype(BF)
    self_queries = (
        (jnp.dot(hidden_zero, w_self_query, preferred_element_type=F32) + b_self_query) * scale
    ).astype(BF)
    self_key_rows = project(hidden_zero, w_self_key)
    self_values = project(hidden_zero, w_self_value, b_self_value)
    keys_here = project(flat_memory, w_key)
    values_here = project(flat_memory, w_value, b_value)
    prior_hidden = layer_norm(prior_tokens.astype(F32), ln0_gain, ln0_bias)[0].astype(BF)
    prior_keys = project(prior_hidden, w_self_key)
    prior_values = project(prior_hidden, w_self_value, b_self_value)
    self_attended, self_logs = self_forward(
        meta, self_queries, prior_keys, self_key_rows, prior_values, self_values
    )
    self_part = project(self_attended, w_self_out)
    self_other = core_swap(self_part)
    prior_image_keys = project(prior_memory, w_key)
    prior_image_values = project(prior_memory, w_value, b_value)
    start = input_values + (self_part.astype(F32) + self_other.astype(F32)) + b_self_out
    hidden_one, normed_one, inverse_one = layer_norm(start, ln1_gain, ln1_bias)
    hidden_one = hidden_one.astype(BF)
    queries = (
        (jnp.dot(hidden_one, w_query, preferred_element_type=F32) + b_query) * scale
    ).astype(BF)
    attended, log_totals = cross_forward(
        memory_rows, meta, queries, prior_image_keys, keys_here, prior_image_values, values_here
    )
    cross_part = project(attended, w_out)
    cross_other = core_swap(cross_part)
    inner = min(4, count)
    tile = 512
    middle, down_part, grad_part, forward_grads, up_bias_grad = feed_forward(
        inner, count // inner, tile, start, cross_part, cross_other, b_out, ln2_gain, ln2_bias, cotangent, w_up, b_up, w_down
    )
    grad_other = core_swap(grad_part)
    forward_sums = two_level_scatter(forward_grads, count).astype(F32)
    down_other = core_swap(down_part)
    layer_out = (middle + (down_part.astype(F32) + down_other.astype(F32)) + b_down).astype(BF)
    grad_outer = cotangent.astype(F32)
    down_bias_grad = jnp.sum(grad_outer, axis=0)
    unused_hidden, normed_two, inverse_two = layer_norm(middle, ln2_gain, ln2_bias)
    back_two, gain_two_grad, bias_two_grad = norm_back(
        grad_part.astype(F32) + grad_other.astype(F32), normed_two, inverse_two, ln2_gain
    )
    grad_middle = grad_outer + back_two
    grad_branch = grad_middle.astype(BF)
    out_bias_grad = jnp.sum(grad_branch.astype(F32), axis=0)
    grad_attended = jnp.einsum("td,hd->th", grad_branch, w_out, preferred_element_type=F32).astype(BF)
    prior_image_key_grads, key_grads, prior_image_value_grads, value_grads, grad_queries = cross_back(
        memory_rows,
        meta,
        queries,
        grad_attended,
        attended,
        log_totals,
        prior_image_keys,
        keys_here,
        prior_image_values,
        values_here,
    )
    hidden_part = (back(grad_queries, w_query) * scale).astype(BF)
    hidden_other = core_swap(hidden_part)
    me_list = jnp.full((1,), me, jnp.int32)
    cross_sums = cube_sum(
        weight_grads(
            count,
            me_list,
            (hidden_one, flat_memory, prior_memory, grad_branch),
            (grad_queries, key_grads, prior_image_key_grads, value_grads, prior_image_value_grads, attended),
            (
                (((0, 0),), scale),
                (((1, 1), (2, 2)), 1.0),
                (((1, 3), (2, 4)), 1.0),
                (((3, 5),), 1.0),
            ),
        ),
        count,
    )
    memory_back = given_back(back(prior_image_key_grads, w_key) + back(prior_image_value_grads, w_value), core)
    memory_part = (back(key_grads, w_key) + back(value_grads, w_value)).astype(BF)
    memory_other = core_swap(memory_part)
    value_bias_grad = jnp.sum(value_grads.astype(F32), axis=0) + jnp.sum(prior_image_value_grads.astype(F32), axis=0)
    query_bias_grad = jnp.sum(grad_queries.astype(F32), axis=0) * scale
    back_one, gain_one_grad, bias_one_grad = norm_back(
        hidden_part.astype(F32) + hidden_other.astype(F32), normed_one, inverse_one, ln1_gain
    )
    grad_start = grad_middle + back_one
    d_memory = memory_total(memory_rows, jnp.stack([last_image, core]), memory_part, memory_other, *memory_back)
    grad_start_low = grad_start.astype(BF)
    self_out_bias_grad = jnp.sum(grad_start_low.astype(F32), axis=0)
    grad_self_attended = jnp.einsum(
        "td,hd->th", grad_start_low, w_self_out, preferred_element_type=F32
    ).astype(BF)
    prior_key_grads, prior_value_grads, prior_query_grads = self_prior_back(
        meta, self_queries, grad_self_attended, self_attended, self_logs, prior_keys, prior_values
    )
    zero_back = given_back(back(prior_key_grads, w_self_key) + back(prior_value_grads, w_self_value), core)
    self_key_grads, self_value_grads, grad_self_queries = self_own_back(
        meta,
        self_queries,
        grad_self_attended,
        self_attended,
        self_logs,
        self_key_rows,
        self_values,
        prior_query_grads,
    )
    zero_part = (
        back(grad_self_queries, w_self_query) * scale
        + back(self_key_grads, w_self_key)
        + back(self_value_grads, w_self_value)
    ).astype(BF)
    zero_other = core_swap(zero_part)
    self_sums = cube_sum(
        weight_grads(
            count,
            me_list,
            (hidden_zero, prior_hidden, grad_start_low),
            (grad_self_queries, self_key_grads, prior_key_grads, self_value_grads, prior_value_grads, self_attended),
            (
                (((0, 0),), scale),
                (((0, 1), (1, 2)), 1.0),
                (((0, 3), (1, 4)), 1.0),
                (((2, 5),), 1.0),
            ),
        ),
        count,
    )
    self_query_bias_grad = jnp.sum(grad_self_queries.astype(F32), axis=0) * scale
    self_value_bias_grad = jnp.sum(self_value_grads.astype(F32), axis=0) + jnp.sum(prior_value_grads.astype(F32), axis=0)
    returned_rows = jnp.pad(rejoined(*zero_back, core), ((skipped, 0), (0, 0)))
    grad_hidden_zero = zero_part.astype(F32) + zero_other.astype(F32) + returned_rows.astype(F32)
    back_zero, gain_zero_grad, bias_zero_grad = norm_back(
        grad_hidden_zero, self_normed_rows, inverse_zero, ln0_gain
    )
    d_tokens = (grad_start + back_zero).astype(BF)
    small_sums = butterfly_sum(
        (
            gain_zero_grad,
            bias_zero_grad,
            self_query_bias_grad,
            self_value_bias_grad,
            self_out_bias_grad,
            gain_one_grad,
            bias_one_grad,
            query_bias_grad,
            value_bias_grad,
            out_bias_grad,
            gain_two_grad,
            bias_two_grad,
            up_bias_grad[0],
            down_bias_grad,
        )
    )
    local = w_query.shape[1]

    def cut(table, number):
        return table[:, number * local : (number + 1) * local]

    pieces = forward_sums.reshape(forward_sums.shape[0], -1, 2, tile)
    summed_up = pieces[:, :, 0].reshape(forward_sums.shape[0], -1)
    summed_down = pieces[:, :, 1].reshape(forward_sums.shape[0], -1).T
    return (
        layer_out,
        d_tokens,
        d_memory,
        small_sums[0],
        small_sums[1],
        cut(self_sums, 0),
        small_sums[2],
        cut(self_sums, 1),
        cut(self_sums, 2),
        small_sums[3],
        cut(self_sums, 3).T,
        small_sums[4],
        small_sums[5],
        small_sums[6],
        cut(cross_sums, 0),
        small_sums[7],
        cut(cross_sums, 1),
        cut(cross_sums, 2),
        small_sums[8],
        cut(cross_sums, 3).T,
        small_sums[9],
        small_sums[10],
        small_sums[11],
        summed_up,
        small_sums[12],
        summed_down,
        small_sums[13],
    )


def solution(mesh):
    in_specs = (
        P("dp", None),
        P("dp"),
        P("dp"),
        P("dp", None, None),
        P(),
        P(),
        P(None, "tensor"),
        P("tensor"),
        P(None, "tensor"),
        P(None, "tensor"),
        P("tensor"),
        P("tensor", None),
        P(),
        P(),
        P(),
        P(None, "tensor"),
        P("tensor"),
        P(None, "tensor"),
        P(None, "tensor"),
        P("tensor"),
        P("tensor", None),
        P(),
        P(),
        P(),
        P(None, "tensor"),
        P("tensor"),
        P("tensor", None),
        P(),
        P("dp", None),
    )
    out_specs = (
        P("dp", None),
        P("dp", None),
        P("dp", None, None),
        P(),
        P(),
        P("dp", "tensor"),
        P("tensor"),
        P("dp", "tensor"),
        P("dp", "tensor"),
        P("tensor"),
        P("tensor", "dp"),
        P(),
        P(),
        P(),
        P("dp", "tensor"),
        P("tensor"),
        P("dp", "tensor"),
        P("dp", "tensor"),
        P("tensor"),
        P("tensor", "dp"),
        P(),
        P(),
        P(),
        P("dp", "tensor"),
        P("tensor"),
        P("tensor", "dp"),
        P(),
    )
    return jax.shard_map(
        per_device, mesh=mesh, in_specs=in_specs, out_specs=out_specs, check_vma=False
    )
```

time: 1120 us -> 544 us (0.49)
  waiting for transfers between devices: 734 us -> 161 us
  Pallas kernels: 76.1 us -> 171 us
  matrix products: 133 us -> 43.9 us
  starting transfers between devices: 30.4 us -> 63.6 us
  other arithmetic: 77.2 us -> 53.1 us
  local copies, waits for them, and re-layouts: 44.6 us -> 27.2 us
    reduce_scatter x10 -> x2, waiting for transfers between devices: 569 us -> 19.1 us  [the longest x1 19.1 us: two_level_scatter(): lax.psum_scatter(first, 'dp', scatter_dimension=0, axis_index_groups=far,...]
    ppermute x9 -> x5, waiting for transfers between devices: 152 us -> 1.01 us  [shifted(): lax.ppermute(value, axis, [(source, source + steps) for source in range(i...]
    ppermute x7 -> x25, waiting for transfers between devices: 4.16 us -> 127 us  [the longest x12 123 us: exchanged(): return lax.ppermute(value, 'dp', [(i, i ^ 1 << bit) for i in range(count)])]
    pallas_call x2 -> x15, Pallas kernels: 31.3 us -> 122 us  [the longest x1 56.8 us: feed_forward(): pl.pallas_call(functools.partial(feed_forward_body, inner, outer), grid=(...]
    dot_general x29 -> x23, matrix products: 131 us -> 41.7 us  [the longest x10 21.8 us: project(): product = jnp.dot(rows, weight, preferred_element_type=F32)]
    ppermute x7 -> x25, starting transfers between devices: 1.29 us -> 45 us  [the longest x12 42.6 us: exchanged(): return lax.ppermute(value, 'dp', [(i, i ^ 1 << bit) for i in range(count)])]
    convert_element_type x16 -> x6, other arithmetic: 34.6 us -> 10.7 us  [the longest x1 7.16 us: per_device(): d_tokens = (grad_start + back_zero).astype(BF)]
    unnamed x155 -> x167, local copies, waits for them, and re-layouts: 35 us -> 14.9 us
  transfers between devices with their start and end apart: 30 -> 36, of which waited for: 18 -> 17; matrix products, arithmetic and copies ran while one was open for 15% -> 19% of each run, Pallas kernels for 5% -> 19%
where the time goes in v3:
time: 544 us; the launch traced here: 537 us
  Pallas kernels  171 us (31%)
  waiting for transfers between devices  161 us (30%)
  starting transfers between devices  63.6 us (12%)
  other arithmetic  53.1 us (10%)
  matrix products  43.9 us (8%)
  local copies, waits for them, and re-layouts  27.2 us (5%)
  between operations  16.9 us (3%)
    ppermute x12, waiting for transfers between devices, exchanged(): return lax.ppermute(value, 'dp', [(i, i ^ 1 << bit) for i in range(count)])  123 us
    pallas_call x1, Pallas kernels, feed_forward(): pl.pallas_call(functools.partial(feed_forward_body, inner, outer), grid=(...  56.8 us
    ppermute x12, starting transfers between devices, exchanged(): return lax.ppermute(value, 'dp', [(i, i ^ 1 << bit) for i in range(count)])  42.6 us
    pallas_call x2, Pallas kernels, weight_grads(): pl.pallas_call(functools.partial(weight_grads_body, count, products, len(...  25.8 us
    pallas_call x1, Pallas kernels, cross_back(): pl.pallas_call(functools.partial(cross_back_body, used), out_shape=tuple(...  25.1 us
    pallas_call x1, Pallas kernels, self_own_back(): pl.pallas_call(self_own_back_body, out_shape=(jax.ShapeDtypeStruct((rows,...  22.1 us
    dot_general x10, matrix products, project(): product = jnp.dot(rows, weight, preferred_element_type=F32)  21.8 us
    reduce_scatter x1, waiting for transfers between devices, two_level_scatter(): lax.psum_scatter(first, 'dp', scatter_dimension=0, axis_index_groups=far,...  19.1 us
  transfers between devices with their start and end apart: 36, of which 17 were waited for; matrix products, arithmetic and copies ran while one was open for 19% of the time, Pallas kernels for 19%

profile of v3, /device:TPU:0, one launch (start us, length us, event | category | flops | bytes accessed | tf_op | source)
XLA Modules:
  0.0 537.0 jit_solution(9485913730007663908)
XLA Ops:
  54.2 14.3 %self_forward.1 = (bf16[1024,512]{1,0:T(8,128)(2,1)}, f32[8,1024]{1,0:T(8,128)}) custom-call(s32[6]{0:T(128)} %stack.26.meta, bf16[1024,512]{1,0:T(8,128)(2,1)} %multiply_convert_fusion.2.q_ref, bf16[768,512]{1,0:T(8,128)(2,1)} %convolution_convert_fusion.6.kp_ref.k_ref, bf16[1024,512]{1,0:T(8,128)(2,1)} %convolution_convert_fusion.5.k_ref, ...), custom_call_target="tpu_custom_call" | custom-call | flops 2147483648 | bytes 8388608 | tf_op jit(solution)/shard_map/self_forward/pallas_call | solution.py:200
  88.2 12.3 %cross_forward.1 = (bf16[1024,512]{1,0:T(8,128)(2,1)}, f32[8,1024]{1,0:T(8,128)}) custom-call(s32[6]{0:T(128)} %stack.26.meta, bf16[1024,512]{1,0:T(8,128)(2,1)} %multiply_convert_fusion.1.q_ref, bf16[592,512]{1,0:T(8,128)(2,1)} %convolution_convert_fusion.7.kp_ref, bf16[1184,512]{1,0:T(8,128)(2,1)} %convolution_convert_fusion.k_ref, ...), custom_call_target="tpu_custom_call" | custom-call | flops 4966055936 | bytes 8388608 | tf_op jit(solution)/shard_map/cross_forward/pallas_call | solution.py:452
  108.6 56.8 %feed_forward.1 = (f32[1024,1024]{1,0:T(8,128)}, bf16[1024,1024]{1,0:T(8,128)(2,1)}, bf16[1024,1024]{1,0:T(8,128)(2,1)}, bf16[1024,4096]{1,0:T(8,128)(2,1)}, f32[1,2048]{1,0:T(1,128)}) custom-call(f32[1024,1024]{1,0:T(8,128)} %copy-done.9, bf16[1024,1024]{1,0:T(8,128)(2,1)} %copy-done.63, bf16[1024,1024]{1,0:T(8,128)(2,1)} %copy-done.64, ...), custom_call_target="tpu_custom_call" | custom-call | flops 25769803776 | bytes 31457280 | tf_op jit(solution)/shard_map/feed_forward/pallas_call | solution.py:629
  177.9 7.1 %convert_reduce_fusion.2 = (f32[1024]{0:T(1024)S(1)}, bf16[1024,1024]{1,0:T(8,128)(2,1)S(1)}, f32[1024,1024]{1,0:T(8,128)}, bf16[1024,1024]{1,0:T(8,128)(2,1)}, f32[1024]{0:T(1024)S(1)}) fusion(f32[1024]{0:T(1024)S(1)} %get-tuple-element.197, f32[1024]{0:T(1024)S(1)} %add_rsqrt_fusion, f32[1024,1024]{1,0:T(8,128)S(1)} %copy-done.13, ...), kind=kLoop, calls=%fused_computation.26 | loop fusion | flops 23066624 | bytes 23101440 | tf_op jit(solution)/shard_map/reduce_sum | solution.py:973
  187.3 25.1 %cross_back.1 = (bf16[592,512]{1,0:T(8,128)(2,1)}, bf16[1184,512]{1,0:T(8,128)(2,1)}, bf16[592,512]{1,0:T(8,128)(2,1)}, bf16[1184,512]{1,0:T(8,128)(2,1)}, bf16[1024,512]{1,0:T(8,128)(2,1)}) custom-call(s32[6]{0:T(128)} %stack.26.meta, bf16[1024,512]{1,0:T(8,128)(2,1)} %multiply_convert_fusion.1.q_ref, bf16[1024,512]{1,0:T(8,128)(2,1)} %convolution_convert_fusion.4.do_ref, ...), custom_call_target="tpu_custom_call" | custom-call | flops 12415139840 | bytes 12582912 | tf_op jit(solution)/shard_map/cross_back/pallas_call | solution.py:514
  212.4 13.8 %weight_grads.3 = (bf16[512,1024]{1,0:T(8,128)(2,1)}, bf16[512,1024]{1,0:T(8,128)(2,1)}, bf16[512,1024]{1,0:T(8,128)(2,1)}, bf16[512,1024]{1,0:T(8,128)(2,1)}) custom-call(s32[1]{0:T(128)} %bitcast.15.me, bf16[1024,1024]{1,0:T(8,128)(2,1)} %copy-done.32, bf16[1184,1024]{1,0:T(8,128)(2,1)} %padded_memory.1.refs_1_, ...), custom_call_target="tpu_custom_call" | custom-call | flops 11744051200 | bytes 16777216 | tf_op jit(solution)/shard_map/weight_grads/pallas_call | solution.py:711
  226.3 7.8 %collective-permute-start.28 = (bf16[512,1024]{1,0:T(8,128)(2,1)}, bf16[512,1024]{1,0:T(8,128)(2,1)S(1)}, u32[]{:S(2)}, u32[]{:S(2)}) collective-permute-start(bf16[512,1024]{1,0:T(8,128)(2,1)} %get-tuple-element.103), channel_id=1, source_target_pairs={{0,2},{2,0},{4,6},{6,4},{8,10},{10,8},{12,14},{14,12},{16,18},{18,... | collective-permute-start | bytes 3145736 | tf_op jit(solution)/shard_map/ppermute | solution.py:759
  234.1 5.2 collective-permute-start.29
  247.6 32.5 %collective-permute-done.28.refs_1_ = bf16[512,1024]{1,0:T(8,128)(2,1)S(1)} collective-permute-done((bf16[512,1024]{1,0:T(8,128)(2,1)}, bf16[512,1024]{1,0:T(8,128)(2,1)S(1)}, u32[]{:S(2)}, u32[]{:S(2)}) %collective-permute-start.28) | collective-permute-done | bytes 1048608 | tf_op jit(solution)/shard_map/ppermute | solution.py:759
  293.9 5.4 %self_prior_back.1 = (bf16[768,512]{1,0:T(8,128)(2,1)}, bf16[768,512]{1,0:T(8,128)(2,1)}, f32[1024,512]{1,0:T(8,128)}) custom-call(s32[6]{0:T(128)} %stack.26.meta, bf16[1024,512]{1,0:T(8,128)(2,1)} %multiply_convert_fusion.2.q_ref, bf16[1024,512]{1,0:T(8,128)(2,1)} %convolution_convert_fusion.3.do_ref, bf16[1024,512]{1,0:T(8,128)(2,1)} %get-tuple-element.71.o_ref.refs_8_, ...), custom_call_target="tpu_custom_call" | custom-call | flops 1610612736 | bytes 8388608 | tf_op jit(solution)/shard_map/self_prior_back/pallas_call | solution.py:373
  299.3 22.1 %self_own_back.1 = (bf16[1024,512]{1,0:T(8,128)(2,1)}, bf16[1024,512]{1,0:T(8,128)(2,1)}, bf16[1024,512]{1,0:T(8,128)(2,1)}) custom-call(s32[6]{0:T(128)} %stack.26.meta, bf16[1024,512]{1,0:T(8,128)(2,1)} %multiply_convert_fusion.2.q_ref, bf16[1024,512]{1,0:T(8,128)(2,1)} %convolution_convert_fusion.3.do_ref, ...), custom_call_target="tpu_custom_call" | custom-call | flops 2684354560 | bytes 8388608 | tf_op jit(solution)/shard_map/self_own_back/pallas_call | solution.py:388
  321.4 12.0 %weight_grads.2 = (bf16[512,1024]{1,0:T(8,128)(2,1)}, bf16[512,1024]{1,0:T(8,128)(2,1)}, bf16[512,1024]{1,0:T(8,128)(2,1)}, bf16[512,1024]{1,0:T(8,128)(2,1)}) custom-call(s32[1]{0:T(128)} %bitcast.15.me, bf16[1024,1024]{1,0:T(8,128)(2,1)} %copy-done.34, bf16[768,1024]{1,0:T(8,128)(2,1)} %copy-done.38, bf16[1024,1024]{1,0:T(8,128)(2,1)} %copy-done.33, ...), custom_call_target="tpu_custom_call" | custom-call | flops 11811160064 | bytes 16777216 | tf_op jit(solution)/shard_map/weight_grads/pallas_call | solution.py:711
  334.9 7.6 %collective-permute-start.23 = (bf16[512,1024]{1,0:T(8,128)(2,1)}, bf16[512,1024]{1,0:T(8,128)(2,1)S(1)}, u32[]{:S(2)}, u32[]{:S(2)}) collective-permute-start(bf16[512,1024]{1,0:T(8,128)(2,1)} %get-tuple-element.93), channel_id=1, source_target_pairs={{0,4},{2,6},{4,0},{6,2},{8,12},{10,14},{12,8},{14,10},{16,20},{18,... | collective-permute-start | bytes 3145736 | tf_op jit(solution)/shard_map/ppermute | solution.py:759
  349.2 9.1 %collective-permute-done.22.refs_1_ = bf16[512,1024]{1,0:T(8,128)(2,1)S(1)} collective-permute-done((bf16[512,1024]{1,0:T(8,128)(2,1)}, bf16[512,1024]{1,0:T(8,128)(2,1)S(1)}, u32[]{:S(2)}, u32[]{:S(2)}) %collective-permute-start.22) | collective-permute-done | bytes 1048608 | tf_op jit(solution)/shard_map/ppermute | solution.py:759
  359.9 5.5 %collective-permute-done.23.refs_3_ = bf16[512,1024]{1,0:T(8,128)(2,1)S(1)} collective-permute-done((bf16[512,1024]{1,0:T(8,128)(2,1)}, bf16[512,1024]{1,0:T(8,128)(2,1)S(1)}, u32[]{:S(2)}, u32[]{:S(2)}) %collective-permute-start.23) | collective-permute-done | bytes 1048608 | tf_op jit(solution)/shard_map/ppermute | solution.py:759
  381.4 30.8 %collective-permute-done.25.refs_3_ = bf16[256,1024]{1,0:T(8,128)(2,1)S(1)} collective-permute-done((bf16[256,1024]{1,0:T(8,128)(2,1)S(1)}, bf16[256,1024]{1,0:T(8,128)(2,1)S(1)}, u32[]{:S(2)}, u32[]{:S(2)}) %collective-permute-start.25) | collective-permute-done | bytes 524320 | tf_op jit(solution)/shard_map/ppermute | solution.py:759
  415.3 11.7 %collective-permute-done.32.refs_1_ = bf16[128,2048]{1,0:T(8,128)(2,1)S(1)} collective-permute-done((bf16[128,2048]{1,0:T(8,128)(2,1)S(1)}, bf16[128,2048]{1,0:T(8,128)(2,1)S(1)}, u32[]{:S(2)}, u32[]{:S(2)}) %collective-permute-start.32) | collective-permute-done | bytes 524320 | tf_op jit(solution)/shard_map/ppermute | solution.py:759
  427.1 10.2 %collective-permute-done.26.refs_1_ = bf16[128,2048]{1,0:T(8,128)(2,1)S(1)} collective-permute-done((bf16[128,2048]{1,0:T(8,128)(2,1)S(1)}, bf16[128,2048]{1,0:T(8,128)(2,1)S(1)}, u32[]{:S(2)}, u32[]{:S(2)}) %collective-permute-start.26) | collective-permute-done | bytes 524320 | tf_op jit(solution)/shard_map/ppermute | solution.py:759
  437.3 10.4 %collective-permute-start.33 = (bf16[64,2048]{1,0:T(8,128)(2,1)S(1)}, bf16[64,2048]{1,0:T(8,128)(2,1)S(1)}, u32[]{:S(2)}, u32[]{:S(2)}) collective-permute-start(bf16[64,2048]{1,0:T(8,128)(2,1)S(1)} %get-tuple-element.113), channel_id=1, source_target_pairs={{0,16},{2,18},{4,20},{6,22},{8,24},{10,26},{12,28},{14,30},{16,0},... | collective-permute-start | bytes 786440 | tf_op jit(solution)/shard_map/ppermute | solution.py:759
  448.2 10.3 %collective-permute-done.33.refs_1_ = bf16[64,2048]{1,0:T(8,128)(2,1)S(1)} collective-permute-done((bf16[64,2048]{1,0:T(8,128)(2,1)S(1)}, bf16[64,2048]{1,0:T(8,128)(2,1)S(1)}, u32[]{:S(2)}, u32[]{:S(2)}) %collective-permute-start.33) | collective-permute-done | bytes 262176 | tf_op jit(solution)/shard_map/ppermute | solution.py:759
  466.1 6.2 %collective-permute-done.27.refs_1_ = bf16[64,2048]{1,0:T(8,128)(2,1)S(1)} collective-permute-done((bf16[64,2048]{1,0:T(8,128)(2,1)S(1)}, bf16[64,2048]{1,0:T(8,128)(2,1)S(1)}, u32[]{:S(2)}, u32[]{:S(2)}) %collective-permute-start.27) | collective-permute-done | bytes 262176 | tf_op jit(solution)/shard_map/ppermute | solution.py:759
  486.3 6.6 %collective-permute-done.20 = f32[104,128]{1,0:T(8,128)S(1)} collective-permute-done((f32[104,128]{1,0:T(8,128)S(1)}, f32[104,128]{1,0:T(8,128)S(1)}, u32[]{:S(2)}, u32[]{:S(2)}) %collective-permute-start.20) | collective-permute-done | bytes 53280 | tf_op jit(solution)/shard_map/ppermute | solution.py:29
  493.0 7.2 %fusion.12 = bf16[1024,1024]{1,0:T(8,128)(2,1)} fusion(f32[1024,1024]{1,0:T(8,128)} %get-tuple-element.163, bf16[1024,1024]{1,0:T(8,128)(2,1)} %param.29, f32[1024]{0:T(1024)S(1)} %broadcast_multiply_fusion.1, f32[1024]{0:T(1024)S(1)} %broadcast_multiply_fusion.2, f32[1024]{0:T(1024)S(1)} %copy-done.53, f32[1024]{0:T(1024)S(1)} %copy-done.55, ...), kind=kLoop, calls=%fused_computation.18 | loop fusion | flops 22020096 | bytes 14176256 | tf_op jit(solution)/shard_map/convert_element_type | solution.py:1062
  503.9 19.1 %reduce-scatter.5.cloned.1.call-done = bf16[64,4096]{1,0:T(8,128)(2,1)} async-done(((bf16[256,4096]{1,0:T(8,128)(2,1)}), bf16[64,4096]{1,0:T(8,128)(2,1)}) %reduce-scatter.5.cloned.1.call-update) | async-done | bytes 524304 | tf_op jit(solution)/shard_map/reduce_scatter | solution.py:863
  (326 shorter events, 171.0 us)
Async XLA Ops:
  7.2 469.9 %reduce-scatter.3.cloned.1.call-start = ((), (), s32[]{:S(2)}) async-start(), calls=%async_computation.2 | async-start | bytes 10485760 | tf_op jit(solution)/shard_map/reduce_scatter | solution.py:862
  9.3 36.2 %collective-permute-start = (s32[128]{0:T(128)S(1)}, s32[128]{0:T(128)S(1)}, u32[]{:S(2)}, u32[]{:S(2)}) collective-permute-start(s32[128]{0:T(128)S(1)} %broadcast_in_dim.4), channel_id=1, source_target_pairs={{0,2},{2,4},{4,6},{6,8},{8,10},{10,12},{12,14},{14,16},{16,18},{18... | collective-permute-start | bytes 1544 | tf_op jit(solution)/shard_map/ppermute | solution.py:20
  16.5 21.7 %collective-permute-start.1 = (bf16[768,512]{1,0:T(8,128)(2,1)}, bf16[768,512]{1,0:T(8,128)(2,1)}, u32[]{:S(2)}, u32[]{:S(2)}) collective-permute-start(bf16[768,512]{1,0:T(8,128)(2,1)} %slice_select_fusion), channel_id=1, source_target_pairs={{0,2},{2,4},{4,6},{6,8},{8,10},{10,12},{12,14},{14,16},{16,18},{18... | collective-permute-start | bytes 2359304 | tf_op jit(solution)/shard_map/ppermute | solution.py:20
  31.9 40.2 %collective-permute-start.4 = (bf16[592,512]{1,0:T(8,128)(2,1)}, bf16[592,512]{1,0:T(8,128)(2,1)}, u32[]{:S(2)}, u32[]{:S(2)}) collective-permute-start(bf16[592,512]{1,0:T(8,128)(2,1)} %dynamic-slice_select_fusion), channel_id=1, source_target_pairs={{0,2},{2,4},{4,6},{6,8},{8,10},{10,12},{12,14},{14,16},{16,18},{18... | collective-permute-start | bytes 1818632 | tf_op jit(solution)/shard_map/ppermute | solution.py:20
  167.3 355.7 %reduce-scatter.5.cloned.1.call-start = ((), (), s32[]{:S(2)}) async-start(), calls=%async_computation.3 | async-start | bytes 2621440 | tf_op jit(solution)/shard_map/reduce_scatter | solution.py:863
  226.3 53.8 %collective-permute-start.28 = (bf16[512,1024]{1,0:T(8,128)(2,1)}, bf16[512,1024]{1,0:T(8,128)(2,1)S(1)}, u32[]{:S(2)}, u32[]{:S(2)}) collective-permute-start(bf16[512,1024]{1,0:T(8,128)(2,1)} %get-tuple-element.103), channel_id=1, source_target_pairs={{0,2},{2,0},{4,6},{6,4},{8,10},{10,8},{12,14},{14,12},{16,18},{18,... | collective-permute-start | bytes 3145736 | tf_op jit(solution)/shard_map/ppermute | solution.py:759
  234.1 48.4 %collective-permute-start.29 = (bf16[512,1024]{1,0:T(8,128)(2,1)}, bf16[512,1024]{1,0:T(8,128)(2,1)S(1)}, u32[]{:S(2)}, u32[]{:S(2)}) collective-permute-start(bf16[512,1024]{1,0:T(8,128)(2,1)} %get-tuple-element.105), channel_id=1, source_target_pairs={{0,4},{2,6},{4,0},{6,2},{8,12},{10,14},{12,8},{14,10},{16,20},{18,... | collective-permute-start | bytes 3145736 | tf_op jit(solution)/shard_map/ppermute | solution.py:759
  240.6 44.6 %collective-permute-start.9 = (bf16[1024,1024]{1,0:T(8,128)(2,1)S(1)}, bf16[1024,1024]{1,0:T(8,128)(2,1)S(1)}, u32[]{:S(2)}, u32[]{:S(2)}) collective-permute-start(bf16[1024,1024]{1,0:T(8,128)(2,1)S(1)} %multiply_convert_fusion), channel_id=1, source_target_pairs={{0,1},{1,0},{2,3},{3,2},{4,5},{5,4},{6,7},{7,6},{8,9},{9,8},{10,11... | collective-permute-start | bytes 6291464 | tf_op jit(solution)/shard_map/ppermute | solution.py:828
  246.2 213.3 %collective-permute-start.14 = (bf16[1184,1024]{1,0:T(8,128)(2,1)S(1)}, bf16[1184,1024]{1,0:T(8,128)(2,1)}, u32[]{:S(2)}, u32[]{:S(2)}) collective-permute-start(bf16[1184,1024]{1,0:T(8,128)(2,1)S(1)} %add_convert_fusion.own), channel_id=1, source_target_pairs={{0,1},{1,0},{2,3},{3,2},{4,5},{5,4},{6,7},{7,6},{8,9},{9,8},{10,11... | collective-permute-start | bytes 7274504 | tf_op jit(solution)/shard_map/ppermute | solution.py:828
  283.7 85.7 %collective-permute-start.30 = (bf16[256,1024]{1,0:T(8,128)(2,1)}, bf16[256,1024]{1,0:T(8,128)(2,1)}, u32[]{:S(2)}, u32[]{:S(2)}) collective-permute-start(bf16[256,1024]{1,0:T(8,128)(2,1)} %get-tuple-element.107), channel_id=1, source_target_pairs={{0,4},{2,6},{4,0},{6,2},{8,12},{10,14},{12,8},{14,10},{16,20},{18,... | collective-permute-start | bytes 1572872 | tf_op jit(solution)/shard_map/ppermute | solution.py:759
  333.4 24.9 %collective-permute-start.22 = (bf16[512,1024]{1,0:T(8,128)(2,1)}, bf16[512,1024]{1,0:T(8,128)(2,1)S(1)}, u32[]{:S(2)}, u32[]{:S(2)}) collective-permute-start(bf16[512,1024]{1,0:T(8,128)(2,1)} %get-tuple-element.91), channel_id=1, source_target_pairs={{0,2},{2,0},{4,6},{6,4},{8,10},{10,8},{12,14},{14,12},{16,18},{18,... | collective-permute-start | bytes 3145736 | tf_op jit(solution)/shard_map/ppermute | solution.py:759
  334.9 30.5 %collective-permute-start.23 = (bf16[512,1024]{1,0:T(8,128)(2,1)}, bf16[512,1024]{1,0:T(8,128)(2,1)S(1)}, u32[]{:S(2)}, u32[]{:S(2)}) collective-permute-start(bf16[512,1024]{1,0:T(8,128)(2,1)} %get-tuple-element.93), channel_id=1, source_target_pairs={{0,4},{2,6},{4,0},{6,2},{8,12},{10,14},{12,8},{14,10},{16,20},{18,... | collective-permute-start | bytes 3145736 | tf_op jit(solution)/shard_map/ppermute | solution.py:759
  346.2 24.7 %collective-permute-start.11 = (bf16[768,512]{1,0:T(8,128)(2,1)S(1)}, bf16[768,512]{1,0:T(8,128)(2,1)S(1)}, u32[]{:S(2)}, u32[]{:S(2)}) collective-permute-start(bf16[768,512]{1,0:T(8,128)(2,1)S(1)} %broadcast_select_fusion.2), channel_id=1, source_target_pairs={{0,1},{1,0},{2,3},{3,2},{4,5},{5,4},{6,7},{7,6},{8,9},{9,8},{10,11... | collective-permute-start | bytes 2359304 | tf_op jit(solution)/shard_map/ppermute | solution.py:828
  365.9 12.6 %collective-permute-start.24 = (bf16[256,1024]{1,0:T(8,128)(2,1)S(1)}, bf16[256,1024]{1,0:T(8,128)(2,1)S(1)}, u32[]{:S(2)}, u32[]{:S(2)}) collective-permute-start(bf16[256,1024]{1,0:T(8,128)(2,1)S(1)} %get-tuple-element.95), channel_id=1, source_target_pairs={{0,4},{2,6},{4,0},{6,2},{8,12},{10,14},{12,8},{14,10},{16,20},{18,... | collective-permute-start | bytes 1572872 | tf_op jit(solution)/shard_map/ppermute | solution.py:759
  369.4 43.1 %collective-permute-start.16 = (bf16[592,512]{1,0:T(8,128)(2,1)S(1)}, bf16[592,512]{1,0:T(8,128)(2,1)S(1)}, u32[]{:S(2)}, u32[]{:S(2)}) collective-permute-start(bf16[592,512]{1,0:T(8,128)(2,1)S(1)} %copy-done.48), channel_id=1, source_target_pairs={{2,0},{4,2},{6,4},{8,6},{10,8},{12,10},{14,12},{16,14},{18,16},{20... | collective-permute-start | bytes 1818632 | tf_op jit(solution)/shard_map/ppermute | solution.py:20
  370.8 101.7 %collective-permute-start.10 = (bf16[1024,1024]{1,0:T(8,128)(2,1)S(1)}, bf16[1024,1024]{1,0:T(8,128)(2,1)S(1)}, u32[]{:S(2)}, u32[]{:S(2)}) collective-permute-start(bf16[1024,1024]{1,0:T(8,128)(2,1)S(1)} %add_convert_fusion.1), channel_id=1, source_target_pairs={{0,1},{1,0},{2,3},{3,2},{4,5},{5,4},{6,7},{7,6},{8,9},{9,8},{10,11... | collective-permute-start | bytes 6291464 | tf_op jit(solution)/shard_map/ppermute | solution.py:828
  370.9 41.3 %collective-permute-start.25 = (bf16[256,1024]{1,0:T(8,128)(2,1)S(1)}, bf16[256,1024]{1,0:T(8,128)(2,1)S(1)}, u32[]{:S(2)}, u32[]{:S(2)}) collective-permute-start(bf16[256,1024]{1,0:T(8,128)(2,1)S(1)} %get-tuple-element.97), channel_id=1, source_target_pairs={{0,2},{2,0},{4,6},{6,4},{8,10},{10,8},{12,14},{14,12},{16,18},{18,... | collective-permute-start | bytes 1572872 | tf_op jit(solution)/shard_map/ppermute | solution.py:759
  378.5 36.5 %collective-permute-start.12 = (bf16[768,512]{1,0:T(8,128)(2,1)S(1)}, bf16[768,512]{1,0:T(8,128)(2,1)S(1)}, u32[]{:S(2)}, u32[]{:S(2)}) collective-permute-start(bf16[768,512]{1,0:T(8,128)(2,1)S(1)} %add_convert_fusion.7), channel_id=1, source_target_pairs={{2,0},{4,2},{6,4},{8,6},{10,8},{12,10},{14,12},{16,14},{18,16},{20... | collective-permute-start | bytes 2359304 | tf_op jit(solution)/shard_map/ppermute | solution.py:20
  412.2 14.8 %collective-permute-start.32 = (bf16[128,2048]{1,0:T(8,128)(2,1)S(1)}, bf16[128,2048]{1,0:T(8,128)(2,1)S(1)}, u32[]{:S(2)}, u32[]{:S(2)}) collective-permute-start(bf16[128,2048]{1,0:T(8,128)(2,1)S(1)} %get-tuple-element.111), channel_id=1, source_target_pairs={{0,8},{2,10},{4,12},{6,14},{8,0},{10,2},{12,4},{14,6},{16,24},{18,... | collective-permute-start | bytes 1572872 | tf_op jit(solution)/shard_map/ppermute | solution.py:759
  412.4 24.9 %collective-permute-start.26 = (bf16[128,2048]{1,0:T(8,128)(2,1)S(1)}, bf16[128,2048]{1,0:T(8,128)(2,1)S(1)}, u32[]{:S(2)}, u32[]{:S(2)}) collective-permute-start(bf16[128,2048]{1,0:T(8,128)(2,1)S(1)} %get-tuple-element.99), channel_id=1, source_target_pairs={{0,8},{2,10},{4,12},{6,14},{8,0},{10,2},{12,4},{14,6},{16,24},{18,... | collective-permute-start | bytes 1572872 | tf_op jit(solution)/shard_map/ppermute | solution.py:759
  415.1 57.3 %collective-permute-start.13 = (bf16[768,512]{1,0:T(8,128)(2,1)S(1)}, bf16[768,512]{1,0:T(8,128)(2,1)S(1)}, u32[]{:S(2)}, u32[]{:S(2)}) collective-permute-start(bf16[768,512]{1,0:T(8,128)(2,1)S(1)} %collective-permute-done.12), channel_id=1, source_target_pairs={{0,1},{1,0},{2,3},{3,2},{4,5},{5,4},{6,7},{7,6},{8,9},{9,8},{10,11... | collective-permute-start | bytes 2359304 | tf_op jit(solution)/shard_map/ppermute | solution.py:828
  427.0 32.5 %collective-permute-start.17 = (bf16[592,512]{1,0:T(8,128)(2,1)S(1)}, bf16[592,512]{1,0:T(8,128)(2,1)S(1)}, u32[]{:S(2)}, u32[]{:S(2)}) collective-permute-start(bf16[592,512]{1,0:T(8,128)(2,1)S(1)} %collective-permute-done.16.mine), channel_id=1, source_target_pairs={{0,1},{1,0},{2,3},{3,2},{4,5},{5,4},{6,7},{7,6},{8,9},{9,8},{10,11... | collective-permute-start | bytes 1818632 | tf_op jit(solution)/shard_map/ppermute | solution.py:828
  437.3 21.2 %collective-permute-start.33 = (bf16[64,2048]{1,0:T(8,128)(2,1)S(1)}, bf16[64,2048]{1,0:T(8,128)(2,1)S(1)}, u32[]{:S(2)}, u32[]{:S(2)}) collective-permute-start(bf16[64,2048]{1,0:T(8,128)(2,1)S(1)} %get-tuple-element.113), channel_id=1, source_target_pairs={{0,16},{2,18},{4,20},{6,22},{8,24},{10,26},{12,28},{14,30},{16,0},... | collective-permute-start | bytes 786440 | tf_op jit(solution)/shard_map/ppermute | solution.py:759
  458.5 13.8 %collective-permute-start.27 = (bf16[64,2048]{1,0:T(8,128)(2,1)S(1)}, bf16[64,2048]{1,0:T(8,128)(2,1)S(1)}, u32[]{:S(2)}, u32[]{:S(2)}) collective-permute-start(bf16[64,2048]{1,0:T(8,128)(2,1)S(1)} %get-tuple-element.101), channel_id=1, source_target_pairs={{0,16},{2,18},{4,20},{6,22},{8,24},{10,26},{12,28},{14,30},{16,0},... | collective-permute-start | bytes 786440 | tf_op jit(solution)/shard_map/ppermute | solution.py:759
  (89 other events, 991.6 us)
Sparse Core Ops, SparseCore 0:
  167.4 114.7 reduce-scatter.2
  477.3 45.6 reduce-scatter.4
